TPU v7x, 32 devices: a whole 2x2x4 slice. The times are simulated.
32 devices in a mesh: dp: 4 (over y, core), row: 2 (over x), col: 4 (over z).
Axes of the slice: x: 2, y: 2, z: 4, core: 2. Of those that a mesh axis runs over, the one named last changes fastest.
Arguments:
- inputs: bfloat16 [4096, 2048], P(('dp', 'col'), 'row'), may hold values from -6 to 6
- first_gain: float32 [1, 2048], P(None, 'row'), may hold values from 0.25 to 1.75
- first_shift: float32 [1, 2048], P(None, 'row'), may hold values from -3 to 3
- project_in: bfloat16 [1, 2048, 3, 2048], P(None, 'row', None, 'col'), may hold values from -0.125 to 0.125
- project_bias: float32 [1, 3, 2048], P(None, None, 'col'), may hold values from -3 to 3
- project_out: bfloat16 [1, 2048, 2048], P(None, 'col', 'row'), may hold values from -0.75 to 0.75
- second_gain: float32 [1, 2048], P(None, 'row'), may hold values from 0.25 to 1.75
- second_shift: float32 [1, 2048], P(None, 'row'), may hold values from -3 to 3
- gate_weight: bfloat16 [1, 2048, 2, 5632], P(None, 'row', None, 'col'), may hold values from -0.125 to 0.125
- down_weight: bfloat16 [1, 5632, 2048], P(None, 'col', 'row'), may hold values from -0.078125 to 0.078125
- cotangent: bfloat16 [4096, 2048], P(('dp', 'col'), 'row'), may hold values from -6 to 6
Outputs:
- layer_outputs: bfloat16 [1, 4096, 2048], P(None, ('dp', 'col'), 'row')
- input_grad: float32 [4096, 2048], P(('dp', 'col'), 'row')
- first_gain_grad: float32 [1, 2048], P(None, 'row')
- first_shift_grad: float32 [1, 2048], P(None, 'row')
- project_in_grad: float32 [1, 2048, 3, 2048], P(None, 'row', None, 'col')
- project_bias_grad: float32 [1, 3, 2048], P(None, None, 'col')
- project_out_grad: float32 [1, 2048, 2048], P(None, 'col', 'row')
- second_gain_grad: float32 [1, 2048], P(None, 'row')
- second_shift_grad: float32 [1, 2048], P(None, 'row')
- gate_weight_grad: float32 [1, 2048, 2, 5632], P(None, 'row', None, 'col')
- down_weight_grad: float32 [1, 5632, 2048], P(None, 'col', 'row')
All inputs are finite; a program needn't handle non-finite values.
Results may differ from a plain program's by a relative error of at most 0.015.
Values may be sent and summed in bfloat16 or wider, within the bound.
No kernel may reach another device: no remote copies, remote signals or barrier semaphores. Data moves between devices by JAX's collectives and lax.ppermute only.
A program may use at most 192 MiB of HBM per device.

v0:
```python
import math

import jax
import jax.numpy as jnp
from jax import lax
from jax.sharding import PartitionSpec as P

HEAD_DIM = 64
ROT = 16
LENGTH = 1024


EPSILON = 1e-05


def rotary_tables(tokens):
    position = (jnp.arange(tokens) % LENGTH).astype(jnp.float32)
    frequency = 10000.0 ** (-(jnp.arange(ROT // 2).astype(jnp.float32) * 2.0 / ROT))
    angles = position[:, None] * frequency[None, :]
    return (jnp.cos(angles), jnp.sin(angles))


def rotate(tensor, cosine_table, sine_table):
    half_rot = ROT // 2
    front_half = tensor[..., :half_rot]
    back_half = tensor[..., half_rot:ROT]
    cosine = cosine_table[:, None, :]
    sine = sine_table[:, None, :]
    return jnp.concatenate(
        [
            front_half * cosine - back_half * sine,
            back_half * cosine + front_half * sine,
            tensor[..., ROT:],
        ],
        axis=-1,
    )


def row_totals(first_part, second_part):
    return lax.psum((first_part, second_part), "row")


def norm_forward(stream, gain_row, shift_row):
    features = stream.shape[1] * lax.axis_size("row")
    summed, squares = row_totals(jnp.sum(stream, axis=1), jnp.sum(stream * stream, axis=1))
    average = summed / features
    variance = squares / features - average * average
    inv_root = lax.rsqrt(variance + EPSILON)
    normed = (stream - average[:, None]) * inv_root[:, None]
    return (normed, inv_root, (normed * gain_row + shift_row).astype(jnp.bfloat16))


def norm_backward(gradient, normed, inv_root, gain_row):
    features = gradient.shape[1] * lax.axis_size("row")
    scaled = gradient * gain_row
    summed, crossed = row_totals(jnp.sum(scaled, axis=1), jnp.sum(scaled * normed, axis=1))
    stream_grad = inv_root[:, None] * (
        scaled - summed[:, None] / features - normed * crossed[:, None] / features
    )
    return (stream_grad, jnp.sum(gradient * normed, axis=0), jnp.sum(gradient, axis=0))


def gather_tokens(local_low):
    return lax.all_gather(local_low, "col", axis=0, tiled=True)


def gather_gradient(local_low):
    return lax.all_gather(local_low, "col", axis=0, tiled=True)


def split_units(partial_sum):
    return lax.psum_scatter(partial_sum, "row", scatter_dimension=2, tiled=True)


def join_units(local_units):
    return lax.all_gather(local_units, "row", axis=1, tiled=True)


def split_unit_grads(partial_sum):
    return lax.psum_scatter(partial_sum, "row", scatter_dimension=1, tiled=True)


def join_unit_grads(local_units):
    return lax.all_gather(local_units, "row", axis=2, tiled=True)


def branch_sum(full_rows, weight_block):
    return lax.psum_scatter(
        jnp.dot(full_rows, weight_block, preferred_element_type=jnp.float32),
        "col",
        scatter_dimension=0,
        tiled=True,
    )


def input_sum(grad_full, weight_block):
    return lax.psum_scatter(
        jnp.einsum("stk,dtk->sd", grad_full, weight_block, preferred_element_type=jnp.float32),
        "col",
        scatter_dimension=0,
        tiled=True,
    )


def weight_product(normed, gain_row, shift_row, grad_full):
    local_low = (normed * gain_row + shift_row).astype(jnp.bfloat16)
    return jnp.einsum(
        "sd,stk->dtk",
        lax.all_gather(local_low, "col", axis=0, tiled=True),
        grad_full,
        preferred_element_type=jnp.float32,
    )


def block_scores(query_heads, key_heads, value_heads, block_index, factor):
    block_rows = min(512, LENGTH)
    offset = block_index * block_rows
    seq_begin = offset // LENGTH * LENGTH
    query_block = lax.dynamic_slice_in_dim(query_heads, offset, block_rows, 0)
    scores = (
        jnp.einsum("qhd,khd->hqk", query_block, key_heads, preferred_element_type=jnp.float32)
        * factor
    )
    query_position = offset - seq_begin + jnp.arange(block_rows)
    causal = query_position[:, None] >= jnp.arange(LENGTH)[None, :]
    scores = jnp.where(causal[None], scores, -jnp.inf)
    return (scores, query_block, key_heads, value_heads, offset, seq_begin)


def attend_forward(query_heads, key_heads, value_heads, factor):
    tokens = query_heads.shape[0]
    block_rows = min(512, LENGTH)

    def one_block(block_index):
        scores, query_block, key_block, value_block, offset, seq_begin = block_scores(
            query_heads, key_heads, value_heads, block_index, factor
        )
        highest = jnp.max(scores, axis=-1, keepdims=True)
        exponent = jnp.exp(scores - highest)
        summed = jnp.sum(exponent, axis=-1, keepdims=True)
        softmax_low = (exponent / summed).astype(jnp.bfloat16)
        attended = jnp.einsum(
            "hqk,khd->qhd", softmax_low, value_block, preferred_element_type=jnp.float32
        )
        return (attended, (highest + jnp.log(summed))[..., 0])

    attended, log_total = lax.map(one_block, jnp.arange(tokens // block_rows))
    return (attended.reshape(tokens, -1), log_total)


def attend_backward(query_heads, key_heads, value_heads, out_heads, log_total, factor):
    tokens = query_heads.shape[0]
    block_rows = min(512, LENGTH)

    def one_block(carry, block_index):
        key_grad, value_grad = carry
        scores, query_block, key_block, value_block, offset, seq_begin = block_scores(
            query_heads, key_heads, value_heads, block_index, factor
        )
        softmax_probs = jnp.exp(scores - log_total[block_index][..., None])
        grad_block = lax.dynamic_slice_in_dim(out_heads, offset, block_rows, 0)
        prob_grad = jnp.einsum(
            "qhd,khd->hqk", grad_block, value_block, preferred_element_type=jnp.float32
        )
        shift_term = jnp.sum(softmax_probs * prob_grad, axis=-1, keepdims=True)
        score_grad = (softmax_probs * (prob_grad - shift_term)).astype(jnp.bfloat16)
        query_grad = (
            jnp.einsum("hqk,khd->qhd", score_grad, key_block, preferred_element_type=jnp.float32)
            * factor
        )
        key_part = (
            jnp.einsum("hqk,qhd->khd", score_grad, query_block, preferred_element_type=jnp.float32)
            * factor
        )
        value_part = jnp.einsum(
            "hqk,qhd->khd",
            softmax_probs.astype(jnp.bfloat16),
            grad_block,
            preferred_element_type=jnp.float32,
        )
        key_grad = key_grad + key_part
        value_grad = value_grad + value_part
        return ((key_grad, value_grad), query_grad)

    zeros_start = jnp.zeros(key_heads.shape, jnp.float32)
    (key_grad, value_grad), query_grad = lax.scan(
        one_block, (zeros_start, zeros_start), jnp.arange(tokens // block_rows)
    )
    return (query_grad.reshape(key_heads.shape), key_grad, value_grad)


def local(
    inputs,
    first_gain,
    first_shift,
    project_in,
    project_bias,
    project_out,
    second_gain,
    second_shift,
    gate_weight,
    down_weight,
    cotangent,
):
    layers = project_in.shape[0]
    tokens = inputs.shape[0] * lax.axis_size("col")
    heads_here = project_in.shape[3] // lax.axis_size("row") // HEAD_DIM
    bias_width = project_bias.shape[2] // lax.axis_size("row")
    row_place = lax.axis_index("row")
    factor = 1.0 / math.sqrt(HEAD_DIM)
    cosine_table, sine_table = rotary_tables(tokens)
    stream = inputs.astype(jnp.float32)
    layer_index = 0
    normed_a, inv_root_a, low_a = norm_forward(
        stream, first_gain[layer_index], first_shift[layer_index]
    )
    full_a = gather_tokens(low_a)
    partial_mix = jnp.einsum(
        "sd,dtk->stk", full_a, project_in[layer_index], preferred_element_type=jnp.float32
    )
    bias_here = lax.dynamic_slice_in_dim(
        project_bias[layer_index], row_place * bias_width, bias_width, 1
    )
    mixed = (split_units(partial_mix) + bias_here[None]).reshape(tokens, 3, heads_here, HEAD_DIM)
    query_heads = rotate(mixed[:, 0], cosine_table, sine_table).astype(jnp.bfloat16)
    key_heads = rotate(mixed[:, 1], cosine_table, sine_table).astype(jnp.bfloat16)
    value_heads = mixed[:, 2].astype(jnp.bfloat16)
    attended, log_total = attend_forward(query_heads, key_heads, value_heads, factor)
    heads_full = join_units(attended.astype(jnp.bfloat16))
    residual = stream + branch_sum(heads_full, project_out[layer_index])
    normed_b, inv_root_b, low_b = norm_forward(
        residual, second_gain[layer_index], second_shift[layer_index]
    )
    full_b = gather_tokens(low_b)
    gate_up = split_units(
        jnp.einsum(
            "sd,dtf->stf", full_b, gate_weight[layer_index], preferred_element_type=jnp.float32
        )
    )
    hidden = (jax.nn.silu(gate_up[:, 0]) * gate_up[:, 1]).astype(jnp.bfloat16)
    hidden_full = join_units(hidden)
    layer_out = (residual + branch_sum(hidden_full, down_weight[layer_index])).astype(jnp.bfloat16)
    outputs = [layer_out]
    kept_a = None
    kept_b = None
    saved = [
        (
            normed_a,
            inv_root_a,
            kept_a,
            query_heads,
            key_heads,
            value_heads,
            log_total,
            heads_full,
            normed_b,
            inv_root_b,
            kept_b,
            gate_up,
            hidden_full,
        )
    ]
    gradient = cotangent.astype(jnp.float32)
    in_grads = [None] * layers
    bias_grads = [None] * layers
    out_grads = [None] * layers
    gate_grads = [None] * layers
    down_grads = [None] * layers
    gain_a_grads = [None] * layers
    shift_a_grads = [None] * layers
    gain_b_grads = [None] * layers
    shift_b_grads = [None] * layers
    for layer_index in reversed(range(layers)):
        (
            normed_a,
            inv_root_a,
            kept_a,
            query_heads,
            key_heads,
            value_heads,
            log_total,
            heads_full,
            normed_b,
            inv_root_b,
            kept_b,
            gate_up,
            hidden_full,
        ) = saved[layer_index]
        grad_full = gather_gradient(gradient.astype(jnp.bfloat16))
        down_grad = jnp.einsum(
            "sf,sd->fd", hidden_full, grad_full, preferred_element_type=jnp.float32
        )
        hidden_grad = split_unit_grads(
            jnp.einsum(
                "sd,fd->sf", grad_full, down_weight[layer_index], preferred_element_type=jnp.float32
            )
        )
        gate_value = gate_up[:, 0]
        up_value = gate_up[:, 1]
        sigmoid_gate = jax.nn.sigmoid(gate_value)
        gate_grad = (
            hidden_grad * up_value * sigmoid_gate * (1.0 + gate_value * (1.0 - sigmoid_gate))
        )
        up_grad = hidden_grad * gate_value * sigmoid_gate
        gate_up_grad = jnp.stack([gate_grad, up_grad], axis=1).astype(jnp.bfloat16)
        gate_up_full = join_unit_grads(gate_up_grad)
        gate_weight_grad = weight_product(
            normed_b, second_gain[layer_index], second_shift[layer_index], gate_up_full
        )
        normed_b_grad = input_sum(gate_up_full, gate_weight[layer_index])
        back_b, gain_b_grad, shift_b_grad = norm_backward(
            normed_b_grad, normed_b, inv_root_b, second_gain[layer_index]
        )
        gradient_two = gradient + back_b
        grad_two_full = gather_gradient(gradient_two.astype(jnp.bfloat16))
        out_grad_weight = jnp.einsum(
            "sk,sd->kd", heads_full, grad_two_full, preferred_element_type=jnp.float32
        )
        attended_grad = split_unit_grads(
            jnp.einsum(
                "sd,kd->sk",
                grad_two_full,
                project_out[layer_index],
                preferred_element_type=jnp.float32,
            )
        )
        attended_grad = attended_grad.astype(jnp.bfloat16).reshape(tokens, heads_here, HEAD_DIM)
        query_grad, key_grad, value_grad = attend_backward(
            query_heads, key_heads, value_heads, attended_grad, log_total, factor
        )
        query_grad = rotate(query_grad, cosine_table, -sine_table)
        key_grad = rotate(key_grad, cosine_table, -sine_table)
        mixed_grad = (
            jnp.stack([query_grad, key_grad, value_grad], axis=1)
            .reshape(tokens, 3, heads_here * HEAD_DIM)
            .astype(jnp.bfloat16)
        )
        mixed_full = join_unit_grads(mixed_grad)
        bias_grad = jnp.sum(mixed_full, axis=0, dtype=jnp.float32)
        in_grad = weight_product(
            normed_a, first_gain[layer_index], first_shift[layer_index], mixed_full
        )
        normed_a_grad = input_sum(mixed_full, project_in[layer_index])
        back_a, gain_a_grad, shift_a_grad = norm_backward(
            normed_a_grad, normed_a, inv_root_a, first_gain[layer_index]
        )
        gradient = gradient_two + back_a
        in_grads[layer_index] = in_grad
        bias_grads[layer_index] = bias_grad
        out_grads[layer_index] = out_grad_weight
        gate_grads[layer_index] = gate_weight_grad
        down_grads[layer_index] = down_grad
        gain_a_grads[layer_index] = gain_a_grad
        shift_a_grads[layer_index] = shift_a_grad
        gain_b_grads[layer_index] = gain_b_grad
        shift_b_grads[layer_index] = shift_b_grad
    stack_in = jnp.stack(in_grads)
    stack_bias = jnp.stack(bias_grads)
    stack_out = jnp.stack(out_grads)
    stack_gate = jnp.stack(gate_grads)
    stack_down = jnp.stack(down_grads)
    stack_in, stack_bias, stack_out, stack_gate, stack_down = (
        lax.psum(stack_in.astype(jnp.bfloat16), "dp").astype(jnp.float32),
        lax.psum(stack_bias.astype(jnp.bfloat16), "dp").astype(jnp.float32),
        lax.psum(stack_out.astype(jnp.bfloat16), "dp").astype(jnp.float32),
        lax.psum(stack_gate.astype(jnp.bfloat16), "dp").astype(jnp.float32),
        lax.psum(stack_down.astype(jnp.bfloat16), "dp").astype(jnp.float32),
    )
    gain_a_total, shift_a_total, gain_b_total, shift_b_total = lax.psum(
        (
            jnp.stack(gain_a_grads),
            jnp.stack(shift_a_grads),
            jnp.stack(gain_b_grads),
            jnp.stack(shift_b_grads),
        ),
        ("dp", "col"),
    )
    return (
        jnp.stack(outputs),
        gradient,
        gain_a_total,
        shift_a_total,
        stack_in,
        stack_bias,
        stack_out,
        gain_b_total,
        shift_b_total,
        stack_gate,
        stack_down,
    )


def solution(mesh):
    return jax.shard_map(
        local,
        mesh=mesh,
        in_specs=(
            P(("dp", "col"), "row"),
            P(None, "row"),
            P(None, "row"),
            P(None, "row", None, "col"),
            P(None, None, "col"),
            P(None, "col", "row"),
            P(None, "row"),
            P(None, "row"),
            P(None, "row", None, "col"),
            P(None, "col", "row"),
            P(("dp", "col"), "row"),
        ),
        out_specs=(
            P(None, ("dp", "col"), "row"),
            P(("dp", "col"), "row"),
            P(None, "row"),
            P(None, "row"),
            P(None, "row", None, "col"),
            P(None, None, "col"),
            P(None, "col", "row"),
            P(None, "row"),
            P(None, "row"),
            P(None, "row", None, "col"),
            P(None, "col", "row"),
        ),
        check_vma=False,
    )
```

profile of v0, /device:TPU:0, one launch (start us, length us, event | category | flops | bytes accessed | tf_op | source)
XLA Modules:
  0.0 1484.0 jit_solution(7739865274060016093)
XLA Ops:
  17.3 47.9 %all-gather.9.cloned.1.call-done = bf16[1024,1024]{1,0:T(8,128)(2,1)} async-done(((bf16[256,1024]{1,0:T(8,128)(2,1)}), bf16[1024,1024]{1,0:T(8,128)(2,1)}) %all-gather.9.cloned.1.call-update) | async-done | bytes 2097168 | tf_op jit(solution)/shard_map/all_gather | solution.py:64
  73.6 74.4 %reduce-scatter.9.cloned.1.call-done = f32[1024,3,256]{2,0,1:T(8,128)} async-done(((f32[1024,3,512]{2,0,1:T(8,128)}), f32[1024,3,256]{2,0,1:T(8,128)}) %reduce-scatter.9.cloned.1.call-update) | async-done | bytes 3145744 | tf_op jit(solution)/shard_map/reduce_scatter | solution.py:72
  160.4 21.1 %while.31 = (s32[]{:T(128)}, bf16[2,512,4,64]{1,3,2,0:T(8,128)(2,1)}, f32[2,4,512]{2,1,0:T(4,128)S(1)}, s32[2]{0:T(128)S(1)}, bf16[1024,4,64]{0,2,1:T(8,128)(2,1...) while((s32[]{:T(128)}, ...), condition=%wide.region_8.9_spmd, body=%wide.region_5.8_spmd.sunk | while | flops 562559488 | bytes 35459536 | solution.py:147
  184.1 21.4 %all-gather.11.cloned.1.call-done = bf16[1024,512]{0,1:T(8,128)(2,1)} async-done(((bf16[1024,256]{0,1:T(8,128)(2,1)}), bf16[1024,512]{0,1:T(8,128)(2,1)}) %all-gather.11.cloned.1.call-update) | async-done | bytes 1048592 | tf_op jit(solution)/shard_map/all_gather | solution.py:76
  211.0 76.3 %reduce-scatter.11.cloned.1.call-done = f32[256,1024]{1,0:T(8,128)} async-done(((f32[1024,1024]{1,0:T(8,128)}), f32[256,1024]{1,0:T(8,128)}) %reduce-scatter.11.cloned.1.call-update) | async-done | bytes 1048592 | tf_op jit(solution)/shard_map/reduce_scatter | solution.py:88
  297.3 37.9 %all-gather.17.cloned.1.call-done = bf16[1024,1024]{1,0:T(8,128)(2,1)} async-done(((bf16[256,1024]{1,0:T(8,128)(2,1)}), bf16[1024,1024]{1,0:T(8,128)(2,1)}) %all-gather.17.cloned.1.call-update) | async-done | bytes 2097168 | tf_op jit(solution)/shard_map/all_gather | solution.py:68
  343.5 38.4 %all-gather.13.cloned.1.call-done = bf16[1024,1024]{1,0:T(8,128)(2,1)} async-done(((bf16[256,1024]{1,0:T(8,128)(2,1)}), bf16[1024,1024]{1,0:T(8,128)(2,1)}) %all-gather.13.cloned.1.call-update) | async-done | bytes 2097168 | tf_op jit(solution)/shard_map/all_gather | solution.py:64
  381.9 11.9 fusion.35
  393.9 61.0 %reduce-scatter.17.cloned.1.call-done = f32[1024,704]{0,1:T(8,128)} async-done(((f32[1024,1408]{0,1:T(8,128)}), f32[1024,704]{0,1:T(8,128)}) %reduce-scatter.17.cloned.1.call-update) | async-done | bytes 2883600 | tf_op jit(solution)/shard_map/reduce_scatter | solution.py:80
  454.9 136.2 %reduce-scatter.13.cloned.1.call-done = f32[1024,2,704]{0,2,1:T(8,128)} async-done(((f32[1024,2,1408]{0,2,1:T(8,128)}), f32[1024,2,704]{0,2,1:T(8,128)}) %reduce-scatter.13.cloned.1.call-update) | async-done | bytes 5767184 | tf_op jit(solution)/shard_map/reduce_scatter | solution.py:72
  598.9 74.0 %all-gather.19.cloned.1.call-done = bf16[1024,2,1408]{0,2,1:T(8,128)(2,1)} async-done(((bf16[1024,2,704]{0,2,1:T(8,128)(2,1)}), bf16[1024,2,1408]{0,2,1:T(8,128)(2,1)}) %all-gather.19.cloned.1.call-update) | async-done | bytes 5767184 | tf_op jit(solution)/shard_map/all_gather | solution.py:84
  672.9 11.5 fusion.51
  684.4 32.5 %all-gather.15.cloned.1.call-done = bf16[1024,1408]{0,1:T(8,128)(2,1)} async-done(((bf16[1024,704]{0,1:T(8,128)(2,1)}), bf16[1024,1408]{0,1:T(8,128)(2,1)}) %all-gather.15.cloned.1.call-update) | async-done | bytes 2883600 | tf_op jit(solution)/shard_map/all_gather | solution.py:76
  725.2 71.5 %reduce-scatter.19.cloned.1.call-done = f32[256,1024]{1,0:T(8,128)} async-done(((f32[1024,1024]{1,0:T(8,128)}), f32[256,1024]{1,0:T(8,128)}) %reduce-scatter.19.cloned.1.call-update) | async-done | bytes 1048592 | tf_op jit(solution)/shard_map/reduce_scatter | solution.py:97
  804.2 72.5 %reduce-scatter.15.cloned.1.call-done = f32[256,1024]{1,0:T(8,128)} async-done(((f32[1024,1024]{1,0:T(8,128)}), f32[256,1024]{1,0:T(8,128)}) %reduce-scatter.15.cloned.1.call-update) | async-done | bytes 1048592 | tf_op jit(solution)/shard_map/reduce_scatter | solution.py:88
  880.6 46.6 %all-gather.21.cloned.1.call-done = bf16[1024,1024]{1,0:T(8,128)(2,1)} async-done(((bf16[256,1024]{1,0:T(8,128)(2,1)}), bf16[1024,1024]{1,0:T(8,128)(2,1)}) %all-gather.21.cloned.1.call-update) | async-done | bytes 2097168 | tf_op jit(solution)/shard_map/all_gather | solution.py:68
  940.3 22.0 %reduce-scatter.21.cloned.1.call-done = f32[1024,256]{1,0:T(8,128)} async-done(((f32[1024,512]{1,0:T(8,128)}), f32[1024,256]{1,0:T(8,128)}) %reduce-scatter.21.cloned.1.call-update) | async-done | bytes 1048592 | tf_op jit(solution)/shard_map/reduce_scatter | solution.py:80
  966.5 61.6 %while.32 = (s32[]{:T(128)}, f32[1024,4,64]{0,2,1:T(8,128)}, f32[1024,4,64]{0,2,1:T(8,128)}, f32[2,512,4,64]{1,0,3,2:T(2,128)}, s32[2]{0:T(128)S(1)}, /*index=5*...) while((s32[]{:T(128)}, f32[1024,4,64]{0,2,1:T(8,128)}, ...), condition=%wide.region_25.26_spmd.clone, body=%wide.region_23.25_spmd.clone.sunk | while | flops 1375599104 | bytes 91288184 | solution.py:186
  1056.4 11.2 convert_bitcast_fusion
  1069.9 24.0 %all-gather.23.cloned.1.call-done = bf16[1024,3,512]{2,0,1:T(8,128)(2,1)} async-done(((bf16[1024,3,256]{2,0,1:T(8,128)(2,1)}), bf16[1024,3,512]{2,0,1:T(8,128)(2,1)}) %all-gather.23.cloned.1.call-update) | async-done | bytes 3145744 | tf_op jit(solution)/shard_map/all_gather | solution.py:84
  1119.4 208.6 %all-reduce.8.cloned.1.call-done = (bf16[1,1024,2,1408]{3,1,2,0:T(8,128)(2,1)}, bf16[1,1024,3,512]{3,1,2,0:T(8,128)(2,1)}, bf16[1,512,1024]{2,1,0:T(8,128)(2,1)}, bf16[1,1408,1024]{2,1,0:T(8,128)(2,1)}) async-done(((bf16[1,1024,2,1408]{3,1,2,0:T(8,128)(2,1)}, bf16[1,1024,3,512]{3,1,2,0:T(8,128)(2,1)}, bf16[1,512,1024]{2,1,0:T(8,128)(2,1)}, bf16[1,1408,1024]{2,1,0:T(8,128)(2,1)}), ...) | async-done | bytes 12845072 | tf_op jit(solution)/shard_map/psum | solution.py:366
  1330.8 12.8 copy.45
  1350.5 56.6 %reduce-scatter.23.cloned.1.call-done = f32[256,1024]{1,0:T(8,128)} async-done(((f32[1024,1024]{1,0:T(8,128)}), f32[256,1024]{1,0:T(8,128)}) %reduce-scatter.23.cloned.1.call-update) | async-done | bytes 1048592 | tf_op jit(solution)/shard_map/reduce_scatter | solution.py:97
  1413.9 59.9 %all-reduce = (f32[1,1024]{1,0:T(1,128)}, f32[1,1024]{1,0:T(1,128)}, f32[1,1024]{1,0:T(1,128)}, f32[1,1024]{1,0:T(1,128)}) all-reduce(f32[1,1024]{1,0:T(1,128)S(1)} %bitcast.186, f32[1,1024]{1,0:T(1,128)S(1)} %bitcast.187, f32[1,1024]{1,0:T(1,128)S(1)} %bitcast.184, ...), channel_id=1, replica_groups=mesh['dp'=4,'row'=2,'col'=4] {'dp','col'}, use_global_device_ids=true, to_apply=%region_32.33 | all-reduce | flops 4096 | bytes 32768 | tf_op jit(solution)/shard_map/psum | solution.py:369
  (211 shorter events, 253.3 us)
Async XLA Ops:
  7.2 58.0 %all-gather.9.cloned.1.call-start = ((), (), s32[]{:S(2)}) async-start(), calls=%async_computation.8 | async-start | bytes 2621440 | tf_op jit(solution)/shard_map/all_gather | solution.py:64
  17.2 130.7 %reduce-scatter.9.cloned.1.call-start = ((), (), s32[]{:S(2)}) async-start(), calls=%async_computation.9 | async-start | bytes 9437184 | tf_op jit(solution)/shard_map/reduce_scatter | solution.py:72
  72.0 133.5 %all-gather.11.cloned.1.call-start = ((), (), s32[]{:S(2)}) async-start(), calls=%async_computation.10 | async-start | bytes 1572864 | tf_op jit(solution)/shard_map/all_gather | solution.py:76
  73.6 85.7 %copy-start.13 = (f32[1024,8]{0,1:T(8,128)}, f32[1024,8]{0,1:T(8,128)S(1)}, u32[]{:S(2)}) copy-start(f32[1024,8]{0,1:T(8,128)S(1)} %get-tuple-element.389) | copy-start | bytes 98308
  184.0 103.3 %reduce-scatter.11.cloned.1.call-start = ((), (), s32[]{:S(2)}) async-start(), calls=%async_computation.11 | async-start | bytes 5242880 | tf_op jit(solution)/shard_map/reduce_scatter | solution.py:88
  210.4 84.3 %copy-start.15 = (f32[1,1024]{1,0:T(1,128)S(1)}, f32[1,1024]{1,0:T(1,128)}, u32[]{:S(2)}) copy-start(f32[1,1024]{1,0:T(1,128)} %param.21) | copy-start | bytes 12292
  210.4 84.3 %copy-start.22 = (f32[1,1024]{1,0:T(1,128)S(1)}, f32[1,1024]{1,0:T(1,128)}, u32[]{:S(2)}) copy-start(f32[1,1024]{1,0:T(1,128)} %param.22) | copy-start | bytes 12292
  210.4 124.9 %all-gather.17.cloned.1.call-start = ((), (), s32[]{:S(2)}) async-start(), calls=%async_computation.16 | async-start | bytes 2621440 | tf_op jit(solution)/shard_map/all_gather | solution.py:68
  211.0 170.9 %all-gather.13.cloned.1.call-start = ((), (), s32[]{:S(2)}) async-start(), calls=%async_computation.12 | async-start | bytes 2621440 | tf_op jit(solution)/shard_map/all_gather | solution.py:64
  297.0 157.9 %reduce-scatter.17.cloned.1.call-start = ((), (), s32[]{:S(2)}) async-start(), calls=%async_computation.17 | async-start | bytes 8650752 | tf_op jit(solution)/shard_map/reduce_scatter | solution.py:80
  343.4 247.6 %reduce-scatter.13.cloned.1.call-start = ((), (), s32[]{:S(2)}) async-start(), calls=%async_computation.13 | async-start | bytes 17301504 | tf_op jit(solution)/shard_map/reduce_scatter | solution.py:72
  393.8 279.0 %all-gather.19.cloned.1.call-start = ((), (), s32[]{:S(2)}) async-start(), calls=%async_computation.18 | async-start | bytes 8650752 | tf_op jit(solution)/shard_map/all_gather | solution.py:84
  598.2 118.7 %all-gather.15.cloned.1.call-start = ((), (), s32[]{:S(2)}) async-start(), calls=%async_computation.14 | async-start | bytes 4325376 | tf_op jit(solution)/shard_map/all_gather | solution.py:76
  598.8 197.9 %reduce-scatter.19.cloned.1.call-start = ((), (), s32[]{:S(2)}) async-start(), calls=%async_computation.19 | async-start | bytes 5242880 | tf_op jit(solution)/shard_map/reduce_scatter | solution.py:97
  684.4 192.3 %reduce-scatter.15.cloned.1.call-start = ((), (), s32[]{:S(2)}) async-start(), calls=%async_computation.15 | async-start | bytes 5242880 | tf_op jit(solution)/shard_map/reduce_scatter | solution.py:88
  725.1 202.1 %all-gather.21.cloned.1.call-start = ((), (), s32[]{:S(2)}) async-start(), calls=%async_computation.20 | async-start | bytes 2621440 | tf_op jit(solution)/shard_map/all_gather | solution.py:68
  880.6 81.8 %reduce-scatter.21.cloned.1.call-start = ((), (), s32[]{:S(2)}) async-start(), calls=%async_computation.21 | async-start | bytes 3145728 | tf_op jit(solution)/shard_map/reduce_scatter | solution.py:80
  931.7 162.2 %all-gather.23.cloned.1.call-start = ((), (), s32[]{:S(2)}) async-start(), calls=%async_computation.22 | async-start | bytes 4718592 | tf_op jit(solution)/shard_map/all_gather | solution.py:84
  1048.8 279.2 %all-reduce.8.cloned.1.call-start = ((), (), s32[]{:S(2)}) async-start(), calls=%async_computation.24 | async-start | bytes 25690112 | tf_op jit(solution)/shard_map/psum | solution.py:366
  1101.6 305.5 %reduce-scatter.23.cloned.1.call-start = ((), (), s32[]{:S(2)}) async-start(), calls=%async_computation.23 | async-start | bytes 5242880 | tf_op jit(solution)/shard_map/reduce_scatter | solution.py:97
  1346.8 60.3 %copy-start.19 = (f32[256]{0:T(256)S(1)}, f32[256]{0:T(256)}, u32[]{:S(2)}) copy-start(f32[256]{0:T(256)} %copy-done.18) | copy-start | bytes 3076
  1346.8 60.3 %copy-start.21 = (f32[256]{0:T(256)S(1)}, f32[256]{0:T(256)}, u32[]{:S(2)}) copy-start(f32[256]{0:T(256)} %copy-done.20) | copy-start | bytes 3076
  1346.8 67.1 %copy-start.16 = (f32[1024]{0:T(1024)S(1)}, f32[1024]{0:T(1024)}, u32[]{:S(2)}) copy-start(f32[1024]{0:T(1024)} %get-tuple-element.300) | copy-start | bytes 12292
  1346.8 67.1 %copy-start.17 = (f32[1024]{0:T(1024)S(1)}, f32[1024]{0:T(1024)}, u32[]{:S(2)}) copy-start(f32[1024]{0:T(1024)} %get-tuple-element.306) | copy-start | bytes 12292
  (28 other events, 202.2 us)
Sparse Core Ops, SparseCore 0:
  17.4 47.7 all-gather.8
  72.2 75.7 reduce-scatter.8
  184.2 21.3 all-gather.10
  210.5 76.7 reduce-scatter.10
  288.7 46.4 all-gather.16
  337.2 44.6 all-gather.12
  384.8 70.0 reduce-scatter.16
  457.9 133.1 reduce-scatter.12
  598.3 74.4 all-gather.18
  674.9 41.9 all-gather.14
  719.9 76.7 reduce-scatter.18
  799.4 77.2 reduce-scatter.14
  880.7 46.4 all-gather.20
  931.8 30.5 reduce-scatter.20
  1048.9 44.9 all-gather.22
  1101.7 226.2 all-reduce.7
  1330.1 76.9 reduce-scatter.22
where the time goes:
time: 1490 us; the launch traced here: 1480 us
  waiting for transfers between devices  1100 us (74%)
  matrix products  127 us (9%)
  blocking collectives  88.4 us (6%)
  other arithmetic  67.5 us (5%)
  local copies, waits for them, and re-layouts  66.9 us (4%)
    reduce_scatter x2, waiting for transfers between devices, split_units(): return lax.psum_scatter(partial_sum, 'row', scatter_dimension=2, tiled=True)  211 us
    psum x1, waiting for transfers between devices, local(): lax.psum(stack_gate.astype(jnp.bfloat16), 'dp').astype(jnp.float32)  209 us
    reduce_scatter x2, waiting for transfers between devices, branch_sum(): lax.psum_scatter(jnp.dot(full_rows, weight_block, preferred_element_type=...  149 us
    reduce_scatter x2, waiting for transfers between devices, input_sum(): lax.psum_scatter(jnp.einsum('stk,dtk->sd', grad_full, weight_block, prefe...  128 us
    all_gather x2, waiting for transfers between devices, join_unit_grads(): return lax.all_gather(local_units, 'row', axis=2, tiled=True)  98 us
    all_gather x2, waiting for transfers between devices, gather_tokens(): return lax.all_gather(local_low, 'col', axis=0, tiled=True)  86.3 us
    all_gather x2, waiting for transfers between devices, gather_gradient(): return lax.all_gather(local_low, 'col', axis=0, tiled=True)  84.5 us
    reduce_scatter x2, waiting for transfers between devices, split_unit_grads(): return lax.psum_scatter(partial_sum, 'row', scatter_dimension=1, tiled=True)  83 us
  transfers between devices with their start and end apart: 17, of which 17 were waited for; matrix products, arithmetic and copies ran while one was open for 7% of the time, Pallas kernels for 0%

commit v1 on v0

v1 whole, which is shorter than its diff:
```python
import functools
import math

import jax
import jax.numpy as jnp
from jax import lax
from jax.experimental import pallas as pl
from jax.experimental.pallas import tpu as pltpu
from jax.sharding import Mesh
from jax.sharding import PartitionSpec as P

HEAD_DIM = 64
ROT = 16
LENGTH = 1024
EPSILON = 1e-05
F32 = jnp.float32
BF16 = jnp.bfloat16
LANES = 128
MIB = 1 << 20


def swap(x, axis):
    return lax.ppermute(x, axis, [(0, 1), (1, 0)])


PAIR = [(0, 1), (1, 0), (2, 3), (3, 2)]
MID = [(1, 2), (2, 1)]
OUT = [(1, 0), (2, 3)]
IN = [(0, 1), (3, 2)]
ORDER4 = ((0, 1, 2, 3), (1, 0, 2, 3), (2, 3, 1, 0), (3, 2, 1, 0))


def slot_order(place, count):
    if count == 4:
        return jnp.array(ORDER4, jnp.int32)[place]
    return jnp.arange(count, dtype=jnp.int32)


def gather_slots(own, count):
    if count != 4:
        return lax.all_gather(own, "col", axis=0, tiled=True)
    one = lax.ppermute(own, "col", PAIR)
    mid = lax.ppermute(own, "col", MID)
    far = lax.ppermute(one, "col", MID)
    two = mid + lax.ppermute(mid, "col", OUT)
    three = far + lax.ppermute(far, "col", OUT)
    return jnp.concatenate([own, one, two, three], axis=0)


def scatter_slots(parts, count):
    rows = parts.shape[0] // count
    if count != 4:
        mine = lax.psum_scatter(parts, "col", scatter_dimension=0, tiled=True)
        return (mine, jnp.zeros_like(mine), jnp.zeros_like(mine))
    part = [parts[i * rows : (i + 1) * rows] for i in range(4)]
    three = part[3] + lax.ppermute(part[3], "col", IN)
    two = part[2] + lax.ppermute(part[2], "col", IN)
    one = part[1] + lax.ppermute(three, "col", MID)
    from_mid = lax.ppermute(two, "col", MID)
    from_pair = lax.ppermute(one, "col", PAIR)
    return (part[0], from_mid, from_pair)


def params(mib, axes=1):
    return pltpu.CompilerParams(
        vmem_limit_bytes=mib * MIB, dimension_semantics=("arbitrary",) * axes
    )


def cost(flops, moved, trans=0):
    return pl.CostEstimate(flops=int(flops), bytes_accessed=int(moved), transcendentals=int(trans))


def stats_of(value):
    width = value.shape[1]
    average = jnp.sum(value, axis=1, keepdims=True) / width
    centred = value - average
    variance = jnp.sum(centred * centred, axis=1, keepdims=True) / width
    inv_root = lax.rsqrt(variance + EPSILON)
    return centred * inv_root, inv_root


def norm_first(stream, gain, shift):
    rows, width = stream.shape
    block = rows // 4

    def body(x_ref, gain_ref, shift_ref, low_ref):
        xhat, unused = stats_of(x_ref[...].astype(F32))
        low_ref[...] = (xhat * gain_ref[...] + shift_ref[...]).astype(BF16)

    row = pl.BlockSpec((block, width), lambda i: (i, 0))
    flat = pl.BlockSpec((1, width), lambda i: (0, 0))
    return pl.pallas_call(
        body,
        grid=(4,),
        in_specs=[row, flat, flat],
        out_specs=row,
        out_shape=jax.ShapeDtypeStruct((rows, width), BF16),
        compiler_params=params(16),
        cost_estimate=cost(rows * width * 10, rows * width * 4),
        name="norm_first",
    )(stream, gain, shift)


def norm_second(stream, terms, gain, shift):
    rows, width = stream.shape
    block = rows // 4

    def body(x_ref, a_ref, b_ref, c_ref, gain_ref, shift_ref, res_ref, low_ref):
        residual = (
            x_ref[...].astype(F32)
            + a_ref[...].astype(F32)
            + b_ref[...].astype(F32)
            + c_ref[...].astype(F32)
        )
        res_ref[...] = residual
        xhat, unused = stats_of(residual)
        low_ref[...] = (xhat * gain_ref[...] + shift_ref[...]).astype(BF16)

    row = pl.BlockSpec((block, width), lambda i: (i, 0))
    flat = pl.BlockSpec((1, width), lambda i: (0, 0))
    return pl.pallas_call(
        body,
        grid=(4,),
        in_specs=[row] * 4 + [flat, flat],
        out_specs=[row, row],
        out_shape=[
            jax.ShapeDtypeStruct((rows, width), F32),
            jax.ShapeDtypeStruct((rows, width), BF16),
        ],
        compiler_params=params(16),
        cost_estimate=cost(rows * width * 12, rows * width * 14),
        name="norm_second",
    )(stream, *terms, gain, shift)


def norm_back(stream, terms, upper, gain, both):
    rows, width = stream.shape
    block = rows // 4

    def body(x_ref, a_ref, b_ref, c_ref, up_ref, gain_ref, low_ref, sums_ref, *full_ref):
        xhat, inv_root = stats_of(x_ref[...].astype(F32))
        grad = a_ref[...].astype(F32) + b_ref[...].astype(F32) + c_ref[...].astype(F32)
        scaled = grad * gain_ref[...]
        mean_scaled = jnp.sum(scaled, axis=1, keepdims=True) / width
        mean_cross = jnp.sum(scaled * xhat, axis=1, keepdims=True) / width
        result = up_ref[...].astype(F32) + inv_root * (scaled - mean_scaled - xhat * mean_cross)
        low_ref[...] = result.astype(BF16)
        if full_ref:
            full_ref[0][...] = result

        @pl.when(pl.program_id(0) == 0)
        def _():
            sums_ref[...] = jnp.zeros_like(sums_ref)

        sums_ref[...] += jnp.concatenate(
            [
                jnp.sum(grad * xhat, axis=0, keepdims=True),
                jnp.sum(grad, axis=0, keepdims=True),
            ],
            axis=0,
        )

    row = pl.BlockSpec((block, width), lambda i: (i, 0))
    flat = pl.BlockSpec((1, width), lambda i: (0, 0))
    sums = pl.BlockSpec((2, width), lambda i: (0, 0))
    return pl.pallas_call(
        body,
        grid=(4,),
        in_specs=[row] * 5 + [flat],
        out_specs=[row, sums] + [row] * both,
        out_shape=[
            jax.ShapeDtypeStruct((rows, width), BF16),
            jax.ShapeDtypeStruct((2, width), F32),
        ]
        + [jax.ShapeDtypeStruct((rows, width), F32)] * both,
        compiler_params=params(24),
        cost_estimate=cost(rows * width * 20, rows * width * 18),
        name="norm_back",
    )(stream, *terms, upper, gain)


def roll_lanes(value, shift):
    return pltpu.roll(value, shift % value.shape[1], 1)


def turn(value, table, sign):
    times = value.shape[1] // LANES
    wide = [jnp.concatenate([table[i]] * times, axis=1) for i in range(3)]
    ahead = roll_lanes(value, -(ROT // 2))
    behind = roll_lanes(value, ROT // 2)
    moved = ahead * wide[1] + behind * wide[2]
    return value * wide[0] + (moved if sign > 0 else -moved)


def qkv_columns(tokens, weight, bias, table, half):
    rows, width = tokens.shape
    columns = weight.shape[2] // 2

    def body(half_ref, x_ref, w_ref, bias_ref, table_ref, out_ref):
        which = pl.program_id(0)
        acc = jnp.dot(x_ref[...], w_ref[0], preferred_element_type=F32) + bias_ref[0]

        @pl.when(which < 2)
        def _():
            out_ref[0] = turn(acc, table_ref, 1).astype(BF16)

        @pl.when(which == 2)
        def _():
            out_ref[0] = acc.astype(BF16)

    return pl.pallas_call(
        body,
        grid_spec=pltpu.PrefetchScalarGridSpec(
            num_scalar_prefetch=1,
            grid=(3,),
            in_specs=[
                pl.BlockSpec((rows, width), lambda j, h: (0, 0)),
                pl.BlockSpec((1, width, columns), lambda j, h: (j, 0, h[0])),
                pl.BlockSpec((1, 1, columns), lambda j, h: (j, 0, h[0])),
                pl.BlockSpec((3, rows, LANES), lambda j, h: (0, 0, 0)),
            ],
            out_specs=pl.BlockSpec((1, rows, columns), lambda j, h: (j, 0, 0)),
        ),
        out_shape=jax.ShapeDtypeStruct((3, rows, columns), BF16),
        compiler_params=params(40),
        cost_estimate=cost(6 * rows * width * columns, 2 * (rows * width + 3 * columns * width)),
        name="qkv_columns",
    )(half, tokens, weight, bias, table)


def place_of(order_ref, slot, core, rows):
    return pl.multiple_of((order_ref[1 + slot] * 2 + core) * rows, rows)


CHUNK = 256


def score_chunk(query, key, first, factor):
    scores = (
        lax.dot_general(query, key, (((1,), (1,)), ((), ())), preferred_element_type=F32) * factor
    )
    at_query = first + lax.broadcasted_iota(jnp.int32, scores.shape, 0)
    at_key = lax.broadcasted_iota(jnp.int32, scores.shape, 1)
    return jnp.where(at_query >= at_key, scores, -jnp.inf)


def attend(mine, other, order, factor):
    unused, rows, columns = mine.shape
    slots = order.shape[0] - 1
    piece = rows // slots
    length = 2 * rows

    def body(order_ref, mine_ref, other_ref, out_mine, out_other, lse_ref, whole, result):
        core = order_ref[0]
        for slot in range(slots):
            here = slice(slot * piece, (slot + 1) * piece)
            whole[:, pl.ds(place_of(order_ref, slot, core, piece), piece), :] = mine_ref[:, here, :]
            whole[:, pl.ds(place_of(order_ref, slot, 1 - core, piece), piece), :] = other_ref[
                :, here, :
            ]
        for head in range(LANES // HEAD_DIM):
            lanes = slice(head * HEAD_DIM, (head + 1) * HEAD_DIM)
            for first in range(0, length, CHUNK):
                upto = first + CHUNK
                scores = score_chunk(
                    whole[0, first:upto, lanes], whole[1, :upto, lanes], first, factor
                )
                highest = jnp.max(scores, axis=1, keepdims=True)
                exponent = jnp.exp(scores - highest)
                summed = jnp.sum(exponent, axis=1, keepdims=True)
                probs = (exponent * (1.0 / summed)).astype(BF16)
                result[first:upto, lanes] = jnp.dot(
                    probs, whole[2, :upto, lanes], preferred_element_type=F32
                ).astype(BF16)
                lse_ref[0, first:upto, head : head + 1] = highest + jnp.log(summed)
        for slot in range(slots):
            here = slice(slot * piece, (slot + 1) * piece)
            out_mine[here, :] = result[pl.ds(place_of(order_ref, slot, core, piece), piece), :]
            out_other[here, :] = result[pl.ds(place_of(order_ref, slot, 1 - core, piece), piece), :]

    groups = columns // LANES
    three = pl.BlockSpec((3, rows, LANES), lambda g, o: (0, 0, g))
    one = pl.BlockSpec((rows, LANES), lambda g, o: (0, g))
    return pl.pallas_call(
        body,
        grid_spec=pltpu.PrefetchScalarGridSpec(
            num_scalar_prefetch=1,
            grid=(groups,),
            in_specs=[three, three],
            out_specs=[one, one, pl.BlockSpec((1, length, 2), lambda g, o: (g, 0, 0))],
            scratch_shapes=[
                pltpu.VMEM((3, length, LANES), BF16),
                pltpu.VMEM((length, LANES), BF16),
            ],
        ),
        out_shape=[
            jax.ShapeDtypeStruct((rows, columns), BF16),
            jax.ShapeDtypeStruct((rows, columns), BF16),
            jax.ShapeDtypeStruct((groups, length, 2), F32),
        ],
        compiler_params=params(48),
        cost_estimate=cost(
            4 * length * length * columns, 16 * rows * columns, columns * length * length / 128
        ),
        name="attend",
    )(order, mine, other)


def attend_back(mine, other, grad_mine, grad_other, lse, table_mine, table_other, order, factor):
    unused, rows, columns = mine.shape
    slots = order.shape[0] - 1
    piece = rows // slots
    length = 2 * rows
    across = (((1,), (1,)), ((), ()))
    down = (((0,), (0,)), ((), ()))

    def body(
        order_ref,
        mine_ref,
        other_ref,
        gm_ref,
        go_ref,
        lse_ref,
        tm_ref,
        to_ref,
        out_mine,
        out_other,
        bias_ref,
        whole,
        grads,
        dq_ref,
        dkv_ref,
    ):
        core = order_ref[0]
        for slot in range(slots):
            here = slice(slot * piece, (slot + 1) * piece)
            one = pl.ds(place_of(order_ref, slot, core, piece), piece)
            two = pl.ds(place_of(order_ref, slot, 1 - core, piece), piece)
            whole[:, one, :] = mine_ref[:, here, :]
            whole[:, two, :] = other_ref[:, here, :]
            grads[one, :] = gm_ref[here, :]
            grads[two, :] = go_ref[here, :]
        heads = LANES // HEAD_DIM
        for head in range(heads):
            lanes = slice(head * HEAD_DIM, (head + 1) * HEAD_DIM)
            for first in reversed(range(0, length, CHUNK)):
                upto = first + CHUNK
                query = whole[0, first:upto, lanes]
                key = whole[1, :upto, lanes]
                value = whole[2, :upto, lanes]
                grad = grads[first:upto, lanes]
                scores = score_chunk(query, key, first, factor)
                probs = jnp.exp(scores - lse_ref[0, first:upto, head : head + 1])
                probs_grad = lax.dot_general(grad, value, across, preferred_element_type=F32)
                shift = jnp.sum(probs * probs_grad, axis=1, keepdims=True)
                scores_grad = (probs * (probs_grad - shift)).astype(BF16)
                dq_ref[first:upto, lanes] = (
                    jnp.dot(scores_grad, key, preferred_element_type=F32) * factor
                )
                dk = lax.dot_general(scores_grad, query, down, preferred_element_type=F32) * factor
                dv = lax.dot_general(
                    probs.astype(BF16), grad, down, preferred_element_type=F32
                )
                if upto == length:
                    dkv_ref[0, :, lanes] = dk
                    dkv_ref[1, :, lanes] = dv
                else:
                    dkv_ref[0, :upto, lanes] += dk
                    dkv_ref[1, :upto, lanes] += dv
        total = [jnp.zeros((1, LANES), F32) for _ in range(3)]
        for slot in range(slots):
            here = slice(slot * piece, (slot + 1) * piece)
            for at, table, out in (
                (core, tm_ref, out_mine),
                (1 - core, to_ref, out_other),
            ):
                rows_at = pl.ds(place_of(order_ref, slot, at, piece), piece)
                angles = table[:, here, :]
                parts = (
                    turn(dq_ref[rows_at, :], angles, -1).astype(BF16),
                    turn(dkv_ref[0, rows_at, :], angles, -1).astype(BF16),
                    dkv_ref[1, rows_at, :].astype(BF16),
                )
                for i in range(3):
                    out[i, here, :] = parts[i]
                    total[i] += jnp.sum(parts[i].astype(F32), axis=0, keepdims=True)
        for i in range(3):
            bias_ref[i] = total[i]

    groups = columns // LANES
    three = pl.BlockSpec((3, rows, LANES), lambda g, o: (0, 0, g))
    one = pl.BlockSpec((rows, LANES), lambda g, o: (0, g))
    full = pl.BlockSpec((3, rows, LANES), lambda g, o: (0, 0, 0))
    return pl.pallas_call(
        body,
        grid_spec=pltpu.PrefetchScalarGridSpec(
            num_scalar_prefetch=1,
            grid=(groups,),
            in_specs=[
                three,
                three,
                one,
                one,
                pl.BlockSpec((1, length, 2), lambda g, o: (g, 0, 0)),
                full,
                full,
            ],
            out_specs=[three, three, pl.BlockSpec((3, 1, LANES), lambda g, o: (0, 0, g))],
            scratch_shapes=[
                pltpu.VMEM((3, length, LANES), BF16),
                pltpu.VMEM((length, LANES), BF16),
                pltpu.VMEM((length, LANES), F32),
                pltpu.VMEM((2, length, LANES), F32),
            ],
        ),
        out_shape=[
            jax.ShapeDtypeStruct((3, rows, columns), BF16),
            jax.ShapeDtypeStruct((3, rows, columns), BF16),
            jax.ShapeDtypeStruct((3, 1, columns), F32),
        ],
        compiler_params=params(52),
        cost_estimate=cost(
            10 * length * length * columns, 40 * rows * columns, columns * length * length / 128
        ),
        name="attend_back",
    )(order, mine, other, grad_mine, grad_other, lse, table_mine, table_other)


def mlp(tokens, weight, hidden_grad):
    rows, width = tokens.shape
    units = weight.shape[2]
    block = LANES if units % LANES == 0 else units
    steps = units // block
    across = (((1,), (1,)), ((), ()))

    def body(x_ref, w_ref, hg_ref, hidden_ref, grad_ref, out_ref, acc):
        both = jnp.concatenate([w_ref[0], w_ref[1]], axis=1)
        gate_up = jnp.dot(x_ref[...], both, preferred_element_type=F32)
        gate, up = gate_up[:, :block], gate_up[:, block:]
        sigma = jax.nn.sigmoid(gate)
        silu = gate * sigma
        hidden_ref[...] = (silu * up).astype(BF16)
        grad = hg_ref[...].astype(F32)
        gate_grad = (grad * up * sigma * (1.0 + gate * (1.0 - sigma))).astype(BF16)
        up_grad = (grad * silu).astype(BF16)
        grad_ref[0] = gate_grad
        grad_ref[1] = up_grad
        part = lax.dot_general(
            jnp.concatenate([gate_grad, up_grad], axis=1), both, across, preferred_element_type=F32
        )
        step = pl.program_id(0)

        @pl.when(step == 0)
        def _():
            acc[...] = part

        @pl.when(step > 0)
        def _():
            acc[...] += part

        @pl.when(step == steps - 1)
        def _():
            out_ref[...] = acc[...].astype(BF16)

    return pl.pallas_call(
        body,
        grid=(steps,),
        in_specs=[
            pl.BlockSpec((rows, width), lambda j: (0, 0)),
            pl.BlockSpec((2, width, block), lambda j: (0, 0, j)),
            pl.BlockSpec((rows, block), lambda j: (0, j)),
        ],
        out_specs=[
            pl.BlockSpec((rows, block), lambda j: (0, j)),
            pl.BlockSpec((2, rows, block), lambda j: (0, 0, j)),
            pl.BlockSpec((rows, width), lambda j: (0, 0)),
        ],
        out_shape=[
            jax.ShapeDtypeStruct((rows, units), BF16),
            jax.ShapeDtypeStruct((2, rows, units), BF16),
            jax.ShapeDtypeStruct((rows, width), BF16),
        ],
        scratch_shapes=[pltpu.VMEM((rows, width), F32)],
        compiler_params=params(52),
        cost_estimate=cost(
            8 * rows * width * units, 4 * width * units + 4 * rows * width, rows * units
        ),
        name="mlp",
    )(tokens, weight, hidden_grad)


def rotary_table(position):
    half = ROT // 2
    frequency = 10000.0 ** (-(jnp.arange(half).astype(F32) * 2.0 / ROT))
    angles = position.astype(F32)[:, None] * frequency[None, :]
    cosine, sine = jnp.cos(angles), jnp.sin(angles)
    rest = HEAD_DIM - ROT
    count = position.shape[0]
    zero = jnp.zeros((count, half), F32)
    tail = jnp.zeros((count, rest), F32)
    keep = jnp.concatenate([cosine, cosine, tail + 1.0], axis=1)
    front = jnp.concatenate([-sine, zero, tail], axis=1)
    back = jnp.concatenate([zero, sine, tail], axis=1)
    return jnp.stack([jnp.concatenate([t, t], axis=1) for t in (keep, front, back)])


def local(
    inputs,
    first_gain,
    first_shift,
    project_in,
    project_bias,
    project_out,
    second_gain,
    second_shift,
    gate_weight,
    down_weight,
    cotangent,
):
    y_count = lax.axis_size("y")
    slots = lax.axis_size("col")
    y = lax.axis_index("y")
    core = lax.axis_index("core")
    row = lax.axis_index("row")
    place = lax.axis_index("col")
    factor = 1.0 / math.sqrt(HEAD_DIM)
    half_rows = inputs.shape[0] // 2
    wide = inputs.shape[1]
    width = 2 * wide

    def take(x, start, size, axis):
        return lax.dynamic_slice_in_dim(x, start, size, axis)

    straight = [(0, 0), (1, 2), (2, 1), (3, 3)]
    crossed = [(0, 2), (1, 0), (2, 3), (3, 1)]
    aligned = core == row

    def to_sequence(x):
        a = lax.ppermute(take(x, row * half_rows, half_rows, 0), ("core", "row"), straight)
        b = lax.ppermute(take(x, (1 - row) * half_rows, half_rows, 0), ("core", "row"), crossed)
        return jnp.concatenate([jnp.where(aligned, a, b), jnp.where(aligned, b, a)], axis=1)

    def from_sequence(x):
        own, oth = x[:, :wide], x[:, wide:]
        a = jnp.where(aligned, own, oth)
        b = jnp.where(aligned, oth, own)
        a = lax.ppermute(a, ("core", "row"), [(j, i) for i, j in straight])
        b = lax.ppermute(b, ("core", "row"), [(j, i) for i, j in crossed])
        top = jnp.where(row == 0, a, b)
        bottom = jnp.where(row == 0, b, a)
        return jnp.concatenate([top, bottom], axis=0)

    stream = to_sequence(inputs)

    vectors = jnp.concatenate([first_gain, first_shift, second_gain, second_shift], axis=0)
    vectors = jnp.concatenate([vectors, swap(vectors, "row")], axis=1)
    gain_a, shift_a, gain_b, shift_b = (vectors[i : i + 1] for i in range(4))

    def fetch(w, axis):
        size = w.shape[axis]
        pieces = []
        if y_count == 2:
            part = size // 4
            at = lambda c, yy: c * (size // 2) + yy * part
            first = swap(take(w, at(core, y), part, axis), "row")
            second = swap(first, "y")
            pieces = [
                (first, at(core, y)),
                (second, at(core, 1 - y)),
                (swap(first, "core"), at(1 - core, y)),
                (swap(second, "core"), at(1 - core, 1 - y)),
            ]
        else:
            part = size // 2
            first = swap(take(w, core * part, part, axis), "row")
            pieces = [(first, core * part), (swap(first, "core"), (1 - core) * part)]
        return pieces

    def assemble(w, pieces, cut, join):
        pads = [(0, w.shape[i] if i == join else 0, 0) for i in range(w.ndim)]
        full = lax.pad(w, jnp.zeros((), w.dtype), pads)
        for piece, start in pieces:
            at = [jnp.int32(0)] * w.ndim
            at[join] = jnp.int32(w.shape[join])
            at[cut] = at[cut] + start
            full = lax.dynamic_update_slice(full, piece, at)
        return full

    w_in = jnp.transpose(project_in[0], (1, 0, 2))
    w_in_full = assemble(w_in, fetch(w_in, 1), 1, 1)
    w_out = project_out[0]
    w_out_full = assemble(w_out, fetch(w_out, 0), 0, 1)
    w_down = down_weight[0]
    w_down_full = assemble(w_down, fetch(w_down, 0), 0, 1)
    w_gate = jnp.transpose(gate_weight[0], (1, 0, 2))
    w_gate_full = assemble(w_gate, fetch(w_gate, 1), 1, 1)

    order = slot_order(place, slots)
    table_of = jnp.concatenate([core[None], order]).astype(jnp.int32)
    inside = jnp.arange(half_rows)
    position = lambda c: ((order[:, None] * 2 + c) * half_rows + inside[None, :]).reshape(-1)
    rotary_mine = rotary_table(position(core))
    rotary_other = rotary_table(position(1 - core))

    tokens_a = gather_slots(norm_first(stream, gain_a, shift_a), slots)
    bias = project_bias[0][:, None, :]
    qkv_other = qkv_columns(tokens_a, w_in_full, bias, rotary_mine, (1 - core)[None])
    qkv_from = swap(qkv_other, "core")
    qkv_mine = qkv_columns(tokens_a, w_in_full, bias, rotary_mine, core[None])
    out_mine, out_other, lse = attend(qkv_mine, qkv_from, table_of, factor)
    out_from = swap(out_other, "core")
    attended = jnp.concatenate(
        [jnp.where(core == 0, out_mine, out_from), jnp.where(core == 0, out_from, out_mine)], axis=1
    )
    part_out = jnp.dot(attended, w_out_full, preferred_element_type=F32).astype(BF16)
    terms = scatter_slots(part_out, slots)
    residual, low_b = norm_second(stream, terms, gain_b, shift_b)

    cot = to_sequence(cotangent)
    grad_rows = gather_slots(cot, slots)
    hidden_grad = lax.dot_general(
        grad_rows, w_down_full, (((1,), (1,)), ((), ())), preferred_element_type=F32
    ).astype(BF16)

    tokens_b = gather_slots(low_b, slots)
    hidden, gate_up_grad, part_b = mlp(tokens_b, w_gate_full, hidden_grad)
    terms = scatter_slots(part_b, slots)
    g2_low, sums_b, g2 = norm_back(residual, terms, cot, gain_b, 1)

    part_down = jnp.dot(hidden, w_down_full, preferred_element_type=F32).astype(BF16)
    terms = scatter_slots(part_down, slots)
    layer_low = (residual + sum(t.astype(F32) for t in terms)).astype(BF16)
    layer_out = from_sequence(layer_low)

    g2_rows = gather_slots(g2_low, slots)
    attended_grad = lax.dot_general(
        g2_rows, w_out_full, (((1,), (1,)), ((), ())), preferred_element_type=F32
    ).astype(BF16)
    columns = attended_grad.shape[1] // 2
    grad_mine = take(attended_grad, core * columns, columns, 1)
    grad_from = swap(take(attended_grad, (1 - core) * columns, columns, 1), "core")
    mixed_mine, mixed_other, bias_part = attend_back(
        qkv_mine, qkv_from, grad_mine, grad_from, lse, rotary_mine, rotary_other, table_of, factor
    )
    mixed_from = swap(mixed_other, "core")
    mixed = jnp.concatenate(
        [
            jnp.where(core == 0, mixed_mine, mixed_from),
            jnp.where(core == 0, mixed_from, mixed_mine),
        ],
        axis=2,
    )
    part_a = lax.dot_general(
        mixed[0], w_in_full[0], (((1,), (1,)), ((), ())), preferred_element_type=F32
    )
    for i in (1, 2):
        part_a += lax.dot_general(
            mixed[i], w_in_full[i], (((1,), (1,)), ((), ())), preferred_element_type=F32
        )
    terms = scatter_slots(part_a.astype(BF16), slots)
    input_low, sums_a = norm_back(stream, terms, g2, gain_a, 0)
    input_grad = from_sequence(input_low).astype(F32)

    def sum_y(x):
        if y_count == 2:
            return (x.astype(F32) + swap(x, "y").astype(F32)).astype(x.dtype)
        return lax.psum(x, "y")

    def reduce_weight(grad, cut, join):
        size = grad.shape[cut] if cut != join else grad.shape[cut] // 2
        part = size // 2
        if cut == join:
            shape = list(grad.shape)
            shape[cut : cut + 1] = [2, size]
            grad = grad.reshape(shape)
            cut_at, join_at = cut + 1, join
        else:
            shape = list(grad.shape)
            shape[join : join + 1] = [2, grad.shape[join] // 2]
            cut_at, join_at = cut, join
            halves = jnp.split(grad, 2, axis=join)
            grad = None
        if grad is not None:
            pieces = [lax.index_in_dim(grad, i, join_at, keepdims=False) for i in range(2)]
        else:
            pieces = halves
        sent = [swap(take(p, (1 - core) * part, part, cut), "core") for p in pieces]
        kept = [
            (take(p, core * part, part, cut).astype(F32) + s.astype(F32))
            for p, s in zip(pieces, sent)
        ]
        arrived = swap(kept[1].astype(BF16), "row")
        total = sum_y((kept[0] + arrived.astype(F32)).astype(BF16))
        rest = swap(total, "core")
        first = jnp.where(core == 0, total, rest)
        second = jnp.where(core == 0, rest, total)
        return jnp.concatenate([first, second], axis=cut).astype(F32)

    down = (((0,), (0,)), ((), ()))
    down_grad = lax.dot_general(hidden, grad_rows, down, preferred_element_type=F32).astype(BF16)
    down_grad = reduce_weight(down_grad, 0, 1)
    gate_grad = jnp.stack(
        [
            lax.dot_general(tokens_b, gate_up_grad[i], down, preferred_element_type=F32).astype(BF16)
            for i in range(2)
        ]
    )
    gate_grad = reduce_weight(gate_grad, 1, 1)
    out_grad = lax.dot_general(attended, g2_rows, down, preferred_element_type=F32).astype(BF16)
    out_grad = reduce_weight(out_grad, 0, 1)
    in_grad = jnp.stack(
        [
            lax.dot_general(tokens_a, mixed[i], down, preferred_element_type=F32).astype(BF16)
            for i in range(3)
        ]
    )
    in_grad = reduce_weight(in_grad, 1, 1)

    bias_sum = bias_part[:, 0, :]
    bias_sum = bias_sum + swap(bias_sum, "row")
    bias_sum = lax.psum(bias_sum, "y") if y_count != 2 else bias_sum + swap(bias_sum, "y")
    bias_other = swap(bias_sum, "core")
    bias_grad = jnp.concatenate(
        [jnp.where(core == 0, bias_sum, bias_other), jnp.where(core == 0, bias_other, bias_sum)],
        axis=1,
    )

    def reduce_vector(sums):
        total = sums[:, :wide] + swap(sums[:, wide:], "row")
        total = total + swap(total, "core")
        total = lax.psum(total, "y") if y_count != 2 else total + swap(total, "y")
        if slots != 4:
            return lax.psum(total, "col")
        pair = total + lax.ppermute(total, "col", PAIR)
        inner = pair + lax.ppermute(pair, "col", MID)
        outer = lax.ppermute(inner, "col", OUT)
        return jnp.where((place == 0) | (place == 3), outer, inner)

    vec_b = reduce_vector(sums_b)
    vec_a = reduce_vector(sums_a)
    return (
        layer_out[None],
        input_grad,
        vec_a[0:1],
        vec_a[1:2],
        jnp.transpose(in_grad, (1, 0, 2))[None],
        bias_grad[None],
        out_grad[None],
        vec_b[0:1],
        vec_b[1:2],
        jnp.transpose(gate_grad, (1, 0, 2))[None],
        down_grad[None],
    )


def solution(mesh):
    dp, rows, cols = (mesh.shape[a] for a in ("dp", "row", "col"))
    split = Mesh(mesh.devices.reshape(dp // 2, 2, rows, cols), ("y", "core", "row", "col"))
    tokens = ("y", "core", "col")
    return jax.shard_map(
        local,
        mesh=split,
        in_specs=(
            P(tokens, "row"),
            P(None, "row"),
            P(None, "row"),
            P(None, "row", None, "col"),
            P(None, None, "col"),
            P(None, "col", "row"),
            P(None, "row"),
            P(None, "row"),
            P(None, "row", None, "col"),
            P(None, "col", "row"),
            P(tokens, "row"),
        ),
        out_specs=(
            P(None, tokens, "row"),
            P(tokens, "row"),
            P(None, "row"),
            P(None, "row"),
            P(None, "row", None, "col"),
            P(None, None, "col"),
            P(None, "col", "row"),
            P(None, "row"),
            P(None, "row"),
            P(None, "row", None, "col"),
            P(None, "col", "row"),
        ),
        check_vma=False,
    )
```

time: 1490 us -> 871 us (0.58)
  waiting for transfers between devices: 1100 us -> 290 us
  local copies, waits for them, and re-layouts: 66.9 us -> 215 us
  starting transfers between devices: 9.73 us -> 133 us
  blocking collectives: 88.4 us -> 0 us
  matrix products: 127 us -> 40.2 us
  Pallas kernels: 0 us -> 74.9 us
  other arithmetic: 67.5 us -> 105 us
    reduce_scatter x8 -> x0, waiting for transfers between devices: 571 us -> none  [the longest x2 211 us: split_units(): return lax.psum_scatter(partial_sum, 'row', scatter_dimension=2, tiled=True)]
    all_gather x8 -> x0, waiting for transfers between devices: 323 us -> none  [the longest x2 98 us: join_unit_grads(): return lax.all_gather(local_units, 'row', axis=2, tiled=True)]
    ppermute x0 -> x104, waiting for transfers between devices: none -> 290 us  [the longest x50 180 us: swap(): return lax.ppermute(x, axis, [(0, 1), (1, 0)])]
    psum x1 -> x0, waiting for transfers between devices: 209 us -> none  [local(): lax.psum(stack_gate.astype(jnp.bfloat16), 'dp').astype(jnp.float32)]
    ppermute x0 -> x104, starting transfers between devices: none -> 133 us  [the longest x50 33.9 us: swap(): return lax.ppermute(x, axis, [(0, 1), (1, 0)])]
    another operation x3 -> x7, local copies, waits for them, and re-layouts: 6.12 us -> 125 us  [the longest x2 122 us: local(): jnp.stack([lax.dot_general(tokens_b, gate_up_grad[i], down, preferred_ele...]
    psum x6 -> x0, blocking collectives: 88.4 us -> none  [the longest x1 59.9 us: local(): lax.psum((jnp.stack(gain_a_grads), jnp.stack(shift_a_grads), jnp.stack(ga...]
    dot_general x26 -> x14, matrix products: 127 us -> 40.2 us  [the longest x2 9.93 us: local(): lax.dot_general(tokens_b, gate_up_grad[i], down, preferred_element_type=F32)]
  transfers between devices with their start and end apart: 17 -> 104, of which waited for: 17 -> 33; matrix products, arithmetic and copies ran while one was open for 7% -> 39% of each run, Pallas kernels for 0% -> 5%
where the time goes in v1:
time: 871 us; the launch traced here: 861 us
  waiting for transfers between devices  290 us (33%)
  local copies, waits for them, and re-layouts  215 us (25%)
  starting transfers between devices  133 us (15%)
  other arithmetic  105 us (12%)
  Pallas kernels  74.9 us (9%)
  matrix products  40.2 us (5%)
    ppermute x50, waiting for transfers between devices, swap(): return lax.ppermute(x, axis, [(0, 1), (1, 0)])  180 us
    another operation x2, local copies, waits for them, and re-layouts, local(): jnp.stack([lax.dot_general(tokens_b, gate_up_grad[i], down, preferred_ele...  122 us
    pallas_call x1, Pallas kernels, mlp(): pl.pallas_call(body, grid=(steps,), in_specs=[pl.BlockSpec((rows, width),...  34.3 us
    ppermute x50, starting transfers between devices, swap(): return lax.ppermute(x, axis, [(0, 1), (1, 0)])  33.9 us
    ppermute x4, waiting for transfers between devices, gather_slots(): two = mid + lax.ppermute(mid, 'col', OUT)  24.3 us
    ppermute x4, waiting for transfers between devices, gather_slots(): three = far + lax.ppermute(far, 'col', OUT)  22.4 us
    dynamic_update_slice x16, local copies, waits for them, and re-layouts, assemble(): full = lax.dynamic_update_slice(full, piece, at)  22.3 us
    pad x4, local copies, waits for them, and re-layouts, assemble(): full = lax.pad(w, jnp.zeros((), w.dtype), pads)  20.8 us
  transfers between devices with their start and end apart: 104, of which 33 were waited for; matrix products, arithmetic and copies ran while one was open for 39% of the time, Pallas kernels for 5%

profile of v1, /device:TPU:0, one launch (start us, length us, event | category | flops | bytes accessed | tf_op | source)
XLA Modules:
  0.0 861.0 jit_solution(11290814476846226649)
XLA Ops:
  22.1 8.9 %collective-permute-done.8 = bf16[3,256,512]{2,1,0:T(8,128)(2,1)S(1)} collective-permute-done((bf16[3,256,512]{2,1,0:T(8,128)(2,1)S(1)}, bf16[3,256,512]{2,1,0:T(8,128)(2,1)S(1)}, u32[]{:S(2)}, u32[]{:S(2)}) %collective-permute-start.8) | collective-permute-done | bytes 786464 | tf_op jit(solution)/shard_map/ppermute | solution.py:23
  100.2 11.1 %attend.1 = (bf16[512,256]{1,0:T(8,128)(2,1)S(1)}, bf16[512,256]{1,0:T(8,128)(2,1)S(1)}, f32[2,1024,2]{2,1,0:T(8,128)S(1)}) custom-call(s32[5]{0:T(128)S(1)} %pad_add_fusion.order_ref, bf16[3,512,256]{2,1,0:T(8,128)(2,1)S(1)} %qkv_columns.2.mine_ref, bf16[3,512,256]{2,1,0:T(8,128)(2,1)} %collective-permute-done.12.other_ref), custom_call_target="tpu_custom_call" | custom-call | flops 1073741824 | bytes 2097152 | tf_op jit(solution)/shard_map/attend/pallas_call | solution.py:285
  175.8 7.9 pad.14
  211.3 8.1 collective-permute-done.23
  235.5 11.3 %collective-permute-done.25 = bf16[128,2048]{1,0:T(8,128)(2,1)S(1)} collective-permute-done((bf16[128,2048]{1,0:T(8,128)(2,1)S(1)}, bf16[128,2048]{1,0:T(8,128)(2,1)S(1)}, u32[]{:S(2)}, u32[]{:S(2)}) %collective-permute-start.25) | collective-permute-done | bytes 524320 | tf_op jit(solution)/shard_map/ppermute | solution.py:45
  247.0 9.2 %collective-permute-done.27 = bf16[128,2048]{1,0:T(8,128)(2,1)S(1)} collective-permute-done((bf16[128,2048]{1,0:T(8,128)(2,1)S(1)}, bf16[128,2048]{1,0:T(8,128)(2,1)S(1)}, u32[]{:S(2)}, u32[]{:S(2)}) %collective-permute-start.27) | collective-permute-done | bytes 524320 | tf_op jit(solution)/shard_map/ppermute | solution.py:46
  258.7 34.3 %mlp.1 = (bf16[512,1408]{1,0:T(8,128)(2,1)S(1)}, bf16[2,512,1408]{2,1,0:T(8,128)(2,1)}, bf16[512,2048]{1,0:T(8,128)(2,1)}) custom-call(bf16[512,2048]{1,0:T(8,128)(2,1)} %pad_maximum_fusion.2.x_ref, bf16[2,2048,1408]{2,1,0:T(8,128)(2,1)} %constant_dynamic-update-slice_fusion.w_ref, bf16[512,1408]{1,0:T(8,128)(2,1)} %convolution_convert_fusion.7.hg_ref), custom_call_target="tpu_custom_call" | custom-call | flops 11811160064 | bytes 15728640 | tf_op jit(solution)/shard_map/mlp/pallas_call | solution.py:466
  308.3 111.2 %copy.39 = bf16[1,2,1024,1408]{3,0,2,1:T(2,128)(2,1)S(1)} copy(bf16[1,2,1024,1408]{3,2,1,0:T(8,128)(2,1)S(1)} %bitcast.152) | data formatting | bytes 11534336 | tf_op jit(solution)/shard_map/stack | solution.py:703
  425.6 10.5 %copy.38 = bf16[1,2,1024,1408]{3,0,2,1:T(2,128)(2,1)} copy(bf16[1,2,1024,1408]{3,2,1,0:T(8,128)(2,1)S(1)} %bitcast.151) | data formatting | bytes 11534336 | tf_op jit(solution)/shard_map/stack | solution.py:703
  436.1 14.2 %fusion = bf16[2,1,1024,1408]{3,0,2,1:T(2,128)(2,1)} fusion(bf16[1,2,1024,1408]{3,0,2,1:T(2,128)(2,1)} %copy.38, bf16[1,2,1024,1408]{3,0,2,1:T(2,128)(2,1)S(1)} %copy.39), kind=kLoop, calls=%fused_computation.8 | loop fusion | flops 11534336 | bytes 17301504 | tf_op jit(solution)/shard_map/stack | solution.py:703
  450.3 10.3 %fusion.7 = bf16[2,512,1408]{2,0,1:T(2,128)(2,1)} fusion(s32[]{:T(128)S(6)} %select_n.279, bf16[1,2,1024,1408]{3,0,2,1:T(2,128)(2,1)} %copy-done.11, bf16[1,2,1024,1408]{3,0,2,1:T(2,128)(2,1)} %copy.38), kind=kLoop, calls=%fused_computation.33 | loop fusion | flops 5767168 | bytes 14417924 | tf_op jit(solution)/shard_map/dynamic_slice | solution.py:533
  485.9 7.9 collective-permute-done.54.c_ref
  524.7 7.9 collective-permute-done.55
  541.9 9.7 %collective-permute-done.57 = bf16[128,2048]{1,0:T(8,128)(2,1)S(1)} collective-permute-done((bf16[128,2048]{1,0:T(8,128)(2,1)S(1)}, bf16[128,2048]{1,0:T(8,128)(2,1)S(1)}, u32[]{:S(2)}, u32[]{:S(2)}) %collective-permute-start.57) | collective-permute-done | bytes 524320 | tf_op jit(solution)/shard_map/ppermute | solution.py:45
  553.2 9.9 %fusion.1 = bf16[2,512,1408]{2,0,1:T(2,128)(2,1)} fusion(bf16[2,512,1408]{2,0,1:T(2,128)(2,1)} %collective-permute-done.95, s32[]{:T(128)S(6)} %select_n.278, bf16[1,2,1024,1408]{3,0,2,1:T(2,128)(2,1)S(1)} %bitcast.144, bf16[1,2,1024,1408]{3,0,2,1:T(2,128)(2,1)} %copy.38), kind=kLoop, calls=%fused_computation.10 | loop fusion | flops 11534336 | bytes 17301508 | tf_op jit(solution)/shard_map/convert_element_type | solution.py:693
  569.5 16.4 %attend_back.1 = (bf16[3,512,256]{2,1,0:T(8,128)(2,1)S(1)}, bf16[3,512,256]{2,1,0:T(8,128)(2,1)}, f32[3,1,256]{2,1,0:T(1,128)S(1)}) custom-call(s32[5]{0:T(128)S(1)} %pad_add_fusion.order_ref, bf16[3,512,256]{2,1,0:T(8,128)(2,1)} %copy-done.6, bf16[3,512,256]{2,1,0:T(8,128)(2,1)} %collective-permute-done.12.other_ref, ...), custom_call_target="tpu_custom_call" | custom-call | flops 2684354560 | bytes 5242880 | tf_op jit(solution)/shard_map/attend_back/pallas_call | solution.py:395
  592.5 43.8 %collective-permute-done.80 = f32[3,256]{1,0:T(4,128)S(1)} collective-permute-done((f32[3,256]{1,0:T(4,128)S(1)}, f32[3,256]{1,0:T(4,128)S(1)}, u32[]{:S(2)}, u32[]{:S(2)}) %collective-permute-start.80) | collective-permute-done | bytes 3104 | tf_op jit(solution)/shard_map/ppermute | solution.py:23
  646.9 12.2 %collective-permute-start.64 = (bf16[128,2048]{1,0:T(8,128)(2,1)S(1)}, bf16[128,2048]{1,0:T(8,128)(2,1)S(1)}, u32[]{:S(2)}, u32[]{:S(2)}) collective-permute-start(bf16[128,2048]{1,0:T(8,128)(2,1)S(1)} %slice.203), channel_id=1, source_target_pairs={{0,1},{3,2},{4,5},{7,6},{8,9},{11,10},{12,13},{15,14},{16,17},{19,... | collective-permute-start | bytes 1572872 | tf_op jit(solution)/shard_map/ppermute | solution.py:56
  684.4 8.7 %fusion.3 = bf16[2,512,1408]{2,0,1:T(2,128)(2,1)} fusion(bf16[2,512,1408]{2,0,1:T(2,128)(2,1)} %collective-permute-done.96, bf16[2,512,1408]{2,0,1:T(2,128)(2,1)} %collective-permute-done.94, bf16[2,1,1024,1408]{3,0,2,1:T(2,128)(2,1)S(1)} %bitcast.147, s32[]{:T(128)S(6)} %select_n.278), kind=kLoop, calls=%fused_computation.13 | loop fusion | flops 8650752 | bytes 11534340 | tf_op jit(solution)/shard_map/convert_element_type | solution.py:694
  701.1 37.9 %collective-permute-done.86 = bf16[256,1024]{1,0:T(8,128)(2,1)S(1)} collective-permute-done((bf16[256,1024]{1,0:T(8,128)(2,1)}, bf16[256,1024]{1,0:T(8,128)(2,1)S(1)}, u32[]{:S(2)}, u32[]{:S(2)}) %collective-permute-start.86) | collective-permute-done | bytes 524320 | tf_op jit(solution)/shard_map/ppermute | solution.py:23
  741.8 10.7 %collective-permute-done.66.c_ref = bf16[128,2048]{1,0:T(8,128)(2,1)S(1)} collective-permute-done((bf16[128,2048]{1,0:T(8,128)(2,1)S(1)}, bf16[128,2048]{1,0:T(8,128)(2,1)S(1)}, u32[]{:S(2)}, u32[]{:S(2)}) %collective-permute-start.66) | collective-permute-done | bytes 524320 | tf_op jit(solution)/shard_map/ppermute | solution.py:60
  756.3 16.6 %collective-permute-done.69 = f32[2,1024]{1,0:T(2,128)S(1)} collective-permute-done((f32[2,1024]{1,0:T(2,128)S(1)}, f32[2,1024]{1,0:T(2,128)S(1)}, u32[]{:S(2)}, u32[]{:S(2)}) %collective-permute-start.69) | collective-permute-done | bytes 8224 | tf_op jit(solution)/shard_map/ppermute | solution.py:23
  780.5 20.5 %collective-permute-done.71 = f32[2,1024]{1,0:T(2,128)S(1)} collective-permute-done((f32[2,1024]{1,0:T(2,128)S(1)}, f32[2,1024]{1,0:T(2,128)S(1)}, u32[]{:S(2)}, u32[]{:S(2)}) %collective-permute-start.71) | collective-permute-done | bytes 8224 | tf_op jit(solution)/shard_map/ppermute | solution.py:23
  804.1 29.2 %collective-permute-done.78 = bf16[3,512,512]{2,1,0:T(8,128)(2,1)S(1)} collective-permute-done((bf16[3,512,512]{2,1,0:T(8,128)(2,1)S(1)}, bf16[3,512,512]{2,1,0:T(8,128)(2,1)S(1)}, u32[]{:S(2)}, u32[]{:S(2)}) %collective-permute-start.78) | collective-permute-done | bytes 1572896 | tf_op jit(solution)/shard_map/ppermute | solution.py:23
  (505 shorter events, 389.7 us)
Async XLA Ops:
  34.1 51.4 %collective-permute-start.14 = (bf16[128,1024]{1,0:T(8,128)(2,1)}, bf16[128,1024]{1,0:T(8,128)(2,1)}, u32[]{:S(2)}, u32[]{:S(2)}) collective-permute-start(bf16[128,1024]{1,0:T(8,128)(2,1)} %dynamic-slice_bitcast_fusion.5), channel_id=1, source_target_pairs={{0,4},{4,0},{1,5},{5,1},{2,6},{6,2},{3,7},{7,3},{8,12},{12,8},{9,1... | collective-permute-start | bytes 786440 | tf_op jit(solution)/shard_map/ppermute | solution.py:23
  80.4 60.6 %collective-permute-start.28 = (bf16[2,256,1408]{2,1,0:T(8,128)(2,1)}, bf16[2,256,1408]{2,1,0:T(8,128)(2,1)}, u32[]{:S(2)}, u32[]{:S(2)}) collective-permute-start(bf16[2,256,1408]{2,1,0:T(8,128)(2,1)} %bitcast.133), channel_id=1, source_target_pairs={{0,4},{4,0},{1,5},{5,1},{2,6},{6,2},{3,7},{7,3},{8,12},{12,8},{9,1... | collective-permute-start | bytes 4325384 | tf_op jit(solution)/shard_map/ppermute | solution.py:23
  142.4 66.9 %collective-permute-start.29 = (bf16[2,256,1408]{2,1,0:T(8,128)(2,1)}, bf16[2,256,1408]{2,1,0:T(8,128)(2,1)}, u32[]{:S(2)}, u32[]{:S(2)}) collective-permute-start(bf16[2,256,1408]{2,1,0:T(8,128)(2,1)} %collective-permute-done.28), channel_id=1, source_target_pairs={{0,16},{16,0},{1,17},{17,1},{2,18},{18,2},{3,19},{19,3},{4,20},{20... | collective-permute-start | bytes 4325384 | tf_op jit(solution)/shard_map/ppermute | solution.py:23
  152.1 40.2 %collective-permute-start.19 = (bf16[128,2048]{1,0:T(8,128)(2,1)}, bf16[128,2048]{1,0:T(8,128)(2,1)S(1)}, u32[]{:S(2)}, u32[]{:S(2)}) collective-permute-start(bf16[128,2048]{1,0:T(8,128)(2,1)} %get-tuple-element.92), channel_id=1, source_target_pairs={{1,2},{2,1},{5,6},{6,5},{9,10},{10,9},{13,14},{14,13},{17,18},{18,... | collective-permute-start | bytes 1572872 | tf_op jit(solution)/shard_map/ppermute | solution.py:59
  167.3 42.0 %collective-permute-start.42 = (bf16[352,1024]{1,0:T(8,128)(2,1)}, bf16[352,1024]{1,0:T(8,128)(2,1)}, u32[]{:S(2)}, u32[]{:S(2)}) collective-permute-start(bf16[352,1024]{1,0:T(8,128)(2,1)} %collective-permute-done.40), channel_id=1, source_target_pairs={{0,8},{8,0},{1,9},{9,1},{2,10},{10,2},{3,11},{11,3},{4,12},{12,4},... | collective-permute-start | bytes 2162696 | tf_op jit(solution)/shard_map/ppermute | solution.py:23
  297.8 170.8 %collective-permute-start.43 = (bf16[128,2048]{1,0:T(8,128)(2,1)}, bf16[128,2048]{1,0:T(8,128)(2,1)}, u32[]{:S(2)}, u32[]{:S(2)}) collective-permute-start(bf16[128,2048]{1,0:T(8,128)(2,1)} %get-tuple-element.89), channel_id=1, source_target_pairs={{0,1},{3,2},{4,5},{7,6},{8,9},{11,10},{12,13},{15,14},{16,17},{19,... | collective-permute-start | bytes 1572872 | tf_op jit(solution)/shard_map/ppermute | solution.py:57
  300.3 168.4 %collective-permute-start.45 = (bf16[128,2048]{1,0:T(8,128)(2,1)}, bf16[128,2048]{1,0:T(8,128)(2,1)}, u32[]{:S(2)}, u32[]{:S(2)}) collective-permute-start(bf16[128,2048]{1,0:T(8,128)(2,1)} %get-tuple-element.90), channel_id=1, source_target_pairs={{0,1},{3,2},{4,5},{7,6},{8,9},{11,10},{12,13},{15,14},{16,17},{19,... | collective-permute-start | bytes 1572872 | tf_op jit(solution)/shard_map/ppermute | solution.py:56
  302.4 158.2 %collective-permute-start.52 = (bf16[128,2048]{1,0:T(8,128)(2,1)S(1)}, bf16[128,2048]{1,0:T(8,128)(2,1)}, u32[]{:S(2)}, u32[]{:S(2)}) collective-permute-start(bf16[128,2048]{1,0:T(8,128)(2,1)S(1)} %slice.152), channel_id=1, source_target_pairs={{0,1},{3,2},{4,5},{7,6},{8,9},{11,10},{12,13},{15,14},{16,17},{19,... | collective-permute-start | bytes 1572872 | tf_op jit(solution)/shard_map/ppermute | solution.py:56
  460.7 92.5 %collective-permute-start.95 = (bf16[2,512,1408]{2,0,1:T(2,128)(2,1)}, bf16[2,512,1408]{2,0,1:T(2,128)(2,1)}, u32[]{:S(2)}, u32[]{:S(2)}) collective-permute-start(bf16[2,512,1408]{2,0,1:T(2,128)(2,1)} %fusion.7), channel_id=1, source_target_pairs={{0,8},{8,0},{1,9},{9,1},{2,10},{10,2},{3,11},{11,3},{4,12},{12,4},... | collective-permute-start | bytes 8650760 | tf_op jit(solution)/shard_map/ppermute | solution.py:23
  515.2 164.7 %collective-permute-start.94 = (bf16[2,512,1408]{2,0,1:T(2,128)(2,1)}, bf16[2,512,1408]{2,0,1:T(2,128)(2,1)}, u32[]{:S(2)}, u32[]{:S(2)}) collective-permute-start(bf16[2,512,1408]{2,0,1:T(2,128)(2,1)} %dynamic-slice_bitcast_fusion), channel_id=1, source_target_pairs={{0,8},{8,0},{1,9},{9,1},{2,10},{10,2},{3,11},{11,3},{4,12},{12,4},... | collective-permute-start | bytes 8650760 | tf_op jit(solution)/shard_map/ppermute | solution.py:23
  539.3 46.6 %collective-permute-start.99 = (bf16[704,1024]{1,0:T(8,128)(2,1)}, bf16[704,1024]{1,0:T(8,128)(2,1)}, u32[]{:S(2)}, u32[]{:S(2)}) collective-permute-start(bf16[704,1024]{1,0:T(8,128)(2,1)} %constant_dynamic-slice_fusion.1), channel_id=1, source_target_pairs={{0,8},{8,0},{1,9},{9,1},{2,10},{10,2},{3,11},{11,3},{4,12},{12,4},... | collective-permute-start | bytes 4325384 | tf_op jit(solution)/shard_map/ppermute | solution.py:23
  539.9 46.3 %collective-permute-start.101 = (bf16[704,1024]{1,0:T(8,128)(2,1)}, bf16[704,1024]{1,0:T(8,128)(2,1)}, u32[]{:S(2)}, u32[]{:S(2)}) collective-permute-start(bf16[704,1024]{1,0:T(8,128)(2,1)} %add_convert_fusion.5), channel_id=1, source_target_pairs={{0,4},{4,0},{1,5},{5,1},{2,6},{6,2},{3,7},{7,3},{8,12},{12,8},{9,1... | collective-permute-start | bytes 4325384 | tf_op jit(solution)/shard_map/ppermute | solution.py:23
  563.1 118.4 %collective-permute-start.96 = (bf16[2,512,1408]{2,0,1:T(2,128)(2,1)}, bf16[2,512,1408]{2,0,1:T(2,128)(2,1)}, u32[]{:S(2)}, u32[]{:S(2)}) collective-permute-start(bf16[2,512,1408]{2,0,1:T(2,128)(2,1)} %fusion.1), channel_id=1, source_target_pairs={{0,4},{4,0},{1,5},{5,1},{2,6},{6,2},{3,7},{7,3},{8,12},{12,8},{9,1... | collective-permute-start | bytes 8650760 | tf_op jit(solution)/shard_map/ppermute | solution.py:23
  569.0 71.0 %collective-permute-start.84 = (bf16[256,1024]{1,0:T(8,128)(2,1)S(1)}, bf16[256,1024]{1,0:T(8,128)(2,1)S(1)}, u32[]{:S(2)}, u32[]{:S(2)}) collective-permute-start(bf16[256,1024]{1,0:T(8,128)(2,1)S(1)} %constant_dynamic-slice_fusion.2), channel_id=1, source_target_pairs={{0,8},{8,0},{1,9},{9,1},{2,10},{10,2},{3,11},{11,3},{4,12},{12,4},... | collective-permute-start | bytes 1572872 | tf_op jit(solution)/shard_map/ppermute | solution.py:23
  585.9 56.8 %collective-permute-start.61 = (bf16[3,512,256]{2,1,0:T(8,128)(2,1)}, bf16[3,512,256]{2,1,0:T(8,128)(2,1)S(1)}, u32[]{:S(2)}, u32[]{:S(2)}) collective-permute-start(bf16[3,512,256]{2,1,0:T(8,128)(2,1)} %get-tuple-element.36), channel_id=1, source_target_pairs={{0,8},{8,0},{1,9},{9,1},{2,10},{10,2},{3,11},{11,3},{4,12},{12,4},... | collective-permute-start | bytes 2359304 | tf_op jit(solution)/shard_map/ppermute | solution.py:23
  586.2 50.1 %collective-permute-start.80 = (f32[3,256]{1,0:T(4,128)S(1)}, f32[3,256]{1,0:T(4,128)S(1)}, u32[]{:S(2)}, u32[]{:S(2)}) collective-permute-start(f32[3,256]{1,0:T(4,128)S(1)} %bitcast.166), channel_id=1, source_target_pairs={{0,4},{4,0},{1,5},{5,1},{2,6},{6,2},{3,7},{7,3},{8,12},{12,8},{9,1... | collective-permute-start | bytes 9224 | tf_op jit(solution)/shard_map/ppermute | solution.py:23
  693.1 61.1 %collective-permute-start.102 = (bf16[704,1024]{1,0:T(8,128)(2,1)}, bf16[704,1024]{1,0:T(8,128)(2,1)S(1)}, u32[]{:S(2)}, u32[]{:S(2)}) collective-permute-start(bf16[704,1024]{1,0:T(8,128)(2,1)} %add_convert_fusion.4), channel_id=1, source_target_pairs={{0,16},{16,0},{1,17},{17,1},{2,18},{18,2},{3,19},{19,3},{4,20},{20... | collective-permute-start | bytes 4325384 | tf_op jit(solution)/shard_map/ppermute | solution.py:23
  694.1 45.0 %collective-permute-start.86 = (bf16[256,1024]{1,0:T(8,128)(2,1)}, bf16[256,1024]{1,0:T(8,128)(2,1)S(1)}, u32[]{:S(2)}, u32[]{:S(2)}) collective-permute-start(bf16[256,1024]{1,0:T(8,128)(2,1)} %add_convert_fusion.7), channel_id=1, source_target_pairs={{0,16},{16,0},{1,17},{17,1},{2,18},{18,2},{3,19},{19,3},{4,20},{20... | collective-permute-start | bytes 1572872 | tf_op jit(solution)/shard_map/ppermute | solution.py:23
  695.1 105.9 %collective-permute-start.97 = (bf16[2,512,1408]{2,0,1:T(2,128)(2,1)}, bf16[2,512,1408]{2,0,1:T(2,128)(2,1)S(1)}, u32[]{:S(2)}, u32[]{:S(2)}) collective-permute-start(bf16[2,512,1408]{2,0,1:T(2,128)(2,1)} %fusion.3), channel_id=1, source_target_pairs={{0,16},{16,0},{1,17},{17,1},{2,18},{18,2},{3,19},{19,3},{4,20},{20... | collective-permute-start | bytes 8650760 | tf_op jit(solution)/shard_map/ppermute | solution.py:23
  697.6 43.4 %collective-permute-start.63 = (bf16[128,2048]{1,0:T(8,128)(2,1)S(1)}, bf16[128,2048]{1,0:T(8,128)(2,1)S(1)}, u32[]{:S(2)}, u32[]{:S(2)}) collective-permute-start(bf16[128,2048]{1,0:T(8,128)(2,1)S(1)} %get-tuple-element.78), channel_id=1, source_target_pairs={{1,2},{2,1},{5,6},{6,5},{9,10},{10,9},{13,14},{14,13},{17,18},{18,... | collective-permute-start | bytes 1572872 | tf_op jit(solution)/shard_map/ppermute | solution.py:59
  700.6 76.5 %collective-permute-start.75 = (bf16[3,512,512]{2,1,0:T(8,128)(2,1)S(1)}, bf16[3,512,512]{2,1,0:T(8,128)(2,1)S(1)}, u32[]{:S(2)}, u32[]{:S(2)}) collective-permute-start(bf16[3,512,512]{2,1,0:T(8,128)(2,1)S(1)} %copy-done.42), channel_id=1, source_target_pairs={{0,8},{8,0},{1,9},{9,1},{2,10},{10,2},{3,11},{11,3},{4,12},{12,4},... | collective-permute-start | bytes 4718600 | tf_op jit(solution)/shard_map/ppermute | solution.py:23
  772.9 61.1 %collective-permute-start.103 = (bf16[704,1024]{1,0:T(8,128)(2,1)S(1)}, bf16[704,1024]{1,0:T(8,128)(2,1)S(1)}, u32[]{:S(2)}, u32[]{:S(2)}) collective-permute-start(bf16[704,1024]{1,0:T(8,128)(2,1)S(1)} %add_convert_fusion.3), channel_id=1, source_target_pairs={{0,8},{8,0},{1,9},{9,1},{2,10},{10,2},{3,11},{11,3},{4,12},{12,4},... | collective-permute-start | bytes 4325384 | tf_op jit(solution)/shard_map/ppermute | solution.py:23
  777.8 55.5 %collective-permute-start.78 = (bf16[3,512,512]{2,1,0:T(8,128)(2,1)S(1)}, bf16[3,512,512]{2,1,0:T(8,128)(2,1)S(1)}, u32[]{:S(2)}, u32[]{:S(2)}) collective-permute-start(bf16[3,512,512]{2,1,0:T(8,128)(2,1)S(1)} %fusion.6), channel_id=1, source_target_pairs={{0,16},{16,0},{1,17},{17,1},{2,18},{18,2},{3,19},{19,3},{4,20},{20... | collective-permute-start | bytes 4718600 | tf_op jit(solution)/shard_map/ppermute | solution.py:23
  804.0 48.9 %collective-permute-start.98 = (bf16[2,512,1408]{2,0,1:T(2,128)(2,1)S(1)}, bf16[2,512,1408]{2,0,1:T(2,128)(2,1)S(1)}, u32[]{:S(2)}, u32[]{:S(2)}) collective-permute-start(bf16[2,512,1408]{2,0,1:T(2,128)(2,1)S(1)} %add_convert_fusion), channel_id=1, source_target_pairs={{0,8},{8,0},{1,9},{9,1},{2,10},{10,2},{3,11},{11,3},{4,12},{12,4},... | collective-permute-start | bytes 8650760 | tf_op jit(solution)/shard_map/ppermute | solution.py:23
  (157 other events, 2898.8 us)

commit v2 on v1

--- a/solution.py
+++ b/solution.py
@@ -180,6 +180,11 @@
     )(stream, *terms, upper, gain)
 
 
+def cuts_of(sizes):
+    ends = [sum(sizes[: i + 1]) for i in range(len(sizes))]
+    return [(end - size, end) for end, size in zip(ends, sizes)]
+
+
 def roll_lanes(value, shift):
     return pltpu.roll(value, shift % value.shape[1], 1)
 
@@ -193,13 +198,17 @@
     return value * wide[0] + (moved if sign > 0 else -moved)
 
 
-def qkv_columns(tokens, weight, bias, table, half):
+def qkv_columns(tokens, pieces, bias, table, half):
     rows, width = tokens.shape
-    columns = weight.shape[2] // 2
-
-    def body(half_ref, x_ref, w_ref, bias_ref, table_ref, out_ref):
+    columns = pieces[0].shape[2] // 2
+    cuts = cuts_of([p.shape[1] for p in pieces])
+
+    def body(half_ref, x_ref, *refs):
+        bias_ref, table_ref, out_ref = refs[-3:]
         which = pl.program_id(0)
-        acc = jnp.dot(x_ref[...], w_ref[0], preferred_element_type=F32) + bias_ref[0]
+        acc = bias_ref[0]
+        for w_ref, (low, high) in zip(refs, cuts):
+            acc = acc + jnp.dot(x_ref[:, low:high], w_ref[0], preferred_element_type=F32)
 
         @pl.when(which < 2)
         def _():
@@ -214,9 +223,9 @@
         grid_spec=pltpu.PrefetchScalarGridSpec(
             num_scalar_prefetch=1,
             grid=(3,),
-            in_specs=[
-                pl.BlockSpec((rows, width), lambda j, h: (0, 0)),
-                pl.BlockSpec((1, width, columns), lambda j, h: (j, 0, h[0])),
+            in_specs=[pl.BlockSpec((rows, width), lambda j, h: (0, 0))]
+            + [pl.BlockSpec((1, p.shape[1], columns), lambda j, h: (j, 0, h[0])) for p in pieces]
+            + [
                 pl.BlockSpec((1, 1, columns), lambda j, h: (j, 0, h[0])),
                 pl.BlockSpec((3, rows, LANES), lambda j, h: (0, 0, 0)),
             ],
@@ -226,7 +235,7 @@
         compiler_params=params(40),
         cost_estimate=cost(6 * rows * width * columns, 2 * (rows * width + 3 * columns * width)),
         name="qkv_columns",
-    )(half, tokens, weight, bias, table)
+    )(half, tokens, *pieces, bias, table)
 
 
 def place_of(order_ref, slot, core, rows):
@@ -427,82 +436,182 @@
     )(order, mine, other, grad_mine, grad_other, lse, table_mine, table_other)
 
 
-def mlp(tokens, weight, hidden_grad):
+ACROSS = (((1,), (1,)), ((), ()))
+DOWN = (((0,), (0,)), ((), ()))
+
+
+def feed_forward(tokens, pieces, hidden_grad):
     rows, width = tokens.shape
-    units = weight.shape[2]
+    units = pieces[0].shape[2]
     block = LANES if units % LANES == 0 else units
-    steps = units // block
-    across = (((1,), (1,)), ((), ()))
-
-    def body(x_ref, w_ref, hg_ref, hidden_ref, grad_ref, out_ref, acc):
-        both = jnp.concatenate([w_ref[0], w_ref[1]], axis=1)
-        gate_up = jnp.dot(x_ref[...], both, preferred_element_type=F32)
+    cuts = cuts_of([p.shape[1] for p in pieces])
+
+    def body(x_ref, *refs):
+        hg_ref, hidden_ref, grad_ref = refs[-3:]
+        gate_up = 0.0
+        for w_ref, (low, high) in zip(refs, cuts):
+            both = jnp.concatenate([w_ref[0], w_ref[1]], axis=1)
+            gate_up += jnp.dot(x_ref[:, low:high], both, preferred_element_type=F32)
         gate, up = gate_up[:, :block], gate_up[:, block:]
         sigma = jax.nn.sigmoid(gate)
         silu = gate * sigma
         hidden_ref[...] = (silu * up).astype(BF16)
         grad = hg_ref[...].astype(F32)
-        gate_grad = (grad * up * sigma * (1.0 + gate * (1.0 - sigma))).astype(BF16)
-        up_grad = (grad * silu).astype(BF16)
-        grad_ref[0] = gate_grad
-        grad_ref[1] = up_grad
-        part = lax.dot_general(
-            jnp.concatenate([gate_grad, up_grad], axis=1), both, across, preferred_element_type=F32
-        )
-        step = pl.program_id(0)
-
-        @pl.when(step == 0)
-        def _():
-            acc[...] = part
-
-        @pl.when(step > 0)
-        def _():
-            acc[...] += part
-
-        @pl.when(step == steps - 1)
-        def _():
-            out_ref[...] = acc[...].astype(BF16)
+        grad_ref[0] = (grad * up * sigma * (1.0 + gate * (1.0 - sigma))).astype(BF16)
+        grad_ref[1] = (grad * silu).astype(BF16)
 
     return pl.pallas_call(
         body,
-        grid=(steps,),
-        in_specs=[
-            pl.BlockSpec((rows, width), lambda j: (0, 0)),
-            pl.BlockSpec((2, width, block), lambda j: (0, 0, j)),
-            pl.BlockSpec((rows, block), lambda j: (0, j)),
-        ],
+        grid=(units // block,),
+        in_specs=[pl.BlockSpec((rows, width), lambda j: (0, 0))]
+        + [pl.BlockSpec((2, p.shape[1], block), lambda j: (0, 0, j)) for p in pieces]
+        + [pl.BlockSpec((rows, block), lambda j: (0, j))],
         out_specs=[
             pl.BlockSpec((rows, block), lambda j: (0, j)),
             pl.BlockSpec((2, rows, block), lambda j: (0, 0, j)),
-            pl.BlockSpec((rows, width), lambda j: (0, 0)),
         ],
         out_shape=[
             jax.ShapeDtypeStruct((rows, units), BF16),
             jax.ShapeDtypeStruct((2, rows, units), BF16),
-            jax.ShapeDtypeStruct((rows, width), BF16),
         ],
-        scratch_shapes=[pltpu.VMEM((rows, width), F32)],
-        compiler_params=params(52),
+        compiler_params=params(48),
         cost_estimate=cost(
-            8 * rows * width * units, 4 * width * units + 4 * rows * width, rows * units
-        ),
-        name="mlp",
-    )(tokens, weight, hidden_grad)
+            4 * rows * width * units, 4 * width * units + 2 * rows * width, rows * units
+        ),
+        name="feed_forward",
+    )(tokens, *pieces, hidden_grad)
+
+
+def to_features(values, pieces, across):
+    count, rows, units = values.shape
+    axis = 1 if across else 2
+    sizes = [p.shape[axis] for p in pieces]
+    block = sizes[-1]
+    width = sum(sizes)
+    owner = [i for i, size in enumerate(sizes) for _ in range(size // block)]
+    starts = [owner.index(i) for i in range(len(pieces))]
+    dims = ACROSS if across else (((1,), (0,)), ((), ()))
+
+    def body(v_ref, *refs):
+        step = pl.program_id(0)
+        for i, w_ref in enumerate(refs[:-1]):
+
+            @pl.when((step >= starts[i]) & (step < starts[i] + sizes[i] // block))
+            def _():
+                total = 0.0
+                for n in range(count):
+                    total += lax.dot_general(v_ref[n], w_ref[n], dims, preferred_element_type=F32)
+                refs[-1][...] = total.astype(BF16)
+
+    def spec(i):
+        last = sizes[i] // block - 1
+        at = lambda j: jnp.clip(j - starts[i], 0, last)
+        if across:
+            return pl.BlockSpec((count, block, units), lambda j: (0, at(j), 0))
+        return pl.BlockSpec((count, units, block), lambda j: (0, 0, at(j)))
+
+    return pl.pallas_call(
+        body,
+        grid=(width // block,),
+        in_specs=[pl.BlockSpec((count, rows, units), lambda j: (0, 0, 0))]
+        + [spec(i) for i in range(len(pieces))],
+        out_specs=pl.BlockSpec((rows, block), lambda j: (0, j)),
+        out_shape=jax.ShapeDtypeStruct((rows, width), BF16),
+        compiler_params=params(56),
+        cost_estimate=cost(
+            2 * count * rows * width * units, 2 * count * (width + rows) * units + 2 * rows * width
+        ),
+        name="to_features",
+    )(values, *pieces)
+
+
+def from_features(index, tokens, pieces, block):
+    rows, width = tokens.shape
+    cuts = cuts_of([p.shape[1] for p in pieces])
+    count = index.shape[0]
+
+    def body(index_ref, x_ref, *refs):
+        total = 0.0
+        for w_ref, (low, high) in zip(refs, cuts):
+            total += lax.dot_general(
+                x_ref[:, low:high], w_ref[...], ACROSS, preferred_element_type=F32
+            )
+        refs[-1][0] = total.astype(BF16)
+
+    out = pl.pallas_call(
+        body,
+        grid_spec=pltpu.PrefetchScalarGridSpec(
+            num_scalar_prefetch=1,
+            grid=(count,),
+            in_specs=[pl.BlockSpec((rows, width), lambda j, q: (0, 0))]
+            + [pl.BlockSpec((block, p.shape[1]), lambda j, q: (q[j], 0)) for p in pieces],
+            out_specs=pl.BlockSpec((1, rows, block), lambda j, q: (j, 0, 0)),
+        ),
+        out_shape=jax.ShapeDtypeStruct((count, rows, block), BF16),
+        compiler_params=params(40),
+        cost_estimate=cost(
+            2 * rows * width * block * count, 2 * width * (rows + block * count)
+        ),
+        name="from_features",
+    )(index, tokens, *pieces)
+    return out
+
+
+def grad_quarters(quarters, tokens, others, adds, rows_first):
+    rows, width = tokens.shape
+    count, unused, units = others.shape
+    quarter = width // 4
+    k = quarters.shape[0]
+    form = (quarter, units) if rows_first else (units, quarter)
+
+    def body(q_ref, x_ref, y_ref, *refs):
+        x, y = x_ref[...], y_ref[0]
+        left, right = (x, y) if rows_first else (y, x)
+        total = lax.dot_general(left, right, DOWN, preferred_element_type=F32)
+        for ref in refs[:-1]:
+            total += ref[0, 0].astype(F32)
+        refs[-1][0, 0] = total.astype(BF16)
+
+    def shifted(start):
+        return pl.BlockSpec((1, 1, *form), lambda i, j, q: (i + start, j, 0, 0))
+
+    return pl.pallas_call(
+        body,
+        grid_spec=pltpu.PrefetchScalarGridSpec(
+            num_scalar_prefetch=1,
+            grid=(k, count),
+            in_specs=[
+                pl.BlockSpec((rows, quarter), lambda i, j, q: (0, q[i])),
+                pl.BlockSpec((1, rows, units), lambda i, j, q: (j, 0, 0)),
+            ]
+            + [shifted(start) for unused, start in adds],
+            out_specs=shifted(0),
+        ),
+        out_shape=jax.ShapeDtypeStruct((k, count, *form), BF16),
+        compiler_params=params(48, 2),
+        cost_estimate=cost(
+            2 * k * count * rows * quarter * units,
+            2 * k * count * quarter * units * (1 + len(adds)) + 2 * rows * (width + count * units),
+        ),
+        name="grad_quarters",
+    )(quarters, tokens, others, *[array for array, unused in adds])
 
 
 def rotary_table(position):
     half = ROT // 2
-    frequency = 10000.0 ** (-(jnp.arange(half).astype(F32) * 2.0 / ROT))
+    lane = jnp.arange(LANES) % HEAD_DIM
+    frequency = 10000.0 ** (-((lane % half).astype(F32) * 2.0 / ROT))
     angles = position.astype(F32)[:, None] * frequency[None, :]
-    cosine, sine = jnp.cos(angles), jnp.sin(angles)
-    rest = HEAD_DIM - ROT
-    count = position.shape[0]
-    zero = jnp.zeros((count, half), F32)
-    tail = jnp.zeros((count, rest), F32)
-    keep = jnp.concatenate([cosine, cosine, tail + 1.0], axis=1)
-    front = jnp.concatenate([-sine, zero, tail], axis=1)
-    back = jnp.concatenate([zero, sine, tail], axis=1)
-    return jnp.stack([jnp.concatenate([t, t], axis=1) for t in (keep, front, back)])
+    lane = lane[None, :]
+    cosine = jnp.where(lane < ROT, jnp.cos(angles), 1.0)
+    sine = jnp.sin(angles)
+    return jnp.stack(
+        [
+            cosine,
+            jnp.where(lane < half, -sine, 0.0),
+            jnp.where((lane >= half) & (lane < ROT), sine, 0.0),
+        ]
+    )
 
 
 def local(
@@ -536,13 +645,25 @@
     crossed = [(0, 2), (1, 0), (2, 3), (3, 1)]
     aligned = core == row
 
+    def order_features(own, oth):
+        low, high = oth[..., : wide // 2], oth[..., wide // 2 :]
+        return jnp.concatenate(
+            [own, jnp.where(core == 0, low, high), jnp.where(core == 0, high, low)], axis=-1
+        )
+
+    def natural(oth):
+        low, high = oth[..., : wide // 2], oth[..., wide // 2 :]
+        return jnp.concatenate(
+            [jnp.where(core == 0, low, high), jnp.where(core == 0, high, low)], axis=-1
+        )
+
     def to_sequence(x):
         a = lax.ppermute(take(x, row * half_rows, half_rows, 0), ("core", "row"), straight)
         b = lax.ppermute(take(x, (1 - row) * half_rows, half_rows, 0), ("core", "row"), crossed)
-        return jnp.concatenate([jnp.where(aligned, a, b), jnp.where(aligned, b, a)], axis=1)
+        return order_features(jnp.where(aligned, a, b), jnp.where(aligned, b, a))
 
     def from_sequence(x):
-        own, oth = x[:, :wide], x[:, wide:]
+        own, oth = x[:, :wide], natural(x[:, wide:])
         a = jnp.where(aligned, own, oth)
         b = jnp.where(aligned, oth, own)
         a = lax.ppermute(a, ("core", "row"), [(j, i) for i, j in straight])
@@ -551,50 +672,8 @@
         bottom = jnp.where(row == 0, b, a)
         return jnp.concatenate([top, bottom], axis=0)
 
-    stream = to_sequence(inputs)
-
-    vectors = jnp.concatenate([first_gain, first_shift, second_gain, second_shift], axis=0)
-    vectors = jnp.concatenate([vectors, swap(vectors, "row")], axis=1)
-    gain_a, shift_a, gain_b, shift_b = (vectors[i : i + 1] for i in range(4))
-
-    def fetch(w, axis):
-        size = w.shape[axis]
-        pieces = []
-        if y_count == 2:
-            part = size // 4
-            at = lambda c, yy: c * (size // 2) + yy * part
-            first = swap(take(w, at(core, y), part, axis), "row")
-            second = swap(first, "y")
-            pieces = [
-                (first, at(core, y)),
-                (second, at(core, 1 - y)),
-                (swap(first, "core"), at(1 - core, y)),
-                (swap(second, "core"), at(1 - core, 1 - y)),
-            ]
-        else:
-            part = size // 2
-            first = swap(take(w, core * part, part, axis), "row")
-            pieces = [(first, core * part), (swap(first, "core"), (1 - core) * part)]
-        return pieces
-
-    def assemble(w, pieces, cut, join):
-        pads = [(0, w.shape[i] if i == join else 0, 0) for i in range(w.ndim)]
-        full = lax.pad(w, jnp.zeros((), w.dtype), pads)
-        for piece, start in pieces:
-            at = [jnp.int32(0)] * w.ndim
-            at[join] = jnp.int32(w.shape[join])
-            at[cut] = at[cut] + start
-            full = lax.dynamic_update_slice(full, piece, at)
-        return full
-
-    w_in = jnp.transpose(project_in[0], (1, 0, 2))
-    w_in_full = assemble(w_in, fetch(w_in, 1), 1, 1)
-    w_out = project_out[0]
-    w_out_full = assemble(w_out, fetch(w_out, 0), 0, 1)
-    w_down = down_weight[0]
-    w_down_full = assemble(w_down, fetch(w_down, 0), 0, 1)
-    w_gate = jnp.transpose(gate_weight[0], (1, 0, 2))
-    w_gate_full = assemble(w_gate, fetch(w_gate, 1), 1, 1)
+    def after(x, *others):
+        return lax.optimization_barrier((x, *others))[0]
 
     order = slot_order(place, slots)
     table_of = jnp.concatenate([core[None], order]).astype(jnp.int32)
@@ -603,43 +682,106 @@
     rotary_mine = rotary_table(position(core))
     rotary_other = rotary_table(position(1 - core))
 
-    tokens_a = gather_slots(norm_first(stream, gain_a, shift_a), slots)
+    stream = to_sequence(inputs)
+    vectors = jnp.concatenate([first_gain, first_shift, second_gain, second_shift], axis=0)
+    vectors = order_features(vectors, swap(vectors, "row"))
+    gain_a, shift_a, gain_b, shift_b = (vectors[i : i + 1] for i in range(4))
+    cot = to_sequence(cotangent)
+
+    def part_of(w, axis):
+        part = w.shape[axis] // 2
+        return take(w, core * part, part, axis)
+
+    w_in = jnp.transpose(project_in[0], (1, 0, 2))
+    w_out, w_down = project_out[0], down_weight[0]
+    w_gate = jnp.transpose(gate_weight[0], (1, 0, 2))
+    low_a = norm_first(stream, gain_a, shift_a)
+    in_half = swap(after(part_of(w_in, 1), stream, cot), "row")
+
+    tokens_a = gather_slots(low_a, slots)
+    tokens_a, in_half, w_gate = lax.optimization_barrier((tokens_a, in_half, w_gate))
+    pieces_in = (w_in, in_half, swap(in_half, "core"))
+    out_half = swap(after(part_of(w_out, 1), in_half), "row")
+    down_half = swap(after(part_of(w_down, 1), in_half), "row")
+    cot_rows = gather_slots(after(cot, tokens_a), slots)
     bias = project_bias[0][:, None, :]
-    qkv_other = qkv_columns(tokens_a, w_in_full, bias, rotary_mine, (1 - core)[None])
+    qkv_other = qkv_columns(tokens_a, pieces_in, bias, rotary_mine, (1 - core)[None])
     qkv_from = swap(qkv_other, "core")
-    qkv_mine = qkv_columns(tokens_a, w_in_full, bias, rotary_mine, core[None])
+    qkv_mine = qkv_columns(tokens_a, pieces_in, bias, rotary_mine, core[None])
+    gate_half = swap(after(part_of(w_gate, 1), qkv_mine), "row")
+    out_half = after(out_half, qkv_mine)
+    pieces_out = (w_out, out_half, swap(out_half, "core"))
     out_mine, out_other, lse = attend(qkv_mine, qkv_from, table_of, factor)
     out_from = swap(out_other, "core")
     attended = jnp.concatenate(
         [jnp.where(core == 0, out_mine, out_from), jnp.where(core == 0, out_from, out_mine)], axis=1
     )
-    part_out = jnp.dot(attended, w_out_full, preferred_element_type=F32).astype(BF16)
+    part_out = to_features(attended[None], [p[None] for p in pieces_out], False)
     terms = scatter_slots(part_out, slots)
     residual, low_b = norm_second(stream, terms, gain_b, shift_b)
 
-    cot = to_sequence(cotangent)
-    grad_rows = gather_slots(cot, slots)
-    hidden_grad = lax.dot_general(
-        grad_rows, w_down_full, (((1,), (1,)), ((), ())), preferred_element_type=F32
-    ).astype(BF16)
-
     tokens_b = gather_slots(low_b, slots)
-    hidden, gate_up_grad, part_b = mlp(tokens_b, w_gate_full, hidden_grad)
+    down_half, grad_rows = lax.optimization_barrier((down_half, cot_rows, low_b))[:2]
+    pieces_down = (w_down, down_half, swap(down_half, "core"))
+    units = w_down.shape[0]
+    ways = 2 if units % 32 == 0 else 1
+    hidden_grad = from_features(
+        jnp.arange(ways, dtype=jnp.int32), grad_rows, pieces_down, units // ways
+    )
+    hidden_grad = jnp.concatenate([hidden_grad[i] for i in range(ways)], axis=1)
+    tokens_b, gate_half, hidden_grad = lax.optimization_barrier((tokens_b, gate_half, hidden_grad))
+    pieces_gate = (w_gate, gate_half, swap(gate_half, "core"))
+    hidden, gate_up_grad = feed_forward(tokens_b, pieces_gate, hidden_grad)
+    part_b = to_features(gate_up_grad, pieces_gate, True)
     terms = scatter_slots(part_b, slots)
     g2_low, sums_b, g2 = norm_back(residual, terms, cot, gain_b, 1)
 
-    part_down = jnp.dot(hidden, w_down_full, preferred_element_type=F32).astype(BF16)
-    terms = scatter_slots(part_down, slots)
-    layer_low = (residual + sum(t.astype(F32) for t in terms)).astype(BF16)
-    layer_out = from_sequence(layer_low)
-
+    def quarters(*q):
+        return jnp.stack(q).astype(jnp.int32)
+
+    def to_core(tokens, others, rows_first):
+        sent = grad_quarters(quarters(1 - core, 3 + 0 * core), tokens, others, (), rows_first)
+        return swap(sent, "core")
+
+    def to_row(tokens, others, rows_first, got):
+        oth = grad_quarters(quarters(2 + 0 * core), tokens, others, ((got, 1),), rows_first)
+        return oth
+
+    def to_y(tokens, others, rows_first, got, arrived):
+        own = grad_quarters(
+            quarters(core), tokens, others, ((got, 0), (arrived, 0)), rows_first
+        )[0]
+        return own
+
+    def finish(own, behind, rows_first):
+        if y_count == 2:
+            other = after(swap(own, "y"), behind)
+            total = (own.astype(F32) + other.astype(F32)).astype(BF16)
+        else:
+            total = lax.psum(own, "y")
+        rest = swap(total, "core")
+        return jnp.concatenate(
+            [jnp.where(core == 0, total, rest), jnp.where(core == 0, rest, total)],
+            axis=1 if rows_first else 2,
+        ).astype(F32)
+
+    gate_got = to_core(tokens_b, gate_up_grad, True)
+    down_got = to_core(grad_rows, hidden[None], False)
+    down_oth = to_row(grad_rows, hidden[None], False, down_got)
+    gate_oth = to_row(tokens_b, gate_up_grad, True, gate_got)
+    down_arrived = swap(down_oth, "row")
+    gate_arrived = swap(after(gate_oth, down_oth), "row")
+
+    g2_low = after(g2_low, gate_oth, down_oth)
     g2_rows = gather_slots(g2_low, slots)
-    attended_grad = lax.dot_general(
-        g2_rows, w_out_full, (((1,), (1,)), ((), ())), preferred_element_type=F32
-    ).astype(BF16)
-    columns = attended_grad.shape[1] // 2
-    grad_mine = take(attended_grad, core * columns, columns, 1)
-    grad_from = swap(take(attended_grad, (1 - core) * columns, columns, 1), "core")
+    down_own = to_y(grad_rows, hidden[None], False, down_got, after(down_arrived, g2_rows))
+    columns = w_out.shape[0] // 2
+    grad_other = from_features((1 - core)[None], g2_rows, pieces_out, columns)[0]
+    grad_from = swap(grad_other, "core")
+    grad_mine = from_features(core[None], g2_rows, pieces_out, columns)[0]
+    part_down = to_features(after(hidden, g2_rows)[None], [p[None] for p in pieces_down], False)
+    terms_down = scatter_slots(part_down, slots)
+    out_got = to_core(g2_rows, attended[None], False)
     mixed_mine, mixed_other, bias_part = attend_back(
         qkv_mine, qkv_from, grad_mine, grad_from, lse, rotary_mine, rotary_other, table_of, factor
     )
@@ -651,104 +793,57 @@
         ],
         axis=2,
     )
-    part_a = lax.dot_general(
-        mixed[0], w_in_full[0], (((1,), (1,)), ((), ())), preferred_element_type=F32
-    )
-    for i in (1, 2):
-        part_a += lax.dot_general(
-            mixed[i], w_in_full[i], (((1,), (1,)), ((), ())), preferred_element_type=F32
-        )
-    terms = scatter_slots(part_a.astype(BF16), slots)
+    part_a = to_features(mixed, pieces_in, True)
+    terms = scatter_slots(part_a, slots)
+    in_got = to_core(tokens_a, mixed, True)
+    gate_own = to_y(tokens_b, gate_up_grad, True, gate_got, after(gate_arrived, part_a))
+    out_oth = to_row(g2_rows, attended[None], False, after(out_got, part_a))
+    out_arrived = swap(out_oth, "row")
+    in_oth = to_row(tokens_a, mixed, True, in_got)
+    in_arrived = swap(after(in_oth, out_oth), "row")
+    out_own = to_y(g2_rows, attended[None], False, out_got, out_arrived)
+    in_own = to_y(tokens_a, mixed, True, in_got, in_arrived)
     input_low, sums_a = norm_back(stream, terms, g2, gain_a, 0)
+    layer_low = (residual + sum(t.astype(F32) for t in terms_down)).astype(BF16)
+    layer_out = from_sequence(after(layer_low, part_a))
     input_grad = from_sequence(input_low).astype(F32)
-
-    def sum_y(x):
-        if y_count == 2:
-            return (x.astype(F32) + swap(x, "y").astype(F32)).astype(x.dtype)
-        return lax.psum(x, "y")
-
-    def reduce_weight(grad, cut, join):
-        size = grad.shape[cut] if cut != join else grad.shape[cut] // 2
-        part = size // 2
-        if cut == join:
-            shape = list(grad.shape)
-            shape[cut : cut + 1] = [2, size]
-            grad = grad.reshape(shape)
-            cut_at, join_at = cut + 1, join
+    down_grad = finish(down_own, part_a, False)[0]
+    gate_grad = finish(gate_own, part_a, True)
+    out_grad = finish(out_own, part_a, False)[0]
+    in_grad = finish(in_own, part_a, True)
+
+    def reduce_vector(own, oth, same):
+        total = jnp.concatenate([own, same, oth], axis=0)
+        if slots == 4:
+            pair = total + lax.ppermute(total, "col", PAIR)
+            inner = pair + lax.ppermute(pair, "col", MID)
+            outer = lax.ppermute(inner, "col", OUT)
+            total = jnp.where((place == 0) | (place == 3), outer, inner)
         else:
-            shape = list(grad.shape)
-            shape[join : join + 1] = [2, grad.shape[join] // 2]
-            cut_at, join_at = cut, join
-            halves = jnp.split(grad, 2, axis=join)
-            grad = None
-        if grad is not None:
-            pieces = [lax.index_in_dim(grad, i, join_at, keepdims=False) for i in range(2)]
-        else:
-            pieces = halves
-        sent = [swap(take(p, (1 - core) * part, part, cut), "core") for p in pieces]
-        kept = [
-            (take(p, core * part, part, cut).astype(F32) + s.astype(F32))
-            for p, s in zip(pieces, sent)
-        ]
-        arrived = swap(kept[1].astype(BF16), "row")
-        total = sum_y((kept[0] + arrived.astype(F32)).astype(BF16))
-        rest = swap(total, "core")
-        first = jnp.where(core == 0, total, rest)
-        second = jnp.where(core == 0, rest, total)
-        return jnp.concatenate([first, second], axis=cut).astype(F32)
-
-    down = (((0,), (0,)), ((), ()))
-    down_grad = lax.dot_general(hidden, grad_rows, down, preferred_element_type=F32).astype(BF16)
-    down_grad = reduce_weight(down_grad, 0, 1)
-    gate_grad = jnp.stack(
-        [
-            lax.dot_general(tokens_b, gate_up_grad[i], down, preferred_element_type=F32).astype(BF16)
-            for i in range(2)
-        ]
-    )
-    gate_grad = reduce_weight(gate_grad, 1, 1)
-    out_grad = lax.dot_general(attended, g2_rows, down, preferred_element_type=F32).astype(BF16)
-    out_grad = reduce_weight(out_grad, 0, 1)
-    in_grad = jnp.stack(
-        [
-            lax.dot_general(tokens_a, mixed[i], down, preferred_element_type=F32).astype(BF16)
-            for i in range(3)
-        ]
-    )
-    in_grad = reduce_weight(in_grad, 1, 1)
-
-    bias_sum = bias_part[:, 0, :]
-    bias_sum = bias_sum + swap(bias_sum, "row")
-    bias_sum = lax.psum(bias_sum, "y") if y_count != 2 else bias_sum + swap(bias_sum, "y")
-    bias_other = swap(bias_sum, "core")
-    bias_grad = jnp.concatenate(
-        [jnp.where(core == 0, bias_sum, bias_other), jnp.where(core == 0, bias_other, bias_sum)],
-        axis=1,
-    )
-
-    def reduce_vector(sums):
-        total = sums[:, :wide] + swap(sums[:, wide:], "row")
+            total = lax.psum(total, "col")
         total = total + swap(total, "core")
-        total = lax.psum(total, "y") if y_count != 2 else total + swap(total, "y")
-        if slots != 4:
-            return lax.psum(total, "col")
-        pair = total + lax.ppermute(total, "col", PAIR)
-        inner = pair + lax.ppermute(pair, "col", MID)
-        outer = lax.ppermute(inner, "col", OUT)
-        return jnp.where((place == 0) | (place == 3), outer, inner)
-
-    vec_b = reduce_vector(sums_b)
-    vec_a = reduce_vector(sums_a)
+        count = own.shape[0] + same.shape[0]
+        sent = jnp.concatenate([total[count:], total[own.shape[0] : count]], axis=0)
+        total = total[:count] + swap(sent, "row")
+        return lax.psum(total, "y") if y_count != 2 else total + swap(total, "y")
+
+    bias_all = jnp.zeros((3, 2 * slots * columns), F32)
+    bias_all = lax.dynamic_update_slice(
+        bias_all, bias_part[:, 0, :], (jnp.int32(0), (place * 2 + core) * columns)
+    ).reshape(-1, wide)
+    sums = jnp.concatenate([sums_a, sums_b], axis=0)
+    vectors = reduce_vector(sums[:, :wide], natural(sums[:, wide:]), bias_all)
+    bias_grad = take(vectors[4:].reshape(3, -1), place * 2 * columns, 2 * columns, 1)
     return (
         layer_out[None],
         input_grad,
-        vec_a[0:1],
-        vec_a[1:2],
+        vectors[0:1],
+        vectors[1:2],
         jnp.transpose(in_grad, (1, 0, 2))[None],
         bias_grad[None],
         out_grad[None],
-        vec_b[0:1],
-        vec_b[1:2],
+        vectors[2:3],
+        vectors[3:4],
         jnp.transpose(gate_grad, (1, 0, 2))[None],
         down_grad[None],
     )

time: 871 us -> 663 us (0.76)
  local copies, waits for them, and re-layouts: 215 us -> 36.7 us
  Pallas kernels: 74.9 us -> 134 us
  other arithmetic: 105 us -> 51.1 us
  matrix products: 40.2 us -> 0 us
    another operation x7 -> x0, local copies, waits for them, and re-layouts: 125 us -> none  [the longest x2 122 us: local(): jnp.stack([lax.dot_general(tokens_b, gate_up_grad[i], down, preferred_ele...]
    ppermute x50 -> x32, waiting for transfers between devices: 180 us -> 120 us  [swap(): return lax.ppermute(x, axis, [(0, 1), (1, 0)])]
    pallas_call x1 -> x20, Pallas kernels: 34.3 us -> 93.9 us  [the longest x12 42.5 us: grad_quarters(): pl.pallas_call(body, grid_spec=pltpu.PrefetchScalarGridSpec(num_scalar_pr...]
    dot_general x14 -> x0, matrix products: 40.2 us -> none  [the longest x2 9.93 us: local(): lax.dot_general(tokens_b, gate_up_grad[i], down, preferred_element_type=F32)]
    convert_element_type x15 -> x7, other arithmetic: 40.6 us -> 14.8 us  [the longest x4 8.16 us: finish(): total = (own.astype(F32) + other.astype(F32)).astype(BF16)]
    ppermute x4, starting transfers between devices: 8.48 us -> 34.3 us  [scatter_slots(): two = part[2] + lax.ppermute(part[2], 'col', IN)]
    dynamic_update_slice x16 -> x1, local copies, waits for them, and re-layouts: 22.3 us -> 0.01 us  [local(): lax.dynamic_update_slice(bias_all, bias_part[:, 0, :], (jnp.int32(0), (pl...]
    pad x4 -> x0, local copies, waits for them, and re-layouts: 20.8 us -> none  [assemble(): full = lax.pad(w, jnp.zeros((), w.dtype), pads)]
  transfers between devices with their start and end apart: 104 -> 83, of which waited for: 33 -> 30; matrix products, arithmetic and copies ran while one was open for 39% -> 11% of each run, Pallas kernels for 5% -> 16%
where the time goes in v2:
time: 663 us; the launch traced here: 652 us
  waiting for transfers between devices  287 us (43%)
  starting transfers between devices  141 us (21%)
  Pallas kernels  134 us (20%)
  other arithmetic  51.1 us (8%)
  local copies, waits for them, and re-layouts  36.7 us (6%)
    ppermute x32, waiting for transfers between devices, swap(): return lax.ppermute(x, axis, [(0, 1), (1, 0)])  120 us
    pallas_call x12, Pallas kernels, grad_quarters(): pl.pallas_call(body, grid_spec=pltpu.PrefetchScalarGridSpec(num_scalar_pr...  42.5 us
    ppermute x4, waiting for transfers between devices, gather_slots(): three = far + lax.ppermute(far, 'col', OUT)  39.7 us
    ppermute x4, waiting for transfers between devices, gather_slots(): two = mid + lax.ppermute(mid, 'col', OUT)  35.3 us
    ppermute x4, starting transfers between devices, scatter_slots(): two = part[2] + lax.ppermute(part[2], 'col', IN)  34.3 us
    pallas_call x4, Pallas kernels, to_features(): pl.pallas_call(body, grid=(width // block,), in_specs=[pl.BlockSpec((coun...  32.5 us
    ppermute x4, waiting for transfers between devices, gather_slots(): one = lax.ppermute(own, 'col', PAIR)  31.6 us
    ppermute x32, starting transfers between devices, swap(): return lax.ppermute(x, axis, [(0, 1), (1, 0)])  21.7 us
  transfers between devices with their start and end apart: 83, of which 30 were waited for; matrix products, arithmetic and copies ran while one was open for 11% of the time, Pallas kernels for 16%

profile of v2, /device:TPU:0, one launch (start us, length us, event | category | flops | bytes accessed | tf_op | source)
XLA Modules:
  0.0 652.5 jit_solution(2575549902877567801)
XLA Ops:
  25.8 9.0 %collective-permute-done.3 = bf16[128,2048]{1,0:T(8,128)(2,1)S(1)} collective-permute-done((bf16[128,2048]{1,0:T(8,128)(2,1)S(1)}, bf16[128,2048]{1,0:T(8,128)(2,1)S(1)}, u32[]{:S(2)}, u32[]{:S(2)}) %collective-permute-start.3) | collective-permute-done | bytes 524320 | tf_op jit(solution)/shard_map/ppermute | solution.py:42
  41.3 14.0 %collective-permute-done.5 = bf16[128,2048]{1,0:T(8,128)(2,1)S(1)} collective-permute-done((bf16[128,2048]{1,0:T(8,128)(2,1)S(1)}, bf16[128,2048]{1,0:T(8,128)(2,1)S(1)}, u32[]{:S(2)}, u32[]{:S(2)}) %collective-permute-start.5) | collective-permute-done | bytes 524320 | tf_op jit(solution)/shard_map/ppermute | solution.py:45
  55.4 11.1 %collective-permute-done.7 = bf16[128,2048]{1,0:T(8,128)(2,1)S(1)} collective-permute-done((bf16[128,2048]{1,0:T(8,128)(2,1)S(1)}, bf16[128,2048]{1,0:T(8,128)(2,1)S(1)}, u32[]{:S(2)}, u32[]{:S(2)}) %collective-permute-start.7) | collective-permute-done | bytes 524320 | tf_op jit(solution)/shard_map/ppermute | solution.py:46
  80.5 9.9 %attend.1 = (bf16[512,256]{1,0:T(8,128)(2,1)S(1)}, bf16[512,256]{1,0:T(8,128)(2,1)S(1)}, f32[2,1024,2]{2,1,0:T(8,128)S(1)}) custom-call(s32[5]{0:T(128)S(1)} %pad_add_fusion.order_ref, bf16[3,512,256]{2,1,0:T(8,128)(2,1)S(1)} %qkv_columns.2.mine_ref, bf16[3,512,256]{2,1,0:T(8,128)(2,1)S(1)} %collective-permute-done.12.other_ref), custom_call_target="tpu_custom_call" | custom-call | flops 1073741824 | bytes 2097152 | tf_op jit(solution)/shard_map/attend/pallas_call | solution.py:294
  105.7 8.3 %collective-permute-done.18 = bf16[128,2048]{1,0:T(8,128)(2,1)S(1)} collective-permute-done((bf16[128,2048]{1,0:T(8,128)(2,1)S(1)}, bf16[128,2048]{1,0:T(8,128)(2,1)S(1)}, u32[]{:S(2)}, u32[]{:S(2)}) %collective-permute-start.18) | collective-permute-done | bytes 524320 | tf_op jit(solution)/shard_map/ppermute | solution.py:56
  144.1 8.4 %collective-permute-done.32 = bf16[128,2048]{1,0:T(8,128)(2,1)S(1)} collective-permute-done((bf16[128,2048]{1,0:T(8,128)(2,1)S(1)}, bf16[128,2048]{1,0:T(8,128)(2,1)S(1)}, u32[]{:S(2)}, u32[]{:S(2)}) %collective-permute-start.32) | collective-permute-done | bytes 524320 | tf_op jit(solution)/shard_map/ppermute | solution.py:46
  165.9 11.7 %collective-permute-done.21 = bf16[128,2048]{1,0:T(8,128)(2,1)S(1)} collective-permute-done((bf16[128,2048]{1,0:T(8,128)(2,1)S(1)}, bf16[128,2048]{1,0:T(8,128)(2,1)S(1)}, u32[]{:S(2)}, u32[]{:S(2)}) %collective-permute-start.21) | collective-permute-done | bytes 524320 | tf_op jit(solution)/shard_map/ppermute | solution.py:42
  178.3 13.0 %collective-permute-done.23 = bf16[128,2048]{1,0:T(8,128)(2,1)S(1)} collective-permute-done((bf16[128,2048]{1,0:T(8,128)(2,1)S(1)}, bf16[128,2048]{1,0:T(8,128)(2,1)S(1)}, u32[]{:S(2)}, u32[]{:S(2)}) %collective-permute-start.23) | collective-permute-done | bytes 524320 | tf_op jit(solution)/shard_map/ppermute | solution.py:45
  197.6 9.6 %collective-permute-done.25 = bf16[128,2048]{1,0:T(8,128)(2,1)S(1)} collective-permute-done((bf16[128,2048]{1,0:T(8,128)(2,1)S(1)}, bf16[128,2048]{1,0:T(8,128)(2,1)S(1)}, u32[]{:S(2)}, u32[]{:S(2)}) %collective-permute-start.25) | collective-permute-done | bytes 524320 | tf_op jit(solution)/shard_map/ppermute | solution.py:46
  207.5 10.2 %collective-permute-done.26.refs_1_ = bf16[2,512,1408]{2,1,0:T(8,128)(2,1)S(1)} collective-permute-done((bf16[2,512,1408]{2,1,0:T(8,128)(2,1)S(1)}, bf16[2,512,1408]{2,1,0:T(8,128)(2,1)S(1)}, u32[]{:S(2)}, u32[]{:S(2)}) %collective-permute-start.26) | collective-permute-done | bytes 2883616 | tf_op jit(solution)/shard_map/ppermute | solution.py:23
  224.7 13.2 %feed_forward.1 = (bf16[512,1408]{1,0:T(8,128)(2,1)S(1)}, bf16[2,512,1408]{2,1,0:T(8,128)(2,1)}) custom-call(bf16[512,2048]{1,0:T(8,128)(2,1)S(1)} %pad_maximum_fusion.1.x_ref, bf16[2,1024,1408]{2,1,0:T(8,128)(2,1)} %bitcast.88, bf16[2,512,1408]{2,1,0:T(8,128)(2,1)} %copy-done.51, bf16[2,512,1408]{2,1,0:T(8,128)(2,1)} %copy-done.52, ...), custom_call_target="tpu_custom_call" | custom-call | flops 5905580032 | bytes 13631488 | tf_op jit(solution)/shard_map/feed_forward/pallas_call | solution.py:463
  250.2 12.6 %to_features.5 = bf16[512,2048]{1,0:T(8,128)(2,1)} custom-call(bf16[2,512,1408]{2,1,0:T(8,128)(2,1)} %get-tuple-element.71.v_ref.y_ref, bf16[2,1024,1408]{2,1,0:T(8,128)(2,1)} %bitcast.89, bf16[2,512,1408]{2,1,0:T(8,128)(2,1)} %copy-done.51, bf16[2,512,1408]{2,1,0:T(8,128)(2,1)} %copy-done.52), custom_call_target="tpu_custom_call" | custom-call | flops 5905580032 | bytes 16515072 | tf_op jit(solution)/shard_map/to_features/pallas_call | solution.py:513
  265.6 11.5 %collective-permute-done.37 = bf16[128,2048]{1,0:T(8,128)(2,1)S(1)} collective-permute-done((bf16[128,2048]{1,0:T(8,128)(2,1)S(1)}, bf16[128,2048]{1,0:T(8,128)(2,1)S(1)}, u32[]{:S(2)}, u32[]{:S(2)}) %collective-permute-start.37) | collective-permute-done | bytes 524320 | tf_op jit(solution)/shard_map/ppermute | solution.py:56
  285.2 10.3 %collective-permute-done.35 = bf16[128,2048]{1,0:T(8,128)(2,1)S(1)} collective-permute-done((bf16[128,2048]{1,0:T(8,128)(2,1)S(1)}, bf16[128,2048]{1,0:T(8,128)(2,1)S(1)}, u32[]{:S(2)}, u32[]{:S(2)}) %collective-permute-start.35) | collective-permute-done | bytes 524320 | tf_op jit(solution)/shard_map/ppermute | solution.py:57
  298.2 12.2 %collective-permute-start.36 = (bf16[128,2048]{1,0:T(8,128)(2,1)S(1)}, bf16[128,2048]{1,0:T(8,128)(2,1)S(1)}, u32[]{:S(2)}, u32[]{:S(2)}) collective-permute-start(bf16[128,2048]{1,0:T(8,128)(2,1)S(1)} %get-tuple-element.122), channel_id=1, source_target_pairs={{1,2},{2,1},{5,6},{6,5},{9,10},{10,9},{13,14},{14,13},{17,18},{18,... | collective-permute-start | bytes 1572872 | tf_op jit(solution)/shard_map/ppermute | solution.py:59
  325.2 9.3 %collective-permute-done.42 = bf16[128,2048]{1,0:T(8,128)(2,1)S(1)} collective-permute-done((bf16[128,2048]{1,0:T(8,128)(2,1)S(1)}, bf16[128,2048]{1,0:T(8,128)(2,1)S(1)}, u32[]{:S(2)}, u32[]{:S(2)}) %collective-permute-start.42) | collective-permute-done | bytes 524320 | tf_op jit(solution)/shard_map/ppermute | solution.py:42
  349.3 10.6 %collective-permute-done.46 = bf16[128,2048]{1,0:T(8,128)(2,1)} collective-permute-done((bf16[128,2048]{1,0:T(8,128)(2,1)S(1)}, bf16[128,2048]{1,0:T(8,128)(2,1)}, u32[]{:S(2)}, u32[]{:S(2)}) %collective-permute-start.46) | collective-permute-done | bytes 524320 | tf_op jit(solution)/shard_map/ppermute | solution.py:46
  372.7 16.3 %collective-permute-start.47 = (bf16[128,2048]{1,0:T(8,128)(2,1)}, bf16[128,2048]{1,0:T(8,128)(2,1)}, u32[]{:S(2)}, u32[]{:S(2)}) collective-permute-start(bf16[128,2048]{1,0:T(8,128)(2,1)} %get-tuple-element.119), channel_id=1, source_target_pairs={{0,1},{3,2},{4,5},{7,6},{8,9},{11,10},{12,13},{15,14},{16,17},{19,... | collective-permute-start | bytes 1572872 | tf_op jit(solution)/shard_map/ppermute | solution.py:57
  394.2 16.2 %attend_back.1 = (bf16[3,512,256]{2,1,0:T(8,128)(2,1)S(1)}, bf16[3,512,256]{2,1,0:T(8,128)(2,1)}, f32[3,1,256]{2,1,0:T(1,128)S(1)}) custom-call(s32[5]{0:T(128)S(1)} %pad_add_fusion.order_ref, bf16[3,512,256]{2,1,0:T(8,128)(2,1)} %copy-done.27, bf16[3,512,256]{2,1,0:T(8,128)(2,1)} %copy-done.32, bf16[512,256]{1,0:T(8,128)(2,1)S(1)} %bitcast.82, ...), custom_call_target="tpu_custom_call" | custom-call | flops 2684354560 | bytes 5242880 | tf_op jit(solution)/shard_map/attend_back/pallas_call | solution.py:404
  433.6 12.5 %collective-permute-start.58 = (bf16[128,2048]{1,0:T(8,128)(2,1)}, bf16[128,2048]{1,0:T(8,128)(2,1)S(1)}, u32[]{:S(2)}, u32[]{:S(2)}) collective-permute-start(bf16[128,2048]{1,0:T(8,128)(2,1)} %slice.216), channel_id=1, source_target_pairs={{0,1},{3,2},{4,5},{7,6},{8,9},{11,10},{12,13},{15,14},{16,17},{19,... | collective-permute-start | bytes 1572872 | tf_op jit(solution)/shard_map/ppermute | solution.py:56
  487.8 50.6 %collective-permute-done.75 = bf16[1,512,512]{2,1,0:T(8,128)(2,1)S(1)} collective-permute-done((bf16[1,512,512]{2,1,0:T(8,128)(2,1)S(1)}, bf16[1,512,512]{2,1,0:T(8,128)(2,1)S(1)}, u32[]{:S(2)}, u32[]{:S(2)}) %collective-permute-start.75) | collective-permute-done | bytes 524320 | tf_op jit(solution)/shard_map/ppermute | solution.py:23
  562.7 21.2 %collective-permute-done.71.refs_1_ = bf16[1,3,512,512]{3,2,1,0:T(8,128)(2,1)S(1)} collective-permute-done((bf16[1,3,512,512]{3,2,1,0:T(8,128)(2,1)S(1)}, bf16[1,3,512,512]{3,2,1,0:T(8,128)(2,1)S(1)}, u32[]{:S(2)}, u32[]{:S(2)}) %collective-permute-start.71) | collective-permute-done | bytes 1572896 | tf_op jit(solution)/shard_map/ppermute | solution.py:23
  596.2 30.0 %collective-permute-done.68 = f32[10,1024]{1,0:T(8,128)S(1)} collective-permute-done((f32[10,1024]{1,0:T(8,128)S(1)}, f32[10,1024]{1,0:T(8,128)S(1)}, u32[]{:S(2)}, u32[]{:S(2)}) %collective-permute-start.68) | collective-permute-done | bytes 40992 | tf_op jit(solution)/shard_map/ppermute | solution.py:23
  636.7 10.1 %copy.24 = f32[1,1024,2,1408]{3,2,1,0:T(2,128)} copy(f32[1,1024,2,1408]{3,1,2,0:T(8,128)S(1)} %convert_bitcast_fusion) | data formatting | bytes 23068672
  (377 shorter events, 308.1 us)
Async XLA Ops:
  25.1 41.8 %collective-permute-start.10 = (bf16[3,512,512]{2,1,0:T(8,128)(2,1)}, bf16[3,512,512]{2,1,0:T(8,128)(2,1)}, u32[]{:S(2)}, u32[]{:S(2)}) collective-permute-start(bf16[3,512,512]{2,1,0:T(8,128)(2,1)} %dynamic-slice_bitcast_fusion), channel_id=1, source_target_pairs={{0,4},{4,0},{1,5},{5,1},{2,6},{6,2},{3,7},{7,3},{8,12},{12,8},{9,1... | collective-permute-start | bytes 4718600 | tf_op jit(solution)/shard_map/ppermute | solution.py:23
  123.6 38.7 %collective-permute-start.27 = (bf16[1408,512]{1,0:T(8,128)(2,1)S(1)}, bf16[1408,512]{1,0:T(8,128)(2,1)S(1)}, u32[]{:S(2)}, u32[]{:S(2)}) collective-permute-start(bf16[1408,512]{1,0:T(8,128)(2,1)S(1)} %dynamic-slice_bitcast_fusion.1), channel_id=1, source_target_pairs={{0,4},{4,0},{1,5},{5,1},{2,6},{6,2},{3,7},{7,3},{8,12},{12,8},{9,1... | collective-permute-start | bytes 4325384 | tf_op jit(solution)/shard_map/ppermute | solution.py:23
  142.9 74.8 %collective-permute-start.26 = (bf16[2,512,1408]{2,1,0:T(8,128)(2,1)S(1)}, bf16[2,512,1408]{2,1,0:T(8,128)(2,1)S(1)}, u32[]{:S(2)}, u32[]{:S(2)}) collective-permute-start(bf16[2,512,1408]{2,1,0:T(8,128)(2,1)S(1)} %constant_dynamic-slice_fusion.1), channel_id=1, source_target_pairs={{0,4},{4,0},{1,5},{5,1},{2,6},{6,2},{3,7},{7,3},{8,12},{12,8},{9,1... | collective-permute-start | bytes 8650760 | tf_op jit(solution)/shard_map/ppermute | solution.py:23
  246.1 70.6 %collective-permute-start.40 = (bf16[2,2,512,1408]{3,2,1,0:T(8,128)(2,1)}, bf16[2,2,512,1408]{3,2,1,0:T(8,128)(2,1)}, u32[]{:S(2)}, u32[]{:S(2)}) collective-permute-start(bf16[2,2,512,1408]{3,2,1,0:T(8,128)(2,1)} %grad_quarters.12), channel_id=1, source_target_pairs={{0,8},{8,0},{1,9},{9,1},{2,10},{10,2},{3,11},{11,3},{4,12},{12,4},... | collective-permute-start | bytes 17301512 | tf_op jit(solution)/shard_map/ppermute | solution.py:23
  249.8 63.3 %collective-permute-start.41 = (bf16[2,1,1408,512]{3,2,1,0:T(8,128)(2,1)}, bf16[2,1,1408,512]{3,2,1,0:T(8,128)(2,1)}, u32[]{:S(2)}, u32[]{:S(2)}) collective-permute-start(bf16[2,1,1408,512]{3,2,1,0:T(8,128)(2,1)} %grad_quarters.14), channel_id=1, source_target_pairs={{0,8},{8,0},{1,9},{9,1},{2,10},{10,2},{3,11},{11,3},{4,12},{12,4},... | collective-permute-start | bytes 8650760 | tf_op jit(solution)/shard_map/ppermute | solution.py:23
  337.8 34.9 %collective-permute-start.80 = (bf16[1,1,1408,512]{3,2,1,0:T(8,128)(2,1)}, bf16[1,1,1408,512]{3,2,1,0:T(8,128)(2,1)}, u32[]{:S(2)}, u32[]{:S(2)}) collective-permute-start(bf16[1,1,1408,512]{3,2,1,0:T(8,128)(2,1)} %grad_quarters.15), channel_id=1, source_target_pairs={{0,4},{4,0},{1,5},{5,1},{2,6},{6,2},{3,7},{7,3},{8,12},{12,8},{9,1... | collective-permute-start | bytes 4325384 | tf_op jit(solution)/shard_map/ppermute | solution.py:23
  339.7 114.1 %collective-permute-start.77 = (bf16[1,2,512,1408]{3,2,1,0:T(8,128)(2,1)}, bf16[1,2,512,1408]{3,2,1,0:T(8,128)(2,1)}, u32[]{:S(2)}, u32[]{:S(2)}) collective-permute-start(bf16[1,2,512,1408]{3,2,1,0:T(8,128)(2,1)} %grad_quarters.13), channel_id=1, source_target_pairs={{0,4},{4,0},{1,5},{5,1},{2,6},{6,2},{3,7},{7,3},{8,12},{12,8},{9,1... | collective-permute-start | bytes 8650760 | tf_op jit(solution)/shard_map/ppermute | solution.py:23
  362.0 32.2 %collective-permute-start.52 = (bf16[512,256]{1,0:T(8,128)(2,1)S(1)}, bf16[512,256]{1,0:T(8,128)(2,1)S(1)}, u32[]{:S(2)}, u32[]{:S(2)}) collective-permute-start(bf16[512,256]{1,0:T(8,128)(2,1)S(1)} %bitcast.81), channel_id=1, source_target_pairs={{0,8},{8,0},{1,9},{9,1},{2,10},{10,2},{3,11},{11,3},{4,12},{12,4},... | collective-permute-start | bytes 786440 | tf_op jit(solution)/shard_map/ppermute | solution.py:23
  372.7 42.4 %collective-permute-start.47 = (bf16[128,2048]{1,0:T(8,128)(2,1)}, bf16[128,2048]{1,0:T(8,128)(2,1)}, u32[]{:S(2)}, u32[]{:S(2)}) collective-permute-start(bf16[128,2048]{1,0:T(8,128)(2,1)} %get-tuple-element.119), channel_id=1, source_target_pairs={{0,1},{3,2},{4,5},{7,6},{8,9},{11,10},{12,13},{15,14},{16,17},{19,... | collective-permute-start | bytes 1572872 | tf_op jit(solution)/shard_map/ppermute | solution.py:57
  393.4 53.7 %collective-permute-start.70 = (bf16[2,1,512,512]{3,2,1,0:T(8,128)(2,1)}, bf16[2,1,512,512]{3,2,1,0:T(8,128)(2,1)}, u32[]{:S(2)}, u32[]{:S(2)}) collective-permute-start(bf16[2,1,512,512]{3,2,1,0:T(8,128)(2,1)} %grad_quarters.18), channel_id=1, source_target_pairs={{0,8},{8,0},{1,9},{9,1},{2,10},{10,2},{3,11},{11,3},{4,12},{12,4},... | collective-permute-start | bytes 3145736 | tf_op jit(solution)/shard_map/ppermute | solution.py:23
  415.1 44.2 %collective-permute-start.81 = (bf16[1,1408,512]{2,1,0:T(8,128)(2,1)}, bf16[1,1408,512]{2,1,0:T(8,128)(2,1)S(1)}, u32[]{:S(2)}, u32[]{:S(2)}) collective-permute-start(bf16[1,1408,512]{2,1,0:T(8,128)(2,1)} %bitcast.76), channel_id=1, source_target_pairs={{0,16},{16,0},{1,17},{17,1},{2,18},{18,2},{3,19},{19,3},{4,20},{20... | collective-permute-start | bytes 4325384 | tf_op jit(solution)/shard_map/ppermute | solution.py:23
  419.1 44.1 %collective-permute-start.48 = (bf16[128,2048]{1,0:T(8,128)(2,1)}, bf16[128,2048]{1,0:T(8,128)(2,1)}, u32[]{:S(2)}, u32[]{:S(2)}) collective-permute-start(bf16[128,2048]{1,0:T(8,128)(2,1)} %get-tuple-element.117), channel_id=1, source_target_pairs={{1,2},{2,1},{5,6},{6,5},{9,10},{10,9},{13,14},{14,13},{17,18},{18,... | collective-permute-start | bytes 1572872 | tf_op jit(solution)/shard_map/ppermute | solution.py:59
  460.4 82.7 %collective-permute-start.69 = (bf16[2,3,512,512]{3,2,1,0:T(8,128)(2,1)}, bf16[2,3,512,512]{3,2,1,0:T(8,128)(2,1)}, u32[]{:S(2)}, u32[]{:S(2)}) collective-permute-start(bf16[2,3,512,512]{3,2,1,0:T(8,128)(2,1)} %grad_quarters.16), channel_id=1, source_target_pairs={{0,8},{8,0},{1,9},{9,1},{2,10},{10,2},{3,11},{11,3},{4,12},{12,4},... | collective-permute-start | bytes 9437192 | tf_op jit(solution)/shard_map/ppermute | solution.py:23
  462.6 89.4 %collective-permute-start.78 = (bf16[2,512,1408]{2,1,0:T(8,128)(2,1)S(1)}, bf16[2,512,1408]{2,1,0:T(8,128)(2,1)}, u32[]{:S(2)}, u32[]{:S(2)}) collective-permute-start(bf16[2,512,1408]{2,1,0:T(8,128)(2,1)S(1)} %bitcast.74), channel_id=1, source_target_pairs={{0,16},{16,0},{1,17},{17,1},{2,18},{18,2},{3,19},{19,3},{4,20},{20... | collective-permute-start | bytes 8650760 | tf_op jit(solution)/shard_map/ppermute | solution.py:23
  481.4 57.1 %collective-permute-start.75 = (bf16[1,512,512]{2,1,0:T(8,128)(2,1)S(1)}, bf16[1,512,512]{2,1,0:T(8,128)(2,1)S(1)}, u32[]{:S(2)}, u32[]{:S(2)}) collective-permute-start(bf16[1,512,512]{2,1,0:T(8,128)(2,1)S(1)} %bitcast.79), channel_id=1, source_target_pairs={{0,16},{16,0},{1,17},{17,1},{2,18},{18,2},{3,19},{19,3},{4,20},{20... | collective-permute-start | bytes 1572872 | tf_op jit(solution)/shard_map/ppermute | solution.py:23
  483.7 54.9 %collective-permute-start.60 = (bf16[128,2048]{1,0:T(8,128)(2,1)S(1)}, bf16[128,2048]{1,0:T(8,128)(2,1)S(1)}, u32[]{:S(2)}, u32[]{:S(2)}) collective-permute-start(bf16[128,2048]{1,0:T(8,128)(2,1)S(1)} %get-tuple-element.112), channel_id=1, source_target_pairs={{0,1},{1,0},{2,3},{3,2},{4,5},{5,4},{6,7},{7,6},{8,9},{9,8},{10,11... | collective-permute-start | bytes 1572872 | tf_op jit(solution)/shard_map/ppermute | solution.py:60
  486.2 52.9 %collective-permute-start.57 = (bf16[128,2048]{1,0:T(8,128)(2,1)S(1)}, bf16[128,2048]{1,0:T(8,128)(2,1)S(1)}, u32[]{:S(2)}, u32[]{:S(2)}) collective-permute-start(bf16[128,2048]{1,0:T(8,128)(2,1)S(1)} %get-tuple-element.113), channel_id=1, source_target_pairs={{1,2},{2,1},{5,6},{6,5},{9,10},{10,9},{13,14},{14,13},{17,18},{18,... | collective-permute-start | bytes 1572872 | tf_op jit(solution)/shard_map/ppermute | solution.py:59
  538.4 50.9 %collective-permute-start.82 = (bf16[1,1408,512]{2,1,0:T(8,128)(2,1)S(1)}, bf16[1,1408,512]{2,1,0:T(8,128)(2,1)S(1)}, u32[]{:S(2)}, u32[]{:S(2)}) collective-permute-start(bf16[1,1408,512]{2,1,0:T(8,128)(2,1)S(1)} %add_convert_fusion.2), channel_id=1, source_target_pairs={{0,8},{8,0},{1,9},{9,1},{2,10},{10,2},{3,11},{11,3},{4,12},{12,4},... | collective-permute-start | bytes 4325384 | tf_op jit(solution)/shard_map/ppermute | solution.py:23
  543.1 50.3 %collective-permute-start.61 = (bf16[128,1024]{1,0:T(8,128)(2,1)S(1)}, bf16[128,1024]{1,0:T(8,128)(2,1)S(1)}, u32[]{:S(2)}, u32[]{:S(2)}) collective-permute-start(bf16[128,1024]{1,0:T(8,128)(2,1)S(1)} %get-tuple-element.137), channel_id=1, source_target_pairs={{0,0},{8,4},{4,8},{12,12},{1,1},{9,5},{5,9},{13,13},{2,2},{10,6},{... | collective-permute-start | bytes 786440 | tf_op jit(solution)/shard_map/ppermute | solution.py:669
  546.9 37.0 %collective-permute-start.71 = (bf16[1,3,512,512]{3,2,1,0:T(8,128)(2,1)S(1)}, bf16[1,3,512,512]{3,2,1,0:T(8,128)(2,1)S(1)}, u32[]{:S(2)}, u32[]{:S(2)}) collective-permute-start(bf16[1,3,512,512]{3,2,1,0:T(8,128)(2,1)S(1)} %grad_quarters.17), channel_id=1, source_target_pairs={{0,4},{4,0},{1,5},{5,1},{2,6},{6,2},{3,7},{7,3},{8,12},{12,8},{9,1... | collective-permute-start | bytes 4718600 | tf_op jit(solution)/shard_map/ppermute | solution.py:23
  556.0 73.3 %collective-permute-start.79 = (bf16[2,512,1408]{2,1,0:T(8,128)(2,1)}, bf16[2,512,1408]{2,1,0:T(8,128)(2,1)}, u32[]{:S(2)}, u32[]{:S(2)}) collective-permute-start(bf16[2,512,1408]{2,1,0:T(8,128)(2,1)} %add_convert_fusion), channel_id=1, source_target_pairs={{0,8},{8,0},{1,9},{9,1},{2,10},{10,2},{3,11},{11,3},{4,12},{12,4},... | collective-permute-start | bytes 8650760 | tf_op jit(solution)/shard_map/ppermute | solution.py:23
  561.4 32.0 %collective-permute-start.62 = (bf16[128,1024]{1,0:T(8,128)(2,1)S(1)}, bf16[128,1024]{1,0:T(8,128)(2,1)S(1)}, u32[]{:S(2)}, u32[]{:S(2)}) collective-permute-start(bf16[128,1024]{1,0:T(8,128)(2,1)S(1)} %get-tuple-element.138), channel_id=1, source_target_pairs={{8,0},{0,4},{12,8},{4,12},{9,1},{1,5},{13,9},{5,13},{10,2},{2,6},{... | collective-permute-start | bytes 786440 | tf_op jit(solution)/shard_map/ppermute | solution.py:670
  589.3 37.5 %collective-permute-start.72 = (bf16[3,512,512]{2,1,0:T(8,128)(2,1)S(1)}, bf16[3,512,512]{2,1,0:T(8,128)(2,1)}, u32[]{:S(2)}, u32[]{:S(2)}) collective-permute-start(bf16[3,512,512]{2,1,0:T(8,128)(2,1)S(1)} %bitcast.75), channel_id=1, source_target_pairs={{0,16},{16,0},{1,17},{17,1},{2,18},{18,2},{3,19},{19,3},{4,20},{20... | collective-permute-start | bytes 4718600 | tf_op jit(solution)/shard_map/ppermute | solution.py:23
  593.5 32.6 %collective-permute-start.68 = (f32[10,1024]{1,0:T(8,128)S(1)}, f32[10,1024]{1,0:T(8,128)S(1)}, u32[]{:S(2)}, u32[]{:S(2)}) collective-permute-start(f32[10,1024]{1,0:T(8,128)S(1)} %slice_add_fusion.4), channel_id=1, source_target_pairs={{0,16},{16,0},{1,17},{17,1},{2,18},{18,2},{3,19},{19,3},{4,20},{20... | collective-permute-start | bytes 122888 | tf_op jit(solution)/shard_map/ppermute | solution.py:23
  (112 other events, 2122.9 us)

commit v3 on v2

--- a/solution.py
+++ b/solution.py
@@ -36,29 +36,75 @@
     return jnp.arange(count, dtype=jnp.int32)
 
 
-def gather_slots(own, count):
-    if count != 4:
-        return lax.all_gather(own, "col", axis=0, tiled=True)
-    one = lax.ppermute(own, "col", PAIR)
-    mid = lax.ppermute(own, "col", MID)
-    far = lax.ppermute(one, "col", MID)
-    two = mid + lax.ppermute(mid, "col", OUT)
-    three = far + lax.ppermute(far, "col", OUT)
-    return jnp.concatenate([own, one, two, three], axis=0)
-
-
-def scatter_slots(parts, count):
-    rows = parts.shape[0] // count
-    if count != 4:
-        mine = lax.psum_scatter(parts, "col", scatter_dimension=0, tiled=True)
-        return (mine, jnp.zeros_like(mine), jnp.zeros_like(mine))
-    part = [parts[i * rows : (i + 1) * rows] for i in range(4)]
-    three = part[3] + lax.ppermute(part[3], "col", IN)
-    two = part[2] + lax.ppermute(part[2], "col", IN)
-    one = part[1] + lax.ppermute(three, "col", MID)
-    from_mid = lax.ppermute(two, "col", MID)
-    from_pair = lax.ppermute(one, "col", PAIR)
-    return (part[0], from_mid, from_pair)
+def tie(values, *behind):
+    return lax.optimization_barrier((tuple(values), behind))[0]
+
+
+def after(x, *behind):
+    return tie((x,), *behind)[0] if behind else x
+
+
+class Gather:
+    def __init__(self, own, count):
+        self.own, self.count, self.got = own, count, []
+        self.flying = []
+        if count == 4:
+            self.flying = [lax.ppermute(own, "col", PAIR), lax.ppermute(own, "col", MID)]
+
+    def hop(self):
+        if self.count != 4:
+            return
+        if not self.got:
+            one, mid = self.flying
+            self.got = [one, mid]
+            self.flying = [lax.ppermute(one, "col", MID), lax.ppermute(mid, "col", OUT)]
+        else:
+            far, mid_out = self.flying
+            self.got += [far, mid_out]
+            self.flying = [lax.ppermute(far, "col", OUT)]
+
+    def rows(self):
+        if self.count != 4:
+            return lax.all_gather(self.own, "col", axis=0, tiled=True)
+        one, mid, far, mid_out = self.got
+        return jnp.concatenate([self.own, one, mid + mid_out, far + self.flying[0]], axis=0)
+
+
+class Scatter:
+    def __init__(self, parts, count):
+        self.count, self.step, self.parts = count, 0, parts
+        self.flying, self.two = [], None
+        if count == 4:
+            rows = parts.shape[0] // count
+            self.part = [parts[i * rows : (i + 1) * rows] for i in range(4)]
+            self.flying = [lax.ppermute(self.part[3], "col", IN)]
+            self.two = lax.ppermute(self.part[2], "col", IN)
+
+    def hop(self):
+        if self.count != 4:
+            return
+        if self.step == 0:
+            three = self.part[3] + self.flying[0]
+            self.flying = [lax.ppermute(three, "col", MID), self.two]
+        else:
+            one, two = self.part[1] + self.flying[0], self.part[2] + self.flying[1]
+            self.flying = [lax.ppermute(one, "col", PAIR), lax.ppermute(two, "col", MID)]
+        self.step += 1
+
+    def terms(self):
+        if self.count != 4:
+            mine = lax.psum_scatter(self.parts, "col", scatter_dimension=0, tiled=True)
+            return (mine, jnp.zeros_like(mine), jnp.zeros_like(mine))
+        return (self.part[0], *self.flying)
+
+
+def sync(moving, *values):
+    flat = [x for m in moving for x in m.flying] + list(values)
+    flat = list(lax.optimization_barrier(tuple(flat)))
+    for m in moving:
+        count = len(m.flying)
+        m.flying, flat = flat[:count], flat[count:]
+    return flat[0] if len(flat) == 1 else flat
 
 
 def params(mib, axes=1):
@@ -67,8 +113,15 @@
     )
 
 
+SHARE = 8
+
+
 def cost(flops, moved, trans=0):
-    return pl.CostEstimate(flops=int(flops), bytes_accessed=int(moved), transcendentals=int(trans))
+    return pl.CostEstimate(
+        flops=int(flops / SHARE),
+        bytes_accessed=int(moved / SHARE),
+        transcendentals=int(trans / SHARE),
+    )
 
 
 def stats_of(value):
@@ -557,9 +610,10 @@
     return out
 
 
-def grad_quarters(quarters, tokens, others, adds, rows_first):
+def grad_quarters(quarters, tokens, others, adds, rows_first, first=0, count=None):
     rows, width = tokens.shape
-    count, unused, units = others.shape
+    units = others.shape[2]
+    count = others.shape[0] if count is None else count
     quarter = width // 4
     k = quarters.shape[0]
     form = (quarter, units) if rows_first else (units, quarter)
@@ -572,8 +626,8 @@
             total += ref[0, 0].astype(F32)
         refs[-1][0, 0] = total.astype(BF16)
 
-    def shifted(start):
-        return pl.BlockSpec((1, 1, *form), lambda i, j, q: (i + start, j, 0, 0))
+    def shifted(at_k, at_n):
+        return pl.BlockSpec((1, 1, *form), lambda i, j, q: (i + at_k, j + at_n, 0, 0))
 
     return pl.pallas_call(
         body,
@@ -582,10 +636,10 @@
             grid=(k, count),
             in_specs=[
                 pl.BlockSpec((rows, quarter), lambda i, j, q: (0, q[i])),
-                pl.BlockSpec((1, rows, units), lambda i, j, q: (j, 0, 0)),
+                pl.BlockSpec((1, rows, units), lambda i, j, q: (j + first, 0, 0)),
             ]
-            + [shifted(start) for unused, start in adds],
-            out_specs=shifted(0),
+            + [shifted(at_k, at_n) for unused, at_k, at_n in adds],
+            out_specs=shifted(0, 0),
         ),
         out_shape=jax.ShapeDtypeStruct((k, count, *form), BF16),
         compiler_params=params(48, 2),
@@ -594,7 +648,47 @@
             2 * k * count * quarter * units * (1 + len(adds)) + 2 * rows * (width + count * units),
         ),
         name="grad_quarters",
-    )(quarters, tokens, others, *[array for array, unused in adds])
+    )(quarters, tokens, others, *[add[0] for add in adds])
+
+
+def join_pairs(core, parts, rests):
+    rows, units = parts[0].shape[1:]
+    block = 128 if rows % 128 == 0 else rows
+    steps = rows // block
+
+    def body(core_ref, *refs):
+        half = pl.program_id(0)
+        out_ref = refs[-1]
+        for i in range(2):
+
+            @pl.when(half == core_ref[0])
+            def _():
+                out_ref[:, i, :] = refs[i][0].astype(F32)
+
+            @pl.when(half != core_ref[0])
+            def _():
+                out_ref[:, i, :] = refs[2 + i][0].astype(F32)
+
+    def spec(same):
+        def at(h, j, c):
+            wanted = (h == c[0]) if same else (h != c[0])
+            return (0, jnp.where(wanted, j, 0), 0)
+
+        return pl.BlockSpec((1, block, units), at)
+
+    return pl.pallas_call(
+        body,
+        grid_spec=pltpu.PrefetchScalarGridSpec(
+            num_scalar_prefetch=1,
+            grid=(2, steps),
+            in_specs=[spec(True), spec(True), spec(False), spec(False)],
+            out_specs=pl.BlockSpec((block, 2, units), lambda h, j, c: (h * steps + j, 0, 0)),
+        ),
+        out_shape=jax.ShapeDtypeStruct((2 * rows, 2, units), F32),
+        compiler_params=params(40, 2),
+        cost_estimate=cost(rows * units, 24 * rows * units),
+        name="join_pairs",
+    )(core, *parts, *rests)
 
 
 def rotary_table(position):
@@ -672,9 +766,6 @@
         bottom = jnp.where(row == 0, b, a)
         return jnp.concatenate([top, bottom], axis=0)
 
-    def after(x, *others):
-        return lax.optimization_barrier((x, *others))[0]
-
     order = slot_order(place, slots)
     table_of = jnp.concatenate([core[None], order]).astype(jnp.int32)
     inside = jnp.arange(half_rows)
@@ -686,7 +777,6 @@
     vectors = jnp.concatenate([first_gain, first_shift, second_gain, second_shift], axis=0)
     vectors = order_features(vectors, swap(vectors, "row"))
     gain_a, shift_a, gain_b, shift_b = (vectors[i : i + 1] for i in range(4))
-    cot = to_sequence(cotangent)
 
     def part_of(w, axis):
         part = w.shape[axis] // 2
@@ -695,97 +785,145 @@
     w_in = jnp.transpose(project_in[0], (1, 0, 2))
     w_out, w_down = project_out[0], down_weight[0]
     w_gate = jnp.transpose(gate_weight[0], (1, 0, 2))
+    fixed = 0 * core
+
+    def quarters(*q):
+        return jnp.stack(q).astype(jnp.int32)
+
+    def for_core(tokens, others, rows_first, **span):
+        return grad_quarters(quarters(1 - core, 3 + fixed), tokens, others, (), rows_first, **span)
+
+    def for_row(tokens, others, rows_first, got, at=0, **span):
+        return grad_quarters(
+            quarters(2 + fixed), tokens, others, ((got, 1, at),), rows_first, **span
+        )
+
+    def for_y(tokens, others, rows_first, got, arrived, at=0, **span):
+        adds = ((got, 0, at), (arrived, 0, 0))
+        return grad_quarters(quarters(core), tokens, others, adds, rows_first, **span)[0]
+
+    def y_swap(own):
+        return swap(own, "y") if y_count == 2 else lax.psum(own, "y")
+
+    def y_total(own, other):
+        return (own.astype(F32) + other.astype(F32)).astype(BF16) if y_count == 2 else other
+
+    def join(total, rest, axis):
+        return jnp.concatenate(
+            [jnp.where(core == 0, total, rest), jnp.where(core == 0, rest, total)], axis=axis
+        ).astype(F32)
+
     low_a = norm_first(stream, gain_a, shift_a)
-    in_half = swap(after(part_of(w_in, 1), stream, cot), "row")
-
-    tokens_a = gather_slots(low_a, slots)
-    tokens_a, in_half, w_gate = lax.optimization_barrier((tokens_a, in_half, w_gate))
+    in_half = swap(after(part_of(w_in, 1), stream), "row")
+    cot = to_sequence(after(cotangent, low_a))
+    hops = Gather(low_a, slots)
+    rotary_mine = sync([hops], rotary_mine)
+    hops.hop()
+    rotary_other = sync([hops], rotary_other)
+    hops.hop()
+    out_half = swap(after(part_of(w_out, 1), rotary_other), "row")
+    w_gate, gate_part, in_half, cot = sync([hops], w_gate, part_of(w_gate, 1), in_half, cot)
+    tokens_a = hops.rows()
     pieces_in = (w_in, in_half, swap(in_half, "core"))
-    out_half = swap(after(part_of(w_out, 1), in_half), "row")
-    down_half = swap(after(part_of(w_down, 1), in_half), "row")
-    cot_rows = gather_slots(after(cot, tokens_a), slots)
+    cot_hops = Gather(cot, slots)
+    down_half = swap(after(part_of(w_down, 1), cot), "row")
     bias = project_bias[0][:, None, :]
     qkv_other = qkv_columns(tokens_a, pieces_in, bias, rotary_mine, (1 - core)[None])
     qkv_from = swap(qkv_other, "core")
     qkv_mine = qkv_columns(tokens_a, pieces_in, bias, rotary_mine, core[None])
-    gate_half = swap(after(part_of(w_gate, 1), qkv_mine), "row")
-    out_half = after(out_half, qkv_mine)
+    out_mine, out_other, lse = attend(qkv_mine, qkv_from, table_of, factor)
+    out_mine, out_other, out_half = sync([cot_hops], out_mine, out_other, out_half)
+    cot_hops.hop()
     pieces_out = (w_out, out_half, swap(out_half, "core"))
-    out_mine, out_other, lse = attend(qkv_mine, qkv_from, table_of, factor)
     out_from = swap(out_other, "core")
     attended = jnp.concatenate(
         [jnp.where(core == 0, out_mine, out_from), jnp.where(core == 0, out_from, out_mine)], axis=1
     )
     part_out = to_features(attended[None], [p[None] for p in pieces_out], False)
-    terms = scatter_slots(part_out, slots)
-    residual, low_b = norm_second(stream, terms, gain_b, shift_b)
-
-    tokens_b = gather_slots(low_b, slots)
-    down_half, grad_rows = lax.optimization_barrier((down_half, cot_rows, low_b))[:2]
-    pieces_down = (w_down, down_half, swap(down_half, "core"))
+    part_out, gate_part = sync([cot_hops], part_out, gate_part)
+    hops = Scatter(part_out, slots)
+    cot_hops.hop()
+    gate_half = swap(gate_part, "row")
+    down_half = sync([hops, cot_hops], down_half)
+    hops.hop()
+    down_rest = sync([hops], swap(down_half, "core"))
+    hops.hop()
+    pieces_down = (w_down, down_half, down_rest)
     units = w_down.shape[0]
     ways = 2 if units % 32 == 0 else 1
+    grad_rows = cot_hops.rows()
     hidden_grad = from_features(
         jnp.arange(ways, dtype=jnp.int32), grad_rows, pieces_down, units // ways
     )
     hidden_grad = jnp.concatenate([hidden_grad[i] for i in range(ways)], axis=1)
-    tokens_b, gate_half, hidden_grad = lax.optimization_barrier((tokens_b, gate_half, hidden_grad))
-    pieces_gate = (w_gate, gate_half, swap(gate_half, "core"))
-    hidden, gate_up_grad = feed_forward(tokens_b, pieces_gate, hidden_grad)
-    part_b = to_features(gate_up_grad, pieces_gate, True)
-    terms = scatter_slots(part_b, slots)
-    g2_low, sums_b, g2 = norm_back(residual, terms, cot, gain_b, 1)
-
-    def quarters(*q):
-        return jnp.stack(q).astype(jnp.int32)
-
-    def to_core(tokens, others, rows_first):
-        sent = grad_quarters(quarters(1 - core, 3 + 0 * core), tokens, others, (), rows_first)
-        return swap(sent, "core")
-
-    def to_row(tokens, others, rows_first, got):
-        oth = grad_quarters(quarters(2 + 0 * core), tokens, others, ((got, 1),), rows_first)
-        return oth
-
-    def to_y(tokens, others, rows_first, got, arrived):
-        own = grad_quarters(
-            quarters(core), tokens, others, ((got, 0), (arrived, 0)), rows_first
-        )[0]
-        return own
-
-    def finish(own, behind, rows_first):
-        if y_count == 2:
-            other = after(swap(own, "y"), behind)
-            total = (own.astype(F32) + other.astype(F32)).astype(BF16)
-        else:
-            total = lax.psum(own, "y")
-        rest = swap(total, "core")
-        return jnp.concatenate(
-            [jnp.where(core == 0, total, rest), jnp.where(core == 0, rest, total)],
-            axis=1 if rows_first else 2,
-        ).astype(F32)
-
-    gate_got = to_core(tokens_b, gate_up_grad, True)
-    down_got = to_core(grad_rows, hidden[None], False)
-    down_oth = to_row(grad_rows, hidden[None], False, down_got)
-    gate_oth = to_row(tokens_b, gate_up_grad, True, gate_got)
+    grad_rows, hidden_grad = sync([hops], grad_rows, hidden_grad)
+    residual, low_b = norm_second(stream, hops.terms(), gain_b, shift_b)
+
+    hops = Gather(low_b, slots)
+    sync([hops], low_b)
+    hops.hop()
+    gate_half = sync([hops], gate_half)
+    hops.hop()
+    gate_half, gate_rest = sync([hops], gate_half, swap(gate_half, "core"))
+    tokens_b = hops.rows()
+    pieces_gate = (w_gate, gate_half, gate_rest)
+    hidden, pair = feed_forward(tokens_b, pieces_gate, hidden_grad)
+    part_b = to_features(pair, pieces_gate, True)
+    part_b, hidden, pair = sync([], part_b, hidden, pair)
+
+    hops = Scatter(part_b, slots)
+    down_got = swap(for_core(grad_rows, hidden[None], False), "core")
+    gate_sent = for_core(tokens_b, pair, True)
+    down_got, gate_sent = sync([hops], down_got, gate_sent)
+    hops.hop()
+    gate_got = swap(gate_sent, "core")
+    down_oth = for_row(grad_rows, hidden[None], False, down_got)
+    down_oth, gate_got = sync([hops], down_oth, gate_got)
+    hops.hop()
     down_arrived = swap(down_oth, "row")
-    gate_arrived = swap(after(gate_oth, down_oth), "row")
-
-    g2_low = after(g2_low, gate_oth, down_oth)
-    g2_rows = gather_slots(g2_low, slots)
-    down_own = to_y(grad_rows, hidden[None], False, down_got, after(down_arrived, g2_rows))
+    gate_oth = [
+        for_row(tokens_b, pair, True, gate_got, at=i, first=i, count=1) for i in range(2)
+    ]
+    gate_oth = list(sync([hops], *gate_oth))
+    g2_low, sums_b, g2 = norm_back(residual, hops.terms(), cot, gain_b, 1)
+
+    hops = Gather(g2_low, slots)
+    gate_arrived = [swap(gate_oth[0], "row"), None]
+    part_down = to_features(hidden[None], [p[None] for p in pieces_down], False)
+    part_down, down_arrived = sync([hops], part_down, down_arrived)
+    hops.hop()
+    down_own = for_y(grad_rows, hidden[None], False, down_got, down_arrived)
+    down_own, part_down = sync([hops], down_own, part_down)
+    hops.hop()
+    down_other = y_swap(down_own)
+    gate_arrived[0], gate_oth[1] = sync([hops], gate_arrived[0], gate_oth[1])
+    gate_arrived[1] = swap(gate_oth[1], "row")
+    g2_rows = hops.rows()
     columns = w_out.shape[0] // 2
     grad_other = from_features((1 - core)[None], g2_rows, pieces_out, columns)[0]
     grad_from = swap(grad_other, "core")
     grad_mine = from_features(core[None], g2_rows, pieces_out, columns)[0]
-    part_down = to_features(after(hidden, g2_rows)[None], [p[None] for p in pieces_down], False)
-    terms_down = scatter_slots(part_down, slots)
-    out_got = to_core(g2_rows, attended[None], False)
+    gate_own = [
+        for_y(tokens_b, pair, True, gate_got, gate_arrived[0], at=0, first=0, count=1),
+        None,
+    ]
+    out_sent = for_core(g2_rows, attended[None], False)
+    grad_from, grad_mine, out_sent, gate_own[0], part_down, down_other = sync(
+        [], grad_from, grad_mine, out_sent, gate_own[0], part_down, down_other
+    )
+    down_hops = Scatter(part_down, slots)
+    gate_other = [y_swap(gate_own[0]), None]
+    out_got = swap(out_sent, "core")
     mixed_mine, mixed_other, bias_part = attend_back(
         qkv_mine, qkv_from, grad_mine, grad_from, lse, rotary_mine, rotary_other, table_of, factor
     )
+    mixed_mine, mixed_other, out_got, gate_arrived[1] = sync(
+        [down_hops], mixed_mine, mixed_other, out_got, gate_arrived[1]
+    )
+    down_hops.hop()
     mixed_from = swap(mixed_other, "core")
+    out_oth = for_row(g2_rows, attended[None], False, out_got)
+    gate_own[1] = for_y(tokens_b, pair, True, gate_got, gate_arrived[1], at=1, first=1, count=1)
     mixed = jnp.concatenate(
         [
             jnp.where(core == 0, mixed_mine, mixed_from),
@@ -793,24 +931,58 @@
         ],
         axis=2,
     )
+    in_sent = for_core(tokens_a, mixed, True)
+    in_sent, mixed, gate_own[1], gate_other[0], out_oth = sync(
+        [], in_sent, mixed, gate_own[1], gate_other[0], out_oth
+    )
+    in_got = swap(in_sent, "core")
+    out_arrived = swap(out_oth, "row")
+    gate_other[1] = y_swap(gate_own[1])
     part_a = to_features(mixed, pieces_in, True)
-    terms = scatter_slots(part_a, slots)
-    in_got = to_core(tokens_a, mixed, True)
-    gate_own = to_y(tokens_b, gate_up_grad, True, gate_got, after(gate_arrived, part_a))
-    out_oth = to_row(g2_rows, attended[None], False, after(out_got, part_a))
-    out_arrived = swap(out_oth, "row")
-    in_oth = to_row(tokens_a, mixed, True, in_got)
-    in_arrived = swap(after(in_oth, out_oth), "row")
-    out_own = to_y(g2_rows, attended[None], False, out_got, out_arrived)
-    in_own = to_y(tokens_a, mixed, True, in_got, in_arrived)
-    input_low, sums_a = norm_back(stream, terms, g2, gain_a, 0)
-    layer_low = (residual + sum(t.astype(F32) for t in terms_down)).astype(BF16)
-    layer_out = from_sequence(after(layer_low, part_a))
-    input_grad = from_sequence(input_low).astype(F32)
-    down_grad = finish(down_own, part_a, False)[0]
-    gate_grad = finish(gate_own, part_a, True)
-    out_grad = finish(out_own, part_a, False)[0]
-    in_grad = finish(in_own, part_a, True)
+    part_a, in_got, out_arrived = sync([down_hops], part_a, in_got, out_arrived)
+    hops = Scatter(part_a, slots)
+    spans = (dict(at=0, first=0, count=2), dict(at=2, first=2, count=1))
+    in_oth = [for_row(tokens_a, mixed, True, in_got, **span) for span in spans]
+    in_arrived = [swap(x, "row") for x in in_oth]
+    out_own = for_y(g2_rows, attended[None], False, out_got, out_arrived)
+    *in_oth, out_own = sync([hops], *in_oth, out_own)
+    hops.hop()
+    down_total = y_total(down_own, down_other)
+    gate_total = [y_total(gate_own[0], gate_other[0]), None]
+    in_arrived[0], gate_other[1], down_total, gate_total[0] = sync(
+        [hops], in_arrived[0], gate_other[1], down_total, gate_total[0]
+    )
+    hops.hop()
+    out_other_y = y_swap(out_own)
+    in_own = [for_y(tokens_a, mixed, True, in_got, in_arrived[0], **spans[0])]
+    gate_total[1] = y_total(gate_own[1], gate_other[1])
+    in_own[0], gate_total[1], in_arrived[1], out_other_y = sync(
+        [hops], in_own[0], gate_total[1], in_arrived[1], out_other_y
+    )
+    in_other = [y_swap(in_own[0])]
+    input_low, sums_a = norm_back(stream, hops.terms(), g2, gain_a, 0)
+    down_rest = swap(down_total, "core")
+    gate_rest = [swap(x, "core") for x in gate_total]
+    in_own.append(for_y(tokens_a, mixed, True, in_got, in_arrived[1], **spans[1]))
+    input_low, sums_a, in_own[1], down_rest, *gate_rest = sync(
+        [], input_low, sums_a, in_own[1], down_rest, *gate_rest
+    )
+    input_grad = from_sequence(input_low)
+    in_other.append(y_swap(in_own[1]))
+    out_total = y_total(out_own, out_other_y)
+    out_rest = swap(out_total, "core")
+    gate_grad = join_pairs(core[None], gate_total, gate_rest)
+    gate_grad, out_rest, input_grad = sync([], gate_grad, out_rest, input_grad)
+
+    input_grad = input_grad.astype(F32)
+    down_grad = join(down_total, down_rest, 2)[0]
+    out_grad = join(out_total, out_rest, 2)[0]
+    down_hops.flying = list(tie(down_hops.flying, input_grad)) if slots == 4 else []
+    down_hops.hop()
+    layer_low = (residual + sum(t.astype(F32) for t in down_hops.terms())).astype(BF16)
+    layer_out = from_sequence(layer_low)
+    in_total = [y_total(x, o) for x, o in zip(in_own, in_other)]
+    in_grad = jnp.concatenate([join(x, swap(x, "core"), 1) for x in in_total], axis=0)
 
     def reduce_vector(own, oth, same):
         total = jnp.concatenate([own, same, oth], axis=0)
@@ -831,7 +1003,7 @@
     bias_all = lax.dynamic_update_slice(
         bias_all, bias_part[:, 0, :], (jnp.int32(0), (place * 2 + core) * columns)
     ).reshape(-1, wide)
-    sums = jnp.concatenate([sums_a, sums_b], axis=0)
+    sums = after(jnp.concatenate([sums_a, sums_b], axis=0), in_own[1])
     vectors = reduce_vector(sums[:, :wide], natural(sums[:, wide:]), bias_all)
     bias_grad = take(vectors[4:].reshape(3, -1), place * 2 * columns, 2 * columns, 1)
     return (
@@ -844,7 +1016,7 @@
         out_grad[None],
         vectors[2:3],
         vectors[3:4],
-        jnp.transpose(gate_grad, (1, 0, 2))[None],
+        gate_grad[None],
         down_grad[None],
     )
 

time: 663 us -> 573 us (0.86)
  waiting for transfers between devices: 287 us -> 203 us
  starting transfers between devices: 141 us -> 118 us
  Pallas kernels: 134 us -> 150 us
    ppermute x32 -> x38, waiting for transfers between devices: 120 us -> 69.8 us  [swap(): return lax.ppermute(x, axis, [(0, 1), (1, 0)])]
    ppermute x40, waiting for transfers between devices: 157 us -> 110 us  [the longest x8 25.3 us: hop(): self.flying = [lax.ppermute(one, 'col', MID), lax.ppermute(mid, 'col', OUT)]]
    ppermute x40, starting transfers between devices: 105 us -> 71.4 us  [the longest x4 21.2 us: __init__(): self.two = lax.ppermute(self.part[2], 'col', IN)]
    pallas_call x0 -> x1, Pallas kernels: none -> 9.43 us  [join_pairs(): pl.pallas_call(body, grid_spec=pltpu.PrefetchScalarGridSpec(num_scalar_pr...]
    ppermute x32 -> x38, starting transfers between devices: 21.7 us -> 28.8 us  [swap(): return lax.ppermute(x, axis, [(0, 1), (1, 0)])]
    convert_element_type x8 -> x10, other arithmetic: 15.8 us -> 21.1 us  [the longest x6 13.6 us: y_total(): (own.astype(F32) + other.astype(F32)).astype(BF16)]
    pallas_call x12 -> x16, Pallas kernels: 42.5 us -> 46.9 us  [grad_quarters(): pl.pallas_call(body, grid_spec=pltpu.PrefetchScalarGridSpec(num_scalar_pr...]
    unnamed x108 -> x129, local copies, waits for them, and re-layouts: 21.6 us -> 22 us
  transfers between devices with their start and end apart: 83 -> 89, of which waited for: 30 -> 37; matrix products, arithmetic and copies ran while one was open for 11% -> 12% of each run, Pallas kernels for 16% -> 20%
where the time goes in v3:
time: 573 us; the launch traced here: 563 us
  waiting for transfers between devices  203 us (35%)
  Pallas kernels  150 us (26%)
  starting transfers between devices  118 us (21%)
  other arithmetic  52.4 us (9%)
  local copies, waits for them, and re-layouts  37.7 us (7%)
    ppermute x38, waiting for transfers between devices, swap(): return lax.ppermute(x, axis, [(0, 1), (1, 0)])  69.8 us
    pallas_call x16, Pallas kernels, grad_quarters(): pl.pallas_call(body, grid_spec=pltpu.PrefetchScalarGridSpec(num_scalar_pr...  46.9 us
    pallas_call x4, Pallas kernels, to_features(): pl.pallas_call(body, grid=(width // block,), in_specs=[pl.BlockSpec((coun...  33.3 us
    ppermute x38, starting transfers between devices, swap(): return lax.ppermute(x, axis, [(0, 1), (1, 0)])  28.8 us
    ppermute x8, waiting for transfers between devices, hop(): self.flying = [lax.ppermute(one, 'col', MID), lax.ppermute(mid, 'col', OUT)]  25.3 us
    unnamed x129, local copies, waits for them, and re-layouts  22 us
    ppermute x4, starting transfers between devices, __init__(): self.two = lax.ppermute(self.part[2], 'col', IN)  21.2 us
    ppermute x4, waiting for transfers between devices, __init__(): self.two = lax.ppermute(self.part[2], 'col', IN)  20.3 us
  transfers between devices with their start and end apart: 89, of which 37 were waited for; matrix products, arithmetic and copies ran while one was open for 12% of the time, Pallas kernels for 20%

profile of v3, /device:TPU:0, one launch (start us, length us, event | category | flops | bytes accessed | tf_op | source)
XLA Modules:
  0.0 563.2 jit_solution(3092707791480517120)
XLA Ops:
  36.9 5.9 %copy.29 = bf16[1,1024,2,1408]{3,1,2,0:T(8,128)(2,1)} copy(bf16[1,1024,2,1408]{3,2,1,0:T(2,128)(2,1)} %param.20) | data formatting | bytes 11534336 | tf_op args[8]
  51.8 12.0 %collective-permute-done.10 = bf16[128,1024]{1,0:T(8,128)(2,1)S(1)} collective-permute-done((bf16[128,1024]{1,0:T(8,128)(2,1)S(1)}, bf16[128,1024]{1,0:T(8,128)(2,1)S(1)}, u32[]{:S(2)}, u32[]{:S(2)}) %collective-permute-start.10) | collective-permute-done | bytes 262176 | tf_op jit(solution)/shard_map/ppermute | solution.py:756
  87.2 9.9 %attend.1 = (bf16[512,256]{1,0:T(8,128)(2,1)S(1)}, bf16[512,256]{1,0:T(8,128)(2,1)S(1)}, f32[2,1024,2]{2,1,0:T(8,128)S(1)}) custom-call(s32[5]{0:T(128)S(1)} %pad_add_fusion.order_ref, bf16[3,512,256]{2,1,0:T(8,128)(2,1)S(1)} %qkv_columns.2.mine_ref, bf16[3,512,256]{2,1,0:T(8,128)(2,1)S(1)} %collective-permute-done.14.other_ref), custom_call_target="tpu_custom_call" | custom-call | flops 134217728 | bytes 262144 | tf_op jit(solution)/shard_map/attend/pallas_call | solution.py:347
  107.0 9.7 %collective-permute-done.17 = bf16[128,2048]{1,0:T(8,128)(2,1)} collective-permute-done((bf16[128,2048]{1,0:T(8,128)(2,1)}, bf16[128,2048]{1,0:T(8,128)(2,1)}, u32[]{:S(2)}, u32[]{:S(2)}) %collective-permute-start.17) | collective-permute-done | bytes 524320 | tf_op jit(solution)/shard_map/ppermute | solution.py:60
  121.7 8.2 %collective-permute-done.20 = bf16[128,2048]{1,0:T(8,128)(2,1)S(1)} collective-permute-done((bf16[128,2048]{1,0:T(8,128)(2,1)S(1)}, bf16[128,2048]{1,0:T(8,128)(2,1)S(1)}, u32[]{:S(2)}, u32[]{:S(2)}) %collective-permute-start.20) | collective-permute-done | bytes 524320 | tf_op jit(solution)/shard_map/ppermute | solution.py:80
  144.9 8.3 %collective-permute-done.24 = bf16[128,2048]{1,0:T(8,128)(2,1)S(1)} collective-permute-done((bf16[128,2048]{1,0:T(8,128)(2,1)S(1)}, bf16[128,2048]{1,0:T(8,128)(2,1)S(1)}, u32[]{:S(2)}, u32[]{:S(2)}) %collective-permute-start.24) | collective-permute-done | bytes 524320 | tf_op jit(solution)/shard_map/ppermute | solution.py:81
  172.7 9.6 %collective-permute-done.28 = bf16[128,2048]{1,0:T(8,128)(2,1)S(1)} collective-permute-done((bf16[128,2048]{1,0:T(8,128)(2,1)S(1)}, bf16[128,2048]{1,0:T(8,128)(2,1)S(1)}, u32[]{:S(2)}, u32[]{:S(2)}) %collective-permute-start.28) | collective-permute-done | bytes 524320 | tf_op jit(solution)/shard_map/ppermute | solution.py:52
  184.2 15.2 %collective-permute-done.32.refs_1_ = bf16[2,512,1408]{2,1,0:T(8,128)(2,1)S(1)} collective-permute-done((bf16[2,512,1408]{2,1,0:T(8,128)(2,1)}, bf16[2,512,1408]{2,1,0:T(8,128)(2,1)S(1)}, u32[]{:S(2)}, u32[]{:S(2)}) %collective-permute-start.32) | collective-permute-done | bytes 2883616 | tf_op jit(solution)/shard_map/ppermute | solution.py:23
  201.4 14.3 %collective-permute-done.33 = bf16[128,2048]{1,0:T(8,128)(2,1)S(1)} collective-permute-done((bf16[128,2048]{1,0:T(8,128)(2,1)S(1)}, bf16[128,2048]{1,0:T(8,128)(2,1)S(1)}, u32[]{:S(2)}, u32[]{:S(2)}) %collective-permute-start.33) | collective-permute-done | bytes 524320 | tf_op jit(solution)/shard_map/ppermute | solution.py:64
  217.3 13.9 %feed_forward.1 = (bf16[512,1408]{1,0:T(8,128)(2,1)S(1)}, bf16[2,512,1408]{2,1,0:T(8,128)(2,1)}) custom-call(bf16[512,2048]{1,0:T(8,128)(2,1)S(1)} %pad_maximum_fusion.2.x_ref, bf16[2,1024,1408]{2,1,0:T(8,128)(2,1)} %bitcast.87, bf16[2,512,1408]{2,1,0:T(8,128)(2,1)} %copy-done.58, bf16[2,512,1408]{2,1,0:T(8,128)(2,1)} %copy-done.59, ...), custom_call_target="tpu_custom_call" | custom-call | flops 738197504 | bytes 1703936 | tf_op jit(solution)/shard_map/feed_forward/pallas_call | solution.py:516
  231.2 13.1 %to_features.5 = bf16[512,2048]{1,0:T(8,128)(2,1)} custom-call(bf16[2,512,1408]{2,1,0:T(8,128)(2,1)} %get-tuple-element.190.v_ref.y_ref, bf16[2,1024,1408]{2,1,0:T(8,128)(2,1)} %bitcast.88, bf16[2,512,1408]{2,1,0:T(8,128)(2,1)} %copy-done.58, bf16[2,512,1408]{2,1,0:T(8,128)(2,1)} %copy-done.59), custom_call_target="tpu_custom_call" | custom-call | flops 738197504 | bytes 2064384 | tf_op jit(solution)/shard_map/to_features/pallas_call | solution.py:566
  252.3 5.9 %grad_quarters.17 = bf16[2,2,512,1408]{3,2,1,0:T(8,128)(2,1)} custom-call(s32[2]{0:T(128)S(1)} %pad_add_fusion.1.q_ref, bf16[512,2048]{1,0:T(8,128)(2,1)S(1)} %copy-done.2, bf16[2,512,1408]{2,1,0:T(8,128)(2,1)S(1)} %copy-done), custom_call_target="tpu_custom_call" | custom-call | flops 369098752 | bytes 1343488 | tf_op jit(solution)/shard_map/grad_quarters/pallas_call | solution.py:632
  258.3 6.0 %collective-permute-done.35 = bf16[128,2048]{1,0:T(8,128)(2,1)S(1)} collective-permute-done((bf16[128,2048]{1,0:T(8,128)(2,1)S(1)}, bf16[128,2048]{1,0:T(8,128)(2,1)S(1)}, u32[]{:S(2)}, u32[]{:S(2)}) %collective-permute-start.35) | collective-permute-done | bytes 524320 | tf_op jit(solution)/shard_map/ppermute | solution.py:80
  265.1 6.8 %collective-permute-start.38 = (bf16[128,2048]{1,0:T(8,128)(2,1)S(1)}, bf16[128,2048]{1,0:T(8,128)(2,1)S(1)}, u32[]{:S(2)}, u32[]{:S(2)}) collective-permute-start(bf16[128,2048]{1,0:T(8,128)(2,1)S(1)} %get-tuple-element.285), channel_id=1, source_target_pairs={{0,1},{3,2},{4,5},{7,6},{8,9},{11,10},{12,13},{15,14},{16,17},{19,... | collective-permute-start | bytes 1572872 | tf_op jit(solution)/shard_map/ppermute | solution.py:81
  275.4 8.1 %collective-permute-done.38 = bf16[128,2048]{1,0:T(8,128)(2,1)S(1)} collective-permute-done((bf16[128,2048]{1,0:T(8,128)(2,1)S(1)}, bf16[128,2048]{1,0:T(8,128)(2,1)S(1)}, u32[]{:S(2)}, u32[]{:S(2)}) %collective-permute-start.38) | collective-permute-done | bytes 524320 | tf_op jit(solution)/shard_map/ppermute | solution.py:81
  307.2 7.8 %to_features.6 = bf16[512,2048]{1,0:T(8,128)(2,1)} custom-call(bf16[1,512,1408]{2,1,0:T(8,128)(2,1)} %bitcast.69, bf16[1,1408,1024]{2,1,0:T(8,128)(2,1)} %refs_0_.3, bf16[1,1408,512]{2,1,0:T(8,128)(2,1)} %bitcast.24.refs_1_, bf16[1,1408,512]{2,1,0:T(8,128)(2,1)} %bitcast.74), custom_call_target="tpu_custom_call" | custom-call | flops 369098752 | bytes 1163264 | tf_op jit(solution)/shard_map/to_features/pallas_call | solution.py:566
  322.9 10.7 %collective-permute-done.46 = bf16[128,2048]{1,0:T(8,128)(2,1)S(1)} collective-permute-done((bf16[128,2048]{1,0:T(8,128)(2,1)S(1)}, bf16[128,2048]{1,0:T(8,128)(2,1)S(1)}, u32[]{:S(2)}, u32[]{:S(2)}) %collective-permute-start.46) | collective-permute-done | bytes 524320 | tf_op jit(solution)/shard_map/ppermute | solution.py:60
  336.6 10.9 %collective-permute-done.48.refs_1_ = bf16[1,1,512,1408]{3,2,1,0:T(8,128)(2,1)} collective-permute-done((bf16[1,1,512,1408]{3,2,1,0:T(8,128)(2,1)S(1)}, bf16[1,1,512,1408]{3,2,1,0:T(8,128)(2,1)}, u32[]{:S(2)}, u32[]{:S(2)}) %collective-permute-start.48) | collective-permute-done | bytes 1441824 | tf_op jit(solution)/shard_map/ppermute | solution.py:23
  368.1 16.1 %attend_back.1 = (bf16[3,512,256]{2,1,0:T(8,128)(2,1)S(1)}, bf16[3,512,256]{2,1,0:T(8,128)(2,1)}, f32[3,1,256]{2,1,0:T(1,128)S(1)}) custom-call(s32[5]{0:T(128)S(1)} %pad_add_fusion.order_ref, bf16[3,512,256]{2,1,0:T(8,128)(2,1)} %copy-done.22, bf16[3,512,256]{2,1,0:T(8,128)(2,1)} %copy-done.37, bf16[512,256]{1,0:T(8,128)(2,1)S(1)} %bitcast.83, ...), custom_call_target="tpu_custom_call" | custom-call | flops 335544320 | bytes 655360 | tf_op jit(solution)/shard_map/attend_back/pallas_call | solution.py:457
  409.9 7.8 %to_features.7 = bf16[512,2048]{1,0:T(8,128)(2,1)} custom-call(bf16[3,512,512]{2,1,0:T(8,128)(2,1)} %copy-done.4, bf16[3,1024,512]{2,1,0:T(8,128)(2,1)} %bitcast.64, bf16[3,512,512]{2,1,0:T(8,128)(2,1)} %copy-done.14, bf16[3,512,512]{2,1,0:T(8,128)(2,1)} %copy-done.15), custom_call_target="tpu_custom_call" | custom-call | flops 402653184 | bytes 1245184 | tf_op jit(solution)/shard_map/to_features/pallas_call | solution.py:566
  436.3 6.7 %collective-permute-start.62 = (bf16[128,2048]{1,0:T(8,128)(2,1)S(1)}, bf16[128,2048]{1,0:T(8,128)(2,1)S(1)}, u32[]{:S(2)}, u32[]{:S(2)}) collective-permute-start(bf16[128,2048]{1,0:T(8,128)(2,1)S(1)} %get-tuple-element.277), channel_id=1, source_target_pairs={{0,1},{3,2},{4,5},{7,6},{8,9},{11,10},{12,13},{15,14},{16,17},{19,... | collective-permute-start | bytes 1572872 | tf_op jit(solution)/shard_map/ppermute | solution.py:81
  480.8 15.1 %collective-permute-done.85 = bf16[2,512,512]{2,1,0:T(8,128)(2,1)} collective-permute-done((bf16[2,512,512]{2,1,0:T(8,128)(2,1)}, bf16[2,512,512]{2,1,0:T(8,128)(2,1)}, u32[]{:S(2)}, u32[]{:S(2)}) %collective-permute-start.85) | collective-permute-done | bytes 1048608 | tf_op jit(solution)/shard_map/ppermute | solution.py:23
  509.2 5.8 %collective-permute-done.81 = f32[14,1024]{1,0:T(8,128)S(1)} collective-permute-done((f32[14,1024]{1,0:T(8,128)S(1)}, f32[14,1024]{1,0:T(8,128)S(1)}, u32[]{:S(2)}, u32[]{:S(2)}) %collective-permute-start.81) | collective-permute-done | bytes 57376 | tf_op jit(solution)/shard_map/ppermute | solution.py:992
  518.5 9.4 %join_pairs.1 = f32[1024,2,1408]{2,1,0:T(2,128)} custom-call(s32[1]{0:T(128)} %bitcast.9.half_ref.q_ref.index_ref.core_ref, bf16[1,512,1408]{2,1,0:T(8,128)(2,1)} %add_convert_fusion.1.refs_0_, bf16[1,512,1408]{2,1,0:T(8,128)(2,1)} %add_convert_fusion.refs_1_, bf16[1,512,1408]{2,1,0:T(8,128)(2,1)} %collective-permute-done.70.refs_2_, ...), custom_call_target="tpu_custom_call" | custom-call | flops 90112 | bytes 2162688 | tf_op jit(solution)/shard_map/join_pairs/pallas_call | solution.py:679
  (419 shorter events, 323.4 us)
Async XLA Ops:
  25.4 38.8 %collective-permute-start.8 = (bf16[3,512,512]{2,1,0:T(8,128)(2,1)S(1)}, bf16[3,512,512]{2,1,0:T(8,128)(2,1)S(1)}, u32[]{:S(2)}, u32[]{:S(2)}) collective-permute-start(bf16[3,512,512]{2,1,0:T(8,128)(2,1)S(1)} %dynamic-slice_bitcast_fusion), channel_id=1, source_target_pairs={{0,4},{4,0},{1,5},{5,1},{2,6},{6,2},{3,7},{7,3},{8,12},{12,8},{9,1... | collective-permute-start | bytes 4718600 | tf_op jit(solution)/shard_map/ppermute | solution.py:23
  25.5 38.3 %collective-permute-start.10 = (bf16[128,1024]{1,0:T(8,128)(2,1)S(1)}, bf16[128,1024]{1,0:T(8,128)(2,1)S(1)}, u32[]{:S(2)}, u32[]{:S(2)}) collective-permute-start(bf16[128,1024]{1,0:T(8,128)(2,1)S(1)} %get-tuple-element.317), channel_id=1, source_target_pairs={{0,8},{4,0},{8,12},{12,4},{1,9},{5,1},{9,13},{13,5},{2,10},{6,2},{... | collective-permute-start | bytes 786440 | tf_op jit(solution)/shard_map/ppermute | solution.py:756
  26.2 37.6 %collective-permute-start.9 = (bf16[128,1024]{1,0:T(8,128)(2,1)S(1)}, bf16[128,1024]{1,0:T(8,128)(2,1)S(1)}, u32[]{:S(2)}, u32[]{:S(2)}) collective-permute-start(bf16[128,1024]{1,0:T(8,128)(2,1)S(1)} %get-tuple-element.316), channel_id=1, source_target_pairs={{0,0},{4,8},{8,4},{12,12},{1,1},{5,9},{9,5},{13,13},{2,2},{6,10},{... | collective-permute-start | bytes 786440 | tf_op jit(solution)/shard_map/ppermute | solution.py:755
  74.8 23.4 %collective-permute-start.15 = (bf16[512,512]{1,0:T(8,128)(2,1)}, bf16[512,512]{1,0:T(8,128)(2,1)S(1)}, u32[]{:S(2)}, u32[]{:S(2)}) collective-permute-start(bf16[512,512]{1,0:T(8,128)(2,1)} %dynamic-slice_bitcast_fusion.2), channel_id=1, source_target_pairs={{0,4},{4,0},{1,5},{5,1},{2,6},{6,2},{3,7},{7,3},{8,12},{12,8},{9,1... | collective-permute-start | bytes 1572872 | tf_op jit(solution)/shard_map/ppermute | solution.py:23
  78.1 20.1 %collective-permute-start.11 = (bf16[128,2048]{1,0:T(8,128)(2,1)S(1)}, bf16[128,2048]{1,0:T(8,128)(2,1)}, u32[]{:S(2)}, u32[]{:S(2)}) collective-permute-start(bf16[128,2048]{1,0:T(8,128)(2,1)S(1)} %pad_maximum_fusion.9.up_ref), channel_id=1, source_target_pairs={{0,1},{1,0},{2,3},{3,2},{4,5},{5,4},{6,7},{7,6},{8,9},{9,8},{10,11... | collective-permute-start | bytes 1572872 | tf_op jit(solution)/shard_map/ppermute | solution.py:52
  83.1 38.6 %collective-permute-start.22 = (bf16[1408,512]{1,0:T(8,128)(2,1)}, bf16[1408,512]{1,0:T(8,128)(2,1)}, u32[]{:S(2)}, u32[]{:S(2)}) collective-permute-start(bf16[1408,512]{1,0:T(8,128)(2,1)} %dynamic-slice_bitcast_fusion.1), channel_id=1, source_target_pairs={{0,4},{4,0},{1,5},{5,1},{2,6},{6,2},{3,7},{7,3},{8,12},{12,8},{9,1... | collective-permute-start | bytes 4325384 | tf_op jit(solution)/shard_map/ppermute | solution.py:23
  134.0 65.4 %collective-permute-start.32 = (bf16[2,512,1408]{2,1,0:T(8,128)(2,1)}, bf16[2,512,1408]{2,1,0:T(8,128)(2,1)S(1)}, u32[]{:S(2)}, u32[]{:S(2)}) collective-permute-start(bf16[2,512,1408]{2,1,0:T(8,128)(2,1)} %bitcast.90), channel_id=1, source_target_pairs={{0,4},{4,0},{1,5},{5,1},{2,6},{6,2},{3,7},{7,3},{8,12},{12,8},{9,1... | collective-permute-start | bytes 8650760 | tf_op jit(solution)/shard_map/ppermute | solution.py:23
  283.4 34.7 %collective-permute-start.44 = (bf16[1,1,1408,512]{3,2,1,0:T(8,128)(2,1)}, bf16[1,1,1408,512]{3,2,1,0:T(8,128)(2,1)S(1)}, u32[]{:S(2)}, u32[]{:S(2)}) collective-permute-start(bf16[1,1,1408,512]{3,2,1,0:T(8,128)(2,1)} %grad_quarters.18), channel_id=1, source_target_pairs={{0,4},{4,0},{1,5},{5,1},{2,6},{6,2},{3,7},{7,3},{8,12},{12,8},{9,1... | collective-permute-start | bytes 4325384 | tf_op jit(solution)/shard_map/ppermute | solution.py:23
  306.9 40.7 %collective-permute-start.48 = (bf16[1,1,512,1408]{3,2,1,0:T(8,128)(2,1)S(1)}, bf16[1,1,512,1408]{3,2,1,0:T(8,128)(2,1)}, u32[]{:S(2)}, u32[]{:S(2)}) collective-permute-start(bf16[1,1,512,1408]{3,2,1,0:T(8,128)(2,1)S(1)} %grad_quarters.19), channel_id=1, source_target_pairs={{0,4},{4,0},{1,5},{5,1},{2,6},{6,2},{3,7},{7,3},{8,12},{12,8},{9,1... | collective-permute-start | bytes 4325384 | tf_op jit(solution)/shard_map/ppermute | solution.py:23
  333.7 29.8 %collective-permute-start.50 = (bf16[1,1408,512]{2,1,0:T(8,128)(2,1)S(1)}, bf16[1,1408,512]{2,1,0:T(8,128)(2,1)}, u32[]{:S(2)}, u32[]{:S(2)}) collective-permute-start(bf16[1,1408,512]{2,1,0:T(8,128)(2,1)S(1)} %bitcast.75), channel_id=1, source_target_pairs={{0,16},{16,0},{1,17},{17,1},{2,18},{18,2},{3,19},{19,3},{4,20},{20... | collective-permute-start | bytes 4325384 | tf_op jit(solution)/shard_map/ppermute | solution.py:23
  347.7 36.5 %collective-permute-start.53 = (bf16[1,1,512,1408]{3,2,1,0:T(8,128)(2,1)}, bf16[1,1,512,1408]{3,2,1,0:T(8,128)(2,1)}, u32[]{:S(2)}, u32[]{:S(2)}) collective-permute-start(bf16[1,1,512,1408]{3,2,1,0:T(8,128)(2,1)} %grad_quarters.20), channel_id=1, source_target_pairs={{0,4},{4,0},{1,5},{5,1},{2,6},{6,2},{3,7},{7,3},{8,12},{12,8},{9,1... | collective-permute-start | bytes 4325384 | tf_op jit(solution)/shard_map/ppermute | solution.py:23
  363.5 20.8 %collective-permute-start.52 = (bf16[2,1,512,512]{3,2,1,0:T(8,128)(2,1)}, bf16[2,1,512,512]{3,2,1,0:T(8,128)(2,1)S(1)}, u32[]{:S(2)}, u32[]{:S(2)}) collective-permute-start(bf16[2,1,512,512]{3,2,1,0:T(8,128)(2,1)} %copy-done.42), channel_id=1, source_target_pairs={{0,8},{8,0},{1,9},{9,1},{2,10},{10,2},{3,11},{11,3},{4,12},{12,4},... | collective-permute-start | bytes 3145736 | tf_op jit(solution)/shard_map/ppermute | solution.py:23
  366.5 34.1 %collective-permute-start.57 = (bf16[1,512,1408]{2,1,0:T(8,128)(2,1)}, bf16[1,512,1408]{2,1,0:T(8,128)(2,1)}, u32[]{:S(2)}, u32[]{:S(2)}) collective-permute-start(bf16[1,512,1408]{2,1,0:T(8,128)(2,1)} %bitcast.30), channel_id=1, source_target_pairs={{0,16},{16,0},{1,17},{17,1},{2,18},{18,2},{3,19},{19,3},{4,20},{20... | collective-permute-start | bytes 4325384 | tf_op jit(solution)/shard_map/ppermute | solution.py:23
  400.6 20.2 %collective-permute-start.58 = (bf16[2,3,512,512]{3,2,1,0:T(8,128)(2,1)}, bf16[2,3,512,512]{3,2,1,0:T(8,128)(2,1)}, u32[]{:S(2)}, u32[]{:S(2)}) collective-permute-start(bf16[2,3,512,512]{3,2,1,0:T(8,128)(2,1)} %grad_quarters.24), channel_id=1, source_target_pairs={{0,8},{8,0},{1,9},{9,1},{2,10},{10,2},{3,11},{11,3},{4,12},{12,4},... | collective-permute-start | bytes 9437192 | tf_op jit(solution)/shard_map/ppermute | solution.py:23
  408.4 39.2 %collective-permute-start.64 = (bf16[1,512,1408]{2,1,0:T(8,128)(2,1)}, bf16[1,512,1408]{2,1,0:T(8,128)(2,1)}, u32[]{:S(2)}, u32[]{:S(2)}) collective-permute-start(bf16[1,512,1408]{2,1,0:T(8,128)(2,1)} %bitcast.31), channel_id=1, source_target_pairs={{0,16},{16,0},{1,17},{17,1},{2,18},{18,2},{3,19},{19,3},{4,20},{20... | collective-permute-start | bytes 4325384 | tf_op jit(solution)/shard_map/ppermute | solution.py:23
  429.1 26.2 %collective-permute-start.63 = (bf16[1,2,512,512]{3,2,1,0:T(8,128)(2,1)S(1)}, bf16[1,2,512,512]{3,2,1,0:T(8,128)(2,1)S(1)}, u32[]{:S(2)}, u32[]{:S(2)}) collective-permute-start(bf16[1,2,512,512]{3,2,1,0:T(8,128)(2,1)S(1)} %grad_quarters.27), channel_id=1, source_target_pairs={{0,4},{4,0},{1,5},{5,1},{2,6},{6,2},{3,7},{7,3},{8,12},{12,8},{9,1... | collective-permute-start | bytes 3145736 | tf_op jit(solution)/shard_map/ppermute | solution.py:23
  459.1 38.8 %collective-permute-start.69 = (bf16[1,1408,512]{2,1,0:T(8,128)(2,1)}, bf16[1,1408,512]{2,1,0:T(8,128)(2,1)}, u32[]{:S(2)}, u32[]{:S(2)}) collective-permute-start(bf16[1,1408,512]{2,1,0:T(8,128)(2,1)} %add_convert_fusion.2), channel_id=1, source_target_pairs={{0,8},{8,0},{1,9},{9,1},{2,10},{10,2},{3,11},{11,3},{4,12},{12,4},... | collective-permute-start | bytes 4325384 | tf_op jit(solution)/shard_map/ppermute | solution.py:23
  465.4 32.5 %collective-permute-start.70 = (bf16[1,512,1408]{2,1,0:T(8,128)(2,1)}, bf16[1,512,1408]{2,1,0:T(8,128)(2,1)}, u32[]{:S(2)}, u32[]{:S(2)}) collective-permute-start(bf16[1,512,1408]{2,1,0:T(8,128)(2,1)} %add_convert_fusion.1.refs_0_), channel_id=1, source_target_pairs={{0,8},{8,0},{1,9},{9,1},{2,10},{10,2},{3,11},{11,3},{4,12},{12,4},... | collective-permute-start | bytes 4325384 | tf_op jit(solution)/shard_map/ppermute | solution.py:23
  470.1 27.8 %collective-permute-start.71 = (bf16[1,512,1408]{2,1,0:T(8,128)(2,1)}, bf16[1,512,1408]{2,1,0:T(8,128)(2,1)}, u32[]{:S(2)}, u32[]{:S(2)}) collective-permute-start(bf16[1,512,1408]{2,1,0:T(8,128)(2,1)} %add_convert_fusion.refs_1_), channel_id=1, source_target_pairs={{0,8},{8,0},{1,9},{9,1},{2,10},{10,2},{3,11},{11,3},{4,12},{12,4},... | collective-permute-start | bytes 4325384 | tf_op jit(solution)/shard_map/ppermute | solution.py:23
  470.1 25.9 %collective-permute-start.85 = (bf16[2,512,512]{2,1,0:T(8,128)(2,1)}, bf16[2,512,512]{2,1,0:T(8,128)(2,1)}, u32[]{:S(2)}, u32[]{:S(2)}) collective-permute-start(bf16[2,512,512]{2,1,0:T(8,128)(2,1)} %bitcast.33), channel_id=1, source_target_pairs={{0,16},{16,0},{1,17},{17,1},{2,18},{18,2},{3,19},{19,3},{4,20},{20... | collective-permute-start | bytes 3145736 | tf_op jit(solution)/shard_map/ppermute | solution.py:23
  472.9 58.1 %collective-permute-start.72 = (bf16[1,512,512]{2,1,0:T(8,128)(2,1)S(1)}, bf16[1,512,512]{2,1,0:T(8,128)(2,1)S(1)}, u32[]{:S(2)}, u32[]{:S(2)}) collective-permute-start(bf16[1,512,512]{2,1,0:T(8,128)(2,1)S(1)} %add_convert_fusion.6), channel_id=1, source_target_pairs={{0,8},{8,0},{1,9},{9,1},{2,10},{10,2},{3,11},{11,3},{4,12},{12,4},... | collective-permute-start | bytes 1572872 | tf_op jit(solution)/shard_map/ppermute | solution.py:23
  497.8 55.2 %collective-permute-start.86 = (bf16[2,512,512]{2,1,0:T(8,128)(2,1)S(1)}, bf16[2,512,512]{2,1,0:T(8,128)(2,1)}, u32[]{:S(2)}, u32[]{:S(2)}) collective-permute-start(bf16[2,512,512]{2,1,0:T(8,128)(2,1)S(1)} %add_convert_fusion.3), channel_id=1, source_target_pairs={{0,8},{8,0},{1,9},{9,1},{2,10},{10,2},{3,11},{11,3},{4,12},{12,4},... | collective-permute-start | bytes 3145736 | tf_op jit(solution)/shard_map/ppermute | solution.py:23
  505.8 23.8 %collective-permute-start.73 = (bf16[128,1024]{1,0:T(8,128)(2,1)S(1)}, bf16[128,1024]{1,0:T(8,128)(2,1)S(1)}, u32[]{:S(2)}, u32[]{:S(2)}) collective-permute-start(bf16[128,1024]{1,0:T(8,128)(2,1)S(1)} %get-tuple-element.302), channel_id=1, source_target_pairs={{0,0},{8,4},{4,8},{12,12},{1,1},{9,5},{5,9},{13,13},{2,2},{10,6},{... | collective-permute-start | bytes 786440 | tf_op jit(solution)/shard_map/ppermute | solution.py:763
  506.5 24.5 %collective-permute-start.74 = (bf16[128,1024]{1,0:T(8,128)(2,1)S(1)}, bf16[128,1024]{1,0:T(8,128)(2,1)S(1)}, u32[]{:S(2)}, u32[]{:S(2)}) collective-permute-start(bf16[128,1024]{1,0:T(8,128)(2,1)S(1)} %get-tuple-element.303), channel_id=1, source_target_pairs={{8,0},{0,4},{12,8},{4,12},{9,1},{1,5},{13,9},{5,13},{10,2},{2,6},{... | collective-permute-start | bytes 786440 | tf_op jit(solution)/shard_map/ppermute | solution.py:764
  (129 other events, 1349.4 us)

commit v4 on v3

--- a/solution.py
+++ b/solution.py
@@ -298,13 +298,13 @@
 CHUNK = 256
 
 
-def score_chunk(query, key, first, factor):
-    scores = (
-        lax.dot_general(query, key, (((1,), (1,)), ((), ())), preferred_element_type=F32) * factor
-    )
-    at_query = first + lax.broadcasted_iota(jnp.int32, scores.shape, 0)
-    at_key = lax.broadcasted_iota(jnp.int32, scores.shape, 1)
-    return jnp.where(at_query >= at_key, scores, -jnp.inf)
+def score_chunk(query, key, first):
+    scores = lax.dot_general(query, key, (((1,), (1,)), ((), ())), preferred_element_type=F32)
+    last = scores[:, first:]
+    at_query = lax.broadcasted_iota(jnp.int32, last.shape, 0)
+    at_key = lax.broadcasted_iota(jnp.int32, last.shape, 1)
+    last = jnp.where(at_query >= at_key, last, -jnp.inf)
+    return last if first == 0 else jnp.concatenate([scores[:, :first], last], axis=1)
 
 
 def attend(mine, other, order, factor):
@@ -325,16 +325,15 @@
             lanes = slice(head * HEAD_DIM, (head + 1) * HEAD_DIM)
             for first in range(0, length, CHUNK):
                 upto = first + CHUNK
-                scores = score_chunk(
-                    whole[0, first:upto, lanes], whole[1, :upto, lanes], first, factor
-                )
+                query = whole[0, first:upto, lanes] * jnp.bfloat16(factor)
+                scores = score_chunk(query, whole[1, :upto, lanes], first)
                 highest = jnp.max(scores, axis=1, keepdims=True)
                 exponent = jnp.exp(scores - highest)
                 summed = jnp.sum(exponent, axis=1, keepdims=True)
-                probs = (exponent * (1.0 / summed)).astype(BF16)
-                result[first:upto, lanes] = jnp.dot(
-                    probs, whole[2, :upto, lanes], preferred_element_type=F32
-                ).astype(BF16)
+                mixed = jnp.dot(
+                    exponent.astype(BF16), whole[2, :upto, lanes], preferred_element_type=F32
+                )
+                result[first:upto, lanes] = (mixed * (1.0 / summed)).astype(BF16)
                 lse_ref[0, first:upto, head : head + 1] = highest + jnp.log(summed)
         for slot in range(slots):
             here = slice(slot * piece, (slot + 1) * piece)
@@ -408,11 +407,11 @@
             lanes = slice(head * HEAD_DIM, (head + 1) * HEAD_DIM)
             for first in reversed(range(0, length, CHUNK)):
                 upto = first + CHUNK
-                query = whole[0, first:upto, lanes]
+                query = whole[0, first:upto, lanes] * jnp.bfloat16(factor)
                 key = whole[1, :upto, lanes]
                 value = whole[2, :upto, lanes]
                 grad = grads[first:upto, lanes]
-                scores = score_chunk(query, key, first, factor)
+                scores = score_chunk(query, key, first)
                 probs = jnp.exp(scores - lse_ref[0, first:upto, head : head + 1])
                 probs_grad = lax.dot_general(grad, value, across, preferred_element_type=F32)
                 shift = jnp.sum(probs * probs_grad, axis=1, keepdims=True)
@@ -420,7 +419,7 @@
                 dq_ref[first:upto, lanes] = (
                     jnp.dot(scores_grad, key, preferred_element_type=F32) * factor
                 )
-                dk = lax.dot_general(scores_grad, query, down, preferred_element_type=F32) * factor
+                dk = lax.dot_general(scores_grad, query, down, preferred_element_type=F32)
                 dv = lax.dot_general(
                     probs.astype(BF16), grad, down, preferred_element_type=F32
                 )
@@ -496,7 +495,7 @@
 def feed_forward(tokens, pieces, hidden_grad):
     rows, width = tokens.shape
     units = pieces[0].shape[2]
-    block = LANES if units % LANES == 0 else units
+    block = 256 if units > 256 else units
     cuts = cuts_of([p.shape[1] for p in pieces])
 
     def body(x_ref, *refs):
@@ -510,12 +509,12 @@
         silu = gate * sigma
         hidden_ref[...] = (silu * up).astype(BF16)
         grad = hg_ref[...].astype(F32)
-        grad_ref[0] = (grad * up * sigma * (1.0 + gate * (1.0 - sigma))).astype(BF16)
+        grad_ref[0] = (grad * up * (sigma + silu * (1.0 - sigma))).astype(BF16)
         grad_ref[1] = (grad * silu).astype(BF16)
 
     return pl.pallas_call(
         body,
-        grid=(units // block,),
+        grid=(pl.cdiv(units, block),),
         in_specs=[pl.BlockSpec((rows, width), lambda j: (0, 0))]
         + [pl.BlockSpec((2, p.shape[1], block), lambda j: (0, 0, j)) for p in pieces]
         + [pl.BlockSpec((rows, block), lambda j: (0, j))],
@@ -872,10 +871,11 @@
     part_b, hidden, pair = sync([], part_b, hidden, pair)
 
     hops = Scatter(part_b, slots)
-    down_got = swap(for_core(grad_rows, hidden[None], False), "core")
+    down_sent = for_core(grad_rows, hidden[None], False)
     gate_sent = for_core(tokens_b, pair, True)
-    down_got, gate_sent = sync([hops], down_got, gate_sent)
-    hops.hop()
+    down_sent, gate_sent = sync([hops], down_sent, gate_sent)
+    hops.hop()
+    down_got = swap(down_sent, "core")
     gate_got = swap(gate_sent, "core")
     down_oth = for_row(grad_rows, hidden[None], False, down_got)
     down_oth, gate_got = sync([hops], down_oth, gate_got)
@@ -963,49 +963,60 @@
     input_low, sums_a = norm_back(stream, hops.terms(), g2, gain_a, 0)
     down_rest = swap(down_total, "core")
     gate_rest = [swap(x, "core") for x in gate_total]
-    in_own.append(for_y(tokens_a, mixed, True, in_got, in_arrived[1], **spans[1]))
-    input_low, sums_a, in_own[1], down_rest, *gate_rest = sync(
-        [], input_low, sums_a, in_own[1], down_rest, *gate_rest
-    )
-    input_grad = from_sequence(input_low)
-    in_other.append(y_swap(in_own[1]))
     out_total = y_total(out_own, out_other_y)
     out_rest = swap(out_total, "core")
-    gate_grad = join_pairs(core[None], gate_total, gate_rest)
-    gate_grad, out_rest, input_grad = sync([], gate_grad, out_rest, input_grad)
-
-    input_grad = input_grad.astype(F32)
-    down_grad = join(down_total, down_rest, 2)[0]
-    out_grad = join(out_total, out_rest, 2)[0]
-    down_hops.flying = list(tie(down_hops.flying, input_grad)) if slots == 4 else []
-    down_hops.hop()
-    layer_low = (residual + sum(t.astype(F32) for t in down_hops.terms())).astype(BF16)
-    layer_out = from_sequence(layer_low)
-    in_total = [y_total(x, o) for x, o in zip(in_own, in_other)]
-    in_grad = jnp.concatenate([join(x, swap(x, "core"), 1) for x in in_total], axis=0)
-
-    def reduce_vector(own, oth, same):
-        total = jnp.concatenate([own, same, oth], axis=0)
-        if slots == 4:
-            pair = total + lax.ppermute(total, "col", PAIR)
-            inner = pair + lax.ppermute(pair, "col", MID)
-            outer = lax.ppermute(inner, "col", OUT)
-            total = jnp.where((place == 0) | (place == 3), outer, inner)
-        else:
-            total = lax.psum(total, "col")
-        total = total + swap(total, "core")
-        count = own.shape[0] + same.shape[0]
-        sent = jnp.concatenate([total[count:], total[own.shape[0] : count]], axis=0)
-        total = total[:count] + swap(sent, "row")
-        return lax.psum(total, "y") if y_count != 2 else total + swap(total, "y")
+    in_own.append(for_y(tokens_a, mixed, True, in_got, in_arrived[1], **spans[1]))
+    input_low, sums_a, in_own[1], down_rest, out_rest, *gate_rest = sync(
+        [], input_low, sums_a, in_own[1], down_rest, out_rest, *gate_rest
+    )
 
     bias_all = jnp.zeros((3, 2 * slots * columns), F32)
     bias_all = lax.dynamic_update_slice(
         bias_all, bias_part[:, 0, :], (jnp.int32(0), (place * 2 + core) * columns)
     ).reshape(-1, wide)
-    sums = after(jnp.concatenate([sums_a, sums_b], axis=0), in_own[1])
-    vectors = reduce_vector(sums[:, :wide], natural(sums[:, wide:]), bias_all)
+    sums = jnp.concatenate([sums_a, sums_b], axis=0)
+    own, oth = sums[:, :wide], natural(sums[:, wide:])
+    total = jnp.concatenate([own, bias_all, oth], axis=0)
+
+    in_other.append(y_swap(in_own[1]))
+    input_grad = from_sequence(input_low)
+    down_grad = join(down_total, down_rest, 2)[0]
+    if slots == 4:
+        arrived = lax.ppermute(total, "col", PAIR)
+        arrived, input_grad, down_grad = sync([], arrived, input_grad, down_grad)
+        total = total + arrived
+        arrived = lax.ppermute(total, "col", MID)
+        down_hops.flying = list(tie(down_hops.flying, input_grad))
+        down_hops.hop()
+        gate_grad = join_pairs(core[None], gate_total, gate_rest)
+        arrived, gate_grad, in_other[0] = sync([down_hops], arrived, gate_grad, in_other[0])
+        total = total + arrived
+        outer = lax.ppermute(total, "col", OUT)
+        layer_low = (residual + sum(t.astype(F32) for t in down_hops.terms())).astype(BF16)
+        in_total = [y_total(in_own[0], in_other[0])]
+        in_rest = [swap(in_total[0], "core")]
+        outer, layer_low, in_rest[0] = sync([], outer, layer_low, in_rest[0])
+        total = jnp.where((place == 0) | (place == 3), outer, total)
+    else:
+        gate_grad = join_pairs(core[None], gate_total, gate_rest)
+        layer_low = (residual + sum(t.astype(F32) for t in down_hops.terms())).astype(BF16)
+        in_total = [y_total(in_own[0], in_other[0])]
+        in_rest = [swap(in_total[0], "core")]
+        total = lax.psum(total, "col")
+    layer_out = from_sequence(layer_low)
+    out_grad = join(out_total, out_rest, 2)[0]
+    arrived = swap(total, "core")
+    arrived, layer_out, in_other[1], out_grad = sync([], arrived, layer_out, in_other[1], out_grad)
+    total = total + arrived
+    cut = own.shape[0] + bias_all.shape[0]
+    sent = jnp.concatenate([total[cut:], total[own.shape[0] : cut]], axis=0)
+    total = total[:cut] + swap(sent, "row")
+    vectors = lax.psum(total, "y") if y_count != 2 else total + swap(total, "y")
     bias_grad = take(vectors[4:].reshape(3, -1), place * 2 * columns, 2 * columns, 1)
+    input_grad = input_grad.astype(F32)
+    in_total.append(y_total(in_own[1], in_other[1]))
+    in_rest.append(swap(in_total[1], "core"))
+    in_grad = jnp.concatenate([join(x, r, 1) for x, r in zip(in_total, in_rest)], axis=0)
     return (
         layer_out[None],
         input_grad,

time: 573 us -> 542 us (0.946)
  waiting for transfers between devices: 203 us -> 178 us
    ppermute x38, waiting for transfers between devices: 69.8 us -> 61.4 us  [swap(): return lax.ppermute(x, axis, [(0, 1), (1, 0)])]
    ppermute x4, waiting for transfers between devices: 16.2 us -> 9.16 us  [__init__(): self.flying = [lax.ppermute(self.part[3], 'col', IN)]]
  transfers between devices with their start and end apart: 89 -> 89, of which waited for: 37 -> 36; matrix products, arithmetic and copies ran while one was open for 12% -> 12% of each run, Pallas kernels for 20% -> 22%
where the time goes in v4:
time: 542 us; the launch traced here: 533 us
  waiting for transfers between devices  178 us (33%)
  Pallas kernels  146 us (27%)
  starting transfers between devices  119 us (22%)
  other arithmetic  51 us (9%)
  local copies, waits for them, and re-layouts  37.4 us (7%)
    ppermute x38, waiting for transfers between devices, swap(): return lax.ppermute(x, axis, [(0, 1), (1, 0)])  61.4 us
    pallas_call x16, Pallas kernels, grad_quarters(): pl.pallas_call(body, grid_spec=pltpu.PrefetchScalarGridSpec(num_scalar_pr...  46.1 us
    pallas_call x4, Pallas kernels, to_features(): pl.pallas_call(body, grid=(width // block,), in_specs=[pl.BlockSpec((coun...  33.2 us
    ppermute x38, starting transfers between devices, swap(): return lax.ppermute(x, axis, [(0, 1), (1, 0)])  28.7 us
    ppermute x8, waiting for transfers between devices, hop(): self.flying = [lax.ppermute(one, 'col', MID), lax.ppermute(mid, 'col', OUT)]  24.1 us
    unnamed x129, local copies, waits for them, and re-layouts  21.9 us
    ppermute x4, starting transfers between devices, __init__(): self.two = lax.ppermute(self.part[2], 'col', IN)  21.1 us
    ppermute x4, waiting for transfers between devices, hop(): self.flying = [lax.ppermute(far, 'col', OUT)]  18.8 us
  transfers between devices with their start and end apart: 89, of which 36 were waited for; matrix products, arithmetic and copies ran while one was open for 12% of the time, Pallas kernels for 22%

profile of v4, /device:TPU:0, one launch (start us, length us, event | category | flops | bytes accessed | tf_op | source)
XLA Modules:
  0.0 533.4 jit_solution(8663619018776998645)
XLA Ops:
  8.4 5.7 %collective-permute-done.2 = f32[4,1024]{1,0:T(4,128)S(1)} collective-permute-done((f32[4,1024]{1,0:T(4,128)S(1)}, f32[4,1024]{1,0:T(4,128)S(1)}, u32[]{:S(2)}, u32[]{:S(2)}) %collective-permute-start.2) | collective-permute-done | bytes 16416 | tf_op jit(solution)/shard_map/ppermute | solution.py:23
  36.9 5.9 %copy.29 = bf16[1,1024,2,1408]{3,1,2,0:T(8,128)(2,1)} copy(bf16[1,1024,2,1408]{3,2,1,0:T(2,128)(2,1)} %param.20) | data formatting | bytes 11534336 | tf_op args[8]
  51.8 12.0 %collective-permute-done.10 = bf16[128,1024]{1,0:T(8,128)(2,1)S(1)} collective-permute-done((bf16[128,1024]{1,0:T(8,128)(2,1)S(1)}, bf16[128,1024]{1,0:T(8,128)(2,1)S(1)}, u32[]{:S(2)}, u32[]{:S(2)}) %collective-permute-start.10) | collective-permute-done | bytes 262176 | tf_op jit(solution)/shard_map/ppermute | solution.py:755
  87.2 7.9 %attend.1 = (bf16[512,256]{1,0:T(8,128)(2,1)S(1)}, bf16[512,256]{1,0:T(8,128)(2,1)S(1)}, f32[2,1024,2]{2,1,0:T(8,128)S(1)}) custom-call(s32[5]{0:T(128)S(1)} %pad_add_fusion.order_ref, bf16[3,512,256]{2,1,0:T(8,128)(2,1)S(1)} %qkv_columns.2.mine_ref, bf16[3,512,256]{2,1,0:T(8,128)(2,1)S(1)} %collective-permute-done.14.other_ref), custom_call_target="tpu_custom_call" | custom-call | flops 134217728 | bytes 262144 | tf_op jit(solution)/shard_map/attend/pallas_call | solution.py:346
  104.9 9.7 %collective-permute-done.17 = bf16[128,2048]{1,0:T(8,128)(2,1)} collective-permute-done((bf16[128,2048]{1,0:T(8,128)(2,1)}, bf16[128,2048]{1,0:T(8,128)(2,1)}, u32[]{:S(2)}, u32[]{:S(2)}) %collective-permute-start.17) | collective-permute-done | bytes 524320 | tf_op jit(solution)/shard_map/ppermute | solution.py:60
  121.7 6.2 %collective-permute-done.20 = bf16[128,2048]{1,0:T(8,128)(2,1)S(1)} collective-permute-done((bf16[128,2048]{1,0:T(8,128)(2,1)S(1)}, bf16[128,2048]{1,0:T(8,128)(2,1)S(1)}, u32[]{:S(2)}, u32[]{:S(2)}) %collective-permute-start.20) | collective-permute-done | bytes 524320 | tf_op jit(solution)/shard_map/ppermute | solution.py:80
  142.9 8.3 %collective-permute-done.24 = bf16[128,2048]{1,0:T(8,128)(2,1)S(1)} collective-permute-done((bf16[128,2048]{1,0:T(8,128)(2,1)S(1)}, bf16[128,2048]{1,0:T(8,128)(2,1)S(1)}, u32[]{:S(2)}, u32[]{:S(2)}) %collective-permute-start.24) | collective-permute-done | bytes 524320 | tf_op jit(solution)/shard_map/ppermute | solution.py:81
  154.6 5.4 %from_features.3 = bf16[2,512,704]{2,1,0:T(8,128)(2,1)S(1)} custom-call(s32[2]{0:T(128)S(1)} %iota.35.index_ref, bf16[512,2048]{1,0:T(8,128)(2,1)S(1)} %pad_maximum_fusion.1.x_ref, bf16[1408,1024]{1,0:T(8,128)(2,1)S(1)} %bitcast.80, bf16[1408,512]{1,0:T(8,128)(2,1)} %collective-permute-done.22.refs_1_, bf16[1408,512]{1,0:T(8,128)(2,1)S(1)} %collective-permute-done.25.refs_2_), custom_call_target="tpu_custom_call" | custom-call | flops 369098752 | bytes 983040 | tf_op jit(solution)/shard_map/from_features/pallas_call | solution.py:593
  170.7 9.6 %collective-permute-done.28 = bf16[128,2048]{1,0:T(8,128)(2,1)S(1)} collective-permute-done((bf16[128,2048]{1,0:T(8,128)(2,1)S(1)}, bf16[128,2048]{1,0:T(8,128)(2,1)S(1)}, u32[]{:S(2)}, u32[]{:S(2)}) %collective-permute-start.28) | collective-permute-done | bytes 524320 | tf_op jit(solution)/shard_map/ppermute | solution.py:52
  182.2 15.2 %collective-permute-done.32.refs_1_ = bf16[2,512,1408]{2,1,0:T(8,128)(2,1)S(1)} collective-permute-done((bf16[2,512,1408]{2,1,0:T(8,128)(2,1)}, bf16[2,512,1408]{2,1,0:T(8,128)(2,1)S(1)}, u32[]{:S(2)}, u32[]{:S(2)}) %collective-permute-start.32) | collective-permute-done | bytes 2883616 | tf_op jit(solution)/shard_map/ppermute | solution.py:23
  199.4 14.3 %collective-permute-done.33 = bf16[128,2048]{1,0:T(8,128)(2,1)S(1)} collective-permute-done((bf16[128,2048]{1,0:T(8,128)(2,1)S(1)}, bf16[128,2048]{1,0:T(8,128)(2,1)S(1)}, u32[]{:S(2)}, u32[]{:S(2)}) %collective-permute-start.33) | collective-permute-done | bytes 524320 | tf_op jit(solution)/shard_map/ppermute | solution.py:64
  215.3 12.2 %feed_forward.1 = (bf16[512,1408]{1,0:T(8,128)(2,1)S(1)}, bf16[2,512,1408]{2,1,0:T(8,128)(2,1)}) custom-call(bf16[512,2048]{1,0:T(8,128)(2,1)S(1)} %pad_maximum_fusion.2.x_ref, bf16[2,1024,1408]{2,1,0:T(8,128)(2,1)} %bitcast.98, bf16[2,512,1408]{2,1,0:T(8,128)(2,1)} %copy-done.57, bf16[2,512,1408]{2,1,0:T(8,128)(2,1)} %copy-done.58, ...), custom_call_target="tpu_custom_call" | custom-call | flops 738197504 | bytes 1703936 | tf_op jit(solution)/shard_map/feed_forward/pallas_call | solution.py:515
  227.5 13.1 %to_features.5 = bf16[512,2048]{1,0:T(8,128)(2,1)} custom-call(bf16[2,512,1408]{2,1,0:T(8,128)(2,1)} %get-tuple-element.202.v_ref.y_ref, bf16[2,1024,1408]{2,1,0:T(8,128)(2,1)} %bitcast.99, bf16[2,512,1408]{2,1,0:T(8,128)(2,1)} %copy-done.57, bf16[2,512,1408]{2,1,0:T(8,128)(2,1)} %copy-done.58), custom_call_target="tpu_custom_call" | custom-call | flops 738197504 | bytes 2064384 | tf_op jit(solution)/shard_map/to_features/pallas_call | solution.py:565
  248.5 5.9 %grad_quarters.17 = bf16[2,2,512,1408]{3,2,1,0:T(8,128)(2,1)} custom-call(s32[2]{0:T(128)S(1)} %pad_add_fusion.1.q_ref, bf16[512,2048]{1,0:T(8,128)(2,1)S(1)} %copy-done.2, bf16[2,512,1408]{2,1,0:T(8,128)(2,1)S(1)} %copy-done), custom_call_target="tpu_custom_call" | custom-call | flops 369098752 | bytes 1343488 | tf_op jit(solution)/shard_map/grad_quarters/pallas_call | solution.py:631
  255.7 6.7 %collective-permute-start.37 = (bf16[128,2048]{1,0:T(8,128)(2,1)S(1)}, bf16[128,2048]{1,0:T(8,128)(2,1)S(1)}, u32[]{:S(2)}, u32[]{:S(2)}) collective-permute-start(bf16[128,2048]{1,0:T(8,128)(2,1)S(1)} %get-tuple-element.311), channel_id=1, source_target_pairs={{0,1},{3,2},{4,5},{7,6},{8,9},{11,10},{12,13},{15,14},{16,17},{19,... | collective-permute-start | bytes 1572872 | tf_op jit(solution)/shard_map/ppermute | solution.py:81
  262.4 5.8 %collective-permute-done.38.refs_0_ = bf16[2,1,1408,512]{3,2,1,0:T(8,128)(2,1)} collective-permute-done((bf16[2,1,1408,512]{3,2,1,0:T(8,128)(2,1)}, bf16[2,1,1408,512]{3,2,1,0:T(8,128)(2,1)}, u32[]{:S(2)}, u32[]{:S(2)}) %collective-permute-start.38) | collective-permute-done | bytes 2883616 | tf_op jit(solution)/shard_map/ppermute | solution.py:23
  296.7 7.8 %to_features.6 = bf16[512,2048]{1,0:T(8,128)(2,1)} custom-call(bf16[1,512,1408]{2,1,0:T(8,128)(2,1)} %bitcast.78, bf16[1,1408,1024]{2,1,0:T(8,128)(2,1)} %refs_0_.3, bf16[1,1408,512]{2,1,0:T(8,128)(2,1)} %bitcast.24.refs_1_, bf16[1,1408,512]{2,1,0:T(8,128)(2,1)} %bitcast.83), custom_call_target="tpu_custom_call" | custom-call | flops 369098752 | bytes 1163264 | tf_op jit(solution)/shard_map/to_features/pallas_call | solution.py:565
  313.0 9.4 %collective-permute-done.46 = bf16[128,2048]{1,0:T(8,128)(2,1)S(1)} collective-permute-done((bf16[128,2048]{1,0:T(8,128)(2,1)S(1)}, bf16[128,2048]{1,0:T(8,128)(2,1)S(1)}, u32[]{:S(2)}, u32[]{:S(2)}) %collective-permute-start.46) | collective-permute-done | bytes 524320 | tf_op jit(solution)/shard_map/ppermute | solution.py:60
  325.7 11.3 %collective-permute-done.48.refs_1_ = bf16[1,1,512,1408]{3,2,1,0:T(8,128)(2,1)} collective-permute-done((bf16[1,1,512,1408]{3,2,1,0:T(8,128)(2,1)S(1)}, bf16[1,1,512,1408]{3,2,1,0:T(8,128)(2,1)}, u32[]{:S(2)}, u32[]{:S(2)}) %collective-permute-start.48) | collective-permute-done | bytes 1441824 | tf_op jit(solution)/shard_map/ppermute | solution.py:23
  357.5 16.2 %attend_back.1 = (bf16[3,512,256]{2,1,0:T(8,128)(2,1)S(1)}, bf16[3,512,256]{2,1,0:T(8,128)(2,1)}, f32[3,1,256]{2,1,0:T(1,128)S(1)}) custom-call(s32[5]{0:T(128)S(1)} %pad_add_fusion.order_ref, bf16[3,512,256]{2,1,0:T(8,128)(2,1)} %copy-done.22, bf16[3,512,256]{2,1,0:T(8,128)(2,1)} %copy-done.39, bf16[512,256]{1,0:T(8,128)(2,1)S(1)} %bitcast.94, ...), custom_call_target="tpu_custom_call" | custom-call | flops 335544320 | bytes 655360 | tf_op jit(solution)/shard_map/attend_back/pallas_call | solution.py:456
  398.1 7.8 %to_features.7 = bf16[512,2048]{1,0:T(8,128)(2,1)} custom-call(bf16[3,512,512]{2,1,0:T(8,128)(2,1)} %copy-done.4, bf16[3,1024,512]{2,1,0:T(8,128)(2,1)} %bitcast.73, bf16[3,512,512]{2,1,0:T(8,128)(2,1)} %copy-done.14, bf16[3,512,512]{2,1,0:T(8,128)(2,1)} %copy-done.15), custom_call_target="tpu_custom_call" | custom-call | flops 402653184 | bytes 1245184 | tf_op jit(solution)/shard_map/to_features/pallas_call | solution.py:565
  424.4 6.7 %collective-permute-start.62 = (bf16[128,2048]{1,0:T(8,128)(2,1)S(1)}, bf16[128,2048]{1,0:T(8,128)(2,1)S(1)}, u32[]{:S(2)}, u32[]{:S(2)}) collective-permute-start(bf16[128,2048]{1,0:T(8,128)(2,1)S(1)} %get-tuple-element.304), channel_id=1, source_target_pairs={{0,1},{3,2},{4,5},{7,6},{8,9},{11,10},{12,13},{15,14},{16,17},{19,... | collective-permute-start | bytes 1572872 | tf_op jit(solution)/shard_map/ppermute | solution.py:81
  485.5 9.5 %join_pairs.1 = f32[1024,2,1408]{2,1,0:T(2,128)} custom-call(s32[1]{0:T(128)} %bitcast.10.half_ref.q_ref.index_ref.core_ref, bf16[1,512,1408]{2,1,0:T(8,128)(2,1)} %add_convert_fusion.1.refs_0_, bf16[1,512,1408]{2,1,0:T(8,128)(2,1)} %add_convert_fusion.refs_1_, bf16[1,512,1408]{2,1,0:T(8,128)(2,1)} %collective-permute-done.71.refs_2_, ...), custom_call_target="tpu_custom_call" | custom-call | flops 90112 | bytes 2162688 | tf_op jit(solution)/shard_map/join_pairs/pallas_call | solution.py:678
  503.3 5.9 %collective-permute-done.80 = f32[14,1024]{1,0:T(8,128)S(1)} collective-permute-done((f32[14,1024]{1,0:T(8,128)S(1)}, f32[14,1024]{1,0:T(8,128)S(1)}, u32[]{:S(2)}, u32[]{:S(2)}) %collective-permute-start.80) | collective-permute-done | bytes 57376 | tf_op jit(solution)/shard_map/ppermute | solution.py:994
  (419 shorter events, 312.4 us)
Async XLA Ops:
  25.4 38.8 %collective-permute-start.8 = (bf16[3,512,512]{2,1,0:T(8,128)(2,1)S(1)}, bf16[3,512,512]{2,1,0:T(8,128)(2,1)S(1)}, u32[]{:S(2)}, u32[]{:S(2)}) collective-permute-start(bf16[3,512,512]{2,1,0:T(8,128)(2,1)S(1)} %dynamic-slice_bitcast_fusion), channel_id=1, source_target_pairs={{0,4},{4,0},{1,5},{5,1},{2,6},{6,2},{3,7},{7,3},{8,12},{12,8},{9,1... | collective-permute-start | bytes 4718600 | tf_op jit(solution)/shard_map/ppermute | solution.py:23
  25.5 38.3 %collective-permute-start.10 = (bf16[128,1024]{1,0:T(8,128)(2,1)S(1)}, bf16[128,1024]{1,0:T(8,128)(2,1)S(1)}, u32[]{:S(2)}, u32[]{:S(2)}) collective-permute-start(bf16[128,1024]{1,0:T(8,128)(2,1)S(1)} %get-tuple-element.343), channel_id=1, source_target_pairs={{0,8},{4,0},{8,12},{12,4},{1,9},{5,1},{9,13},{13,5},{2,10},{6,2},{... | collective-permute-start | bytes 786440 | tf_op jit(solution)/shard_map/ppermute | solution.py:755
  26.2 37.6 %collective-permute-start.9 = (bf16[128,1024]{1,0:T(8,128)(2,1)S(1)}, bf16[128,1024]{1,0:T(8,128)(2,1)S(1)}, u32[]{:S(2)}, u32[]{:S(2)}) collective-permute-start(bf16[128,1024]{1,0:T(8,128)(2,1)S(1)} %get-tuple-element.342), channel_id=1, source_target_pairs={{0,0},{4,8},{8,4},{12,12},{1,1},{5,9},{9,5},{13,13},{2,2},{6,10},{... | collective-permute-start | bytes 786440 | tf_op jit(solution)/shard_map/ppermute | solution.py:754
  31.8 18.7 %collective-permute-start.6 = (bf16[128,2048]{1,0:T(8,128)(2,1)}, bf16[128,2048]{1,0:T(8,128)(2,1)S(1)}, u32[]{:S(2)}, u32[]{:S(2)}) collective-permute-start(bf16[128,2048]{1,0:T(8,128)(2,1)} %collective-permute-done.4), channel_id=1, source_target_pairs={{1,0},{2,3},{5,4},{6,7},{9,8},{10,11},{13,12},{14,15},{17,16},{18,... | collective-permute-start | bytes 1572872 | tf_op jit(solution)/shard_map/ppermute | solution.py:60
  74.8 21.3 %collective-permute-start.15 = (bf16[512,512]{1,0:T(8,128)(2,1)}, bf16[512,512]{1,0:T(8,128)(2,1)S(1)}, u32[]{:S(2)}, u32[]{:S(2)}) collective-permute-start(bf16[512,512]{1,0:T(8,128)(2,1)} %dynamic-slice_bitcast_fusion.2), channel_id=1, source_target_pairs={{0,4},{4,0},{1,5},{5,1},{2,6},{6,2},{3,7},{7,3},{8,12},{12,8},{9,1... | collective-permute-start | bytes 1572872 | tf_op jit(solution)/shard_map/ppermute | solution.py:23
  83.1 38.6 %collective-permute-start.22 = (bf16[1408,512]{1,0:T(8,128)(2,1)}, bf16[1408,512]{1,0:T(8,128)(2,1)}, u32[]{:S(2)}, u32[]{:S(2)}) collective-permute-start(bf16[1408,512]{1,0:T(8,128)(2,1)} %dynamic-slice_bitcast_fusion.1), channel_id=1, source_target_pairs={{0,4},{4,0},{1,5},{5,1},{2,6},{6,2},{3,7},{7,3},{8,12},{12,8},{9,1... | collective-permute-start | bytes 4325384 | tf_op jit(solution)/shard_map/ppermute | solution.py:23
  132.1 19.1 %collective-permute-start.25 = (bf16[1408,512]{1,0:T(8,128)(2,1)}, bf16[1408,512]{1,0:T(8,128)(2,1)S(1)}, u32[]{:S(2)}, u32[]{:S(2)}) collective-permute-start(bf16[1408,512]{1,0:T(8,128)(2,1)} %collective-permute-done.22.refs_1_), channel_id=1, source_target_pairs={{0,8},{8,0},{1,9},{9,1},{2,10},{10,2},{3,11},{11,3},{4,12},{12,4},... | collective-permute-start | bytes 4325384 | tf_op jit(solution)/shard_map/ppermute | solution.py:23
  132.1 65.3 %collective-permute-start.32 = (bf16[2,512,1408]{2,1,0:T(8,128)(2,1)}, bf16[2,512,1408]{2,1,0:T(8,128)(2,1)S(1)}, u32[]{:S(2)}, u32[]{:S(2)}) collective-permute-start(bf16[2,512,1408]{2,1,0:T(8,128)(2,1)} %bitcast.102), channel_id=1, source_target_pairs={{0,4},{4,0},{1,5},{5,1},{2,6},{6,2},{3,7},{7,3},{8,12},{12,8},{9,1... | collective-permute-start | bytes 8650760 | tf_op jit(solution)/shard_map/ppermute | solution.py:23
  254.4 19.1 %collective-permute-start.39 = (bf16[2,2,512,1408]{3,2,1,0:T(8,128)(2,1)}, bf16[2,2,512,1408]{3,2,1,0:T(8,128)(2,1)}, u32[]{:S(2)}, u32[]{:S(2)}) collective-permute-start(bf16[2,2,512,1408]{3,2,1,0:T(8,128)(2,1)} %grad_quarters.17), channel_id=1, source_target_pairs={{0,8},{8,0},{1,9},{9,1},{2,10},{10,2},{3,11},{11,3},{4,12},{12,4},... | collective-permute-start | bytes 17301512 | tf_op jit(solution)/shard_map/ppermute | solution.py:23
  273.4 34.7 %collective-permute-start.44 = (bf16[1,1,1408,512]{3,2,1,0:T(8,128)(2,1)}, bf16[1,1,1408,512]{3,2,1,0:T(8,128)(2,1)S(1)}, u32[]{:S(2)}, u32[]{:S(2)}) collective-permute-start(bf16[1,1,1408,512]{3,2,1,0:T(8,128)(2,1)} %grad_quarters.18), channel_id=1, source_target_pairs={{0,4},{4,0},{1,5},{5,1},{2,6},{6,2},{3,7},{7,3},{8,12},{12,8},{9,1... | collective-permute-start | bytes 4325384 | tf_op jit(solution)/shard_map/ppermute | solution.py:23
  296.3 40.7 %collective-permute-start.48 = (bf16[1,1,512,1408]{3,2,1,0:T(8,128)(2,1)S(1)}, bf16[1,1,512,1408]{3,2,1,0:T(8,128)(2,1)}, u32[]{:S(2)}, u32[]{:S(2)}) collective-permute-start(bf16[1,1,512,1408]{3,2,1,0:T(8,128)(2,1)S(1)} %grad_quarters.19), channel_id=1, source_target_pairs={{0,4},{4,0},{1,5},{5,1},{2,6},{6,2},{3,7},{7,3},{8,12},{12,8},{9,1... | collective-permute-start | bytes 4325384 | tf_op jit(solution)/shard_map/ppermute | solution.py:23
  322.4 28.6 %collective-permute-start.50 = (bf16[1,1408,512]{2,1,0:T(8,128)(2,1)S(1)}, bf16[1,1408,512]{2,1,0:T(8,128)(2,1)}, u32[]{:S(2)}, u32[]{:S(2)}) collective-permute-start(bf16[1,1408,512]{2,1,0:T(8,128)(2,1)S(1)} %bitcast.84), channel_id=1, source_target_pairs={{0,16},{16,0},{1,17},{17,1},{2,18},{18,2},{3,19},{19,3},{4,20},{20... | collective-permute-start | bytes 4325384 | tf_op jit(solution)/shard_map/ppermute | solution.py:23
  337.1 36.5 %collective-permute-start.53 = (bf16[1,1,512,1408]{3,2,1,0:T(8,128)(2,1)}, bf16[1,1,512,1408]{3,2,1,0:T(8,128)(2,1)}, u32[]{:S(2)}, u32[]{:S(2)}) collective-permute-start(bf16[1,1,512,1408]{3,2,1,0:T(8,128)(2,1)} %grad_quarters.20), channel_id=1, source_target_pairs={{0,4},{4,0},{1,5},{5,1},{2,6},{6,2},{3,7},{7,3},{8,12},{12,8},{9,1... | collective-permute-start | bytes 4325384 | tf_op jit(solution)/shard_map/ppermute | solution.py:23
  351.0 22.7 %collective-permute-start.52 = (bf16[2,1,512,512]{3,2,1,0:T(8,128)(2,1)}, bf16[2,1,512,512]{3,2,1,0:T(8,128)(2,1)S(1)}, u32[]{:S(2)}, u32[]{:S(2)}) collective-permute-start(bf16[2,1,512,512]{3,2,1,0:T(8,128)(2,1)} %copy-done.43), channel_id=1, source_target_pairs={{0,8},{8,0},{1,9},{9,1},{2,10},{10,2},{3,11},{11,3},{4,12},{12,4},... | collective-permute-start | bytes 3145736 | tf_op jit(solution)/shard_map/ppermute | solution.py:23
  352.1 21.6 %collective-permute-start.51 = (bf16[128,2048]{1,0:T(8,128)(2,1)S(1)}, bf16[128,2048]{1,0:T(8,128)(2,1)S(1)}, u32[]{:S(2)}, u32[]{:S(2)}) collective-permute-start(bf16[128,2048]{1,0:T(8,128)(2,1)S(1)} %slice.164), channel_id=1, source_target_pairs={{0,1},{3,2},{4,5},{7,6},{8,9},{11,10},{12,13},{15,14},{16,17},{19,... | collective-permute-start | bytes 1572872 | tf_op jit(solution)/shard_map/ppermute | solution.py:80
  355.9 33.8 %collective-permute-start.57 = (bf16[1,512,1408]{2,1,0:T(8,128)(2,1)}, bf16[1,512,1408]{2,1,0:T(8,128)(2,1)}, u32[]{:S(2)}, u32[]{:S(2)}) collective-permute-start(bf16[1,512,1408]{2,1,0:T(8,128)(2,1)} %bitcast.30), channel_id=1, source_target_pairs={{0,16},{16,0},{1,17},{17,1},{2,18},{18,2},{3,19},{19,3},{4,20},{20... | collective-permute-start | bytes 4325384 | tf_op jit(solution)/shard_map/ppermute | solution.py:23
  389.7 20.2 %collective-permute-start.58 = (bf16[2,3,512,512]{3,2,1,0:T(8,128)(2,1)}, bf16[2,3,512,512]{3,2,1,0:T(8,128)(2,1)}, u32[]{:S(2)}, u32[]{:S(2)}) collective-permute-start(bf16[2,3,512,512]{3,2,1,0:T(8,128)(2,1)} %grad_quarters.24), channel_id=1, source_target_pairs={{0,8},{8,0},{1,9},{9,1},{2,10},{10,2},{3,11},{11,3},{4,12},{12,4},... | collective-permute-start | bytes 9437192 | tf_op jit(solution)/shard_map/ppermute | solution.py:23
  396.6 38.2 %collective-permute-start.64 = (bf16[1,512,1408]{2,1,0:T(8,128)(2,1)}, bf16[1,512,1408]{2,1,0:T(8,128)(2,1)}, u32[]{:S(2)}, u32[]{:S(2)}) collective-permute-start(bf16[1,512,1408]{2,1,0:T(8,128)(2,1)} %bitcast.31), channel_id=1, source_target_pairs={{0,16},{16,0},{1,17},{17,1},{2,18},{18,2},{3,19},{19,3},{4,20},{20... | collective-permute-start | bytes 4325384 | tf_op jit(solution)/shard_map/ppermute | solution.py:23
  418.0 26.2 %collective-permute-start.63 = (bf16[1,2,512,512]{3,2,1,0:T(8,128)(2,1)S(1)}, bf16[1,2,512,512]{3,2,1,0:T(8,128)(2,1)S(1)}, u32[]{:S(2)}, u32[]{:S(2)}) collective-permute-start(bf16[1,2,512,512]{3,2,1,0:T(8,128)(2,1)S(1)} %grad_quarters.27), channel_id=1, source_target_pairs={{0,4},{4,0},{1,5},{5,1},{2,6},{6,2},{3,7},{7,3},{8,12},{12,8},{9,1... | collective-permute-start | bytes 3145736 | tf_op jit(solution)/shard_map/ppermute | solution.py:23
  434.3 19.2 %collective-permute-start.67 = (bf16[1,1,512,512]{3,2,1,0:T(8,128)(2,1)S(1)}, bf16[1,1,512,512]{3,2,1,0:T(8,128)(2,1)S(1)}, u32[]{:S(2)}, u32[]{:S(2)}) collective-permute-start(bf16[1,1,512,512]{3,2,1,0:T(8,128)(2,1)S(1)} %grad_quarters.28), channel_id=1, source_target_pairs={{0,4},{4,0},{1,5},{5,1},{2,6},{6,2},{3,7},{7,3},{8,12},{12,8},{9,1... | collective-permute-start | bytes 1572872 | tf_op jit(solution)/shard_map/ppermute | solution.py:23
  434.8 18.7 %collective-permute-start.68 = (bf16[1,512,512]{2,1,0:T(8,128)(2,1)S(1)}, bf16[1,512,512]{2,1,0:T(8,128)(2,1)S(1)}, u32[]{:S(2)}, u32[]{:S(2)}) collective-permute-start(bf16[1,512,512]{2,1,0:T(8,128)(2,1)S(1)} %bitcast.92), channel_id=1, source_target_pairs={{0,16},{16,0},{1,17},{17,1},{2,18},{18,2},{3,19},{19,3},{4,20},{20... | collective-permute-start | bytes 1572872 | tf_op jit(solution)/shard_map/ppermute | solution.py:23
  448.1 19.2 %collective-permute-start.69 = (bf16[1,1408,512]{2,1,0:T(8,128)(2,1)}, bf16[1,1408,512]{2,1,0:T(8,128)(2,1)}, u32[]{:S(2)}, u32[]{:S(2)}) collective-permute-start(bf16[1,1408,512]{2,1,0:T(8,128)(2,1)} %add_convert_fusion.2), channel_id=1, source_target_pairs={{0,8},{8,0},{1,9},{9,1},{2,10},{10,2},{3,11},{11,3},{4,12},{12,4},... | collective-permute-start | bytes 4325384 | tf_op jit(solution)/shard_map/ppermute | solution.py:23
  459.2 35.8 %collective-permute-start.79 = (bf16[2,512,512]{2,1,0:T(8,128)(2,1)}, bf16[2,512,512]{2,1,0:T(8,128)(2,1)S(1)}, u32[]{:S(2)}, u32[]{:S(2)}) collective-permute-start(bf16[2,512,512]{2,1,0:T(8,128)(2,1)} %bitcast.88), channel_id=1, source_target_pairs={{0,16},{16,0},{1,17},{17,1},{2,18},{18,2},{3,19},{19,3},{4,20},{20... | collective-permute-start | bytes 3145736 | tf_op jit(solution)/shard_map/ppermute | solution.py:23
  498.6 19.6 %collective-permute-start.85 = (bf16[1,512,512]{2,1,0:T(8,128)(2,1)S(1)}, bf16[1,512,512]{2,1,0:T(8,128)(2,1)S(1)}, u32[]{:S(2)}, u32[]{:S(2)}) collective-permute-start(bf16[1,512,512]{2,1,0:T(8,128)(2,1)S(1)} %bitcast.90), channel_id=1, source_target_pairs={{0,16},{16,0},{1,17},{17,1},{2,18},{18,2},{3,19},{19,3},{4,20},{20... | collective-permute-start | bytes 1572872 | tf_op jit(solution)/shard_map/ppermute | solution.py:23
  (129 other events, 1271.0 us)

commit v5 on v4

--- a/solution.py
+++ b/solution.py
@@ -149,7 +149,7 @@
         in_specs=[row, flat, flat],
         out_specs=row,
         out_shape=jax.ShapeDtypeStruct((rows, width), BF16),
-        compiler_params=params(16),
+        compiler_params=params(6),
         cost_estimate=cost(rows * width * 10, rows * width * 4),
         name="norm_first",
     )(stream, gain, shift)
@@ -181,7 +181,7 @@
             jax.ShapeDtypeStruct((rows, width), F32),
             jax.ShapeDtypeStruct((rows, width), BF16),
         ],
-        compiler_params=params(16),
+        compiler_params=params(6),
         cost_estimate=cost(rows * width * 12, rows * width * 14),
         name="norm_second",
     )(stream, *terms, gain, shift)
@@ -227,7 +227,7 @@
             jax.ShapeDtypeStruct((2, width), F32),
         ]
         + [jax.ShapeDtypeStruct((rows, width), F32)] * both,
-        compiler_params=params(24),
+        compiler_params=params(10),
         cost_estimate=cost(rows * width * 20, rows * width * 18),
         name="norm_back",
     )(stream, *terms, upper, gain)
@@ -285,7 +285,7 @@
             out_specs=pl.BlockSpec((1, rows, columns), lambda j, h: (j, 0, 0)),
         ),
         out_shape=jax.ShapeDtypeStruct((3, rows, columns), BF16),
-        compiler_params=params(40),
+        compiler_params=params(16),
         cost_estimate=cost(6 * rows * width * columns, 2 * (rows * width + 3 * columns * width)),
         name="qkv_columns",
     )(half, tokens, *pieces, bias, table)
@@ -360,7 +360,7 @@
             jax.ShapeDtypeStruct((rows, columns), BF16),
             jax.ShapeDtypeStruct((groups, length, 2), F32),
         ],
-        compiler_params=params(48),
+        compiler_params=params(20),
         cost_estimate=cost(
             4 * length * length * columns, 16 * rows * columns, columns * length * length / 128
         ),
@@ -480,7 +480,7 @@
             jax.ShapeDtypeStruct((3, rows, columns), BF16),
             jax.ShapeDtypeStruct((3, 1, columns), F32),
         ],
-        compiler_params=params(52),
+        compiler_params=params(20),
         cost_estimate=cost(
             10 * length * length * columns, 40 * rows * columns, columns * length * length / 128
         ),
@@ -526,7 +526,7 @@
             jax.ShapeDtypeStruct((rows, units), BF16),
             jax.ShapeDtypeStruct((2, rows, units), BF16),
         ],
-        compiler_params=params(48),
+        compiler_params=params(20),
         cost_estimate=cost(
             4 * rows * width * units, 4 * width * units + 2 * rows * width, rows * units
         ),
@@ -569,7 +569,7 @@
         + [spec(i) for i in range(len(pieces))],
         out_specs=pl.BlockSpec((rows, block), lambda j: (0, j)),
         out_shape=jax.ShapeDtypeStruct((rows, width), BF16),
-        compiler_params=params(56),
+        compiler_params=params(32),
         cost_estimate=cost(
             2 * count * rows * width * units, 2 * count * (width + rows) * units + 2 * rows * width
         ),
@@ -600,7 +600,7 @@
             out_specs=pl.BlockSpec((1, rows, block), lambda j, q: (j, 0, 0)),
         ),
         out_shape=jax.ShapeDtypeStruct((count, rows, block), BF16),
-        compiler_params=params(40),
+        compiler_params=params(16),
         cost_estimate=cost(
             2 * rows * width * block * count, 2 * width * (rows + block * count)
         ),
@@ -641,7 +641,7 @@
             out_specs=shifted(0, 0),
         ),
         out_shape=jax.ShapeDtypeStruct((k, count, *form), BF16),
-        compiler_params=params(48, 2),
+        compiler_params=params(20, 2),
         cost_estimate=cost(
             2 * k * count * rows * quarter * units,
             2 * k * count * quarter * units * (1 + len(adds)) + 2 * rows * (width + count * units),
@@ -684,7 +684,7 @@
             out_specs=pl.BlockSpec((block, 2, units), lambda h, j, c: (h * steps + j, 0, 0)),
         ),
         out_shape=jax.ShapeDtypeStruct((2 * rows, 2, units), F32),
-        compiler_params=params(40, 2),
+        compiler_params=params(16, 2),
         cost_estimate=cost(rows * units, 24 * rows * units),
         name="join_pairs",
     )(core, *parts, *rests)
@@ -818,14 +818,16 @@
     hops = Gather(low_a, slots)
     rotary_mine = sync([hops], rotary_mine)
     hops.hop()
-    rotary_other = sync([hops], rotary_other)
-    hops.hop()
-    out_half = swap(after(part_of(w_out, 1), rotary_other), "row")
+    rotary_other, out_part, down_part = sync(
+        [hops], rotary_other, part_of(w_out, 1), part_of(w_down, 1)
+    )
+    hops.hop()
+    out_half = swap(out_part, "row")
     w_gate, gate_part, in_half, cot = sync([hops], w_gate, part_of(w_gate, 1), in_half, cot)
     tokens_a = hops.rows()
     pieces_in = (w_in, in_half, swap(in_half, "core"))
     cot_hops = Gather(cot, slots)
-    down_half = swap(after(part_of(w_down, 1), cot), "row")
+    down_half = swap(after(down_part, cot), "row")
     bias = project_bias[0][:, None, :]
     qkv_other = qkv_columns(tokens_a, pieces_in, bias, rotary_mine, (1 - core)[None])
     qkv_from = swap(qkv_other, "core")
@@ -839,13 +841,13 @@
         [jnp.where(core == 0, out_mine, out_from), jnp.where(core == 0, out_from, out_mine)], axis=1
     )
     part_out = to_features(attended[None], [p[None] for p in pieces_out], False)
-    part_out, gate_part = sync([cot_hops], part_out, gate_part)
+    part_out, gate_part = sync([], part_out, gate_part)
     hops = Scatter(part_out, slots)
+    down_half = sync([hops, cot_hops], down_half)
+    hops.hop()
     cot_hops.hop()
-    gate_half = swap(gate_part, "row")
-    down_half = sync([hops, cot_hops], down_half)
-    hops.hop()
-    down_rest = sync([hops], swap(down_half, "core"))
+    gate_half = swap(after(gate_part, down_half), "row")
+    down_rest = sync([hops, cot_hops], swap(down_half, "core"))
     hops.hop()
     pieces_down = (w_down, down_half, down_rest)
     units = w_down.shape[0]

time: 542 us -> 516 us (0.952)
  Pallas kernels: 146 us -> 106 us
  waiting for transfers between devices: 178 us -> 214 us
  other arithmetic: 51 us -> 32.7 us
  local copies, waits for them, and re-layouts: 37.4 us -> 27.6 us
    ppermute x38, waiting for transfers between devices: 61.4 us -> 83.5 us  [swap(): return lax.ppermute(x, axis, [(0, 1), (1, 0)])]
    pallas_call x16, Pallas kernels: 46.1 us -> 26.8 us  [grad_quarters(): pl.pallas_call(body, grid_spec=pltpu.PrefetchScalarGridSpec(num_scalar_pr...]
    pallas_call x4, Pallas kernels: 33.2 us -> 19 us  [to_features(): pl.pallas_call(body, grid=(width // block,), in_specs=[pl.BlockSpec((coun...]
    ppermute x4, waiting for transfers between devices: 18.8 us -> 25 us  [hop(): self.flying = [lax.ppermute(far, 'col', OUT)]]
    ppermute x2, waiting for transfers between devices: 12 us -> 5.79 us  [to_sequence(): lax.ppermute(take(x, (1 - row) * half_rows, half_rows, 0), ('core', 'row'...]
    ppermute x4, waiting for transfers between devices: 14 us -> 20 us  [hop(): lax.ppermute(one, 'col', PAIR)]
    ppermute x4, starting transfers between devices: 8.78 us -> 14.7 us  [__init__(): self.flying = [lax.ppermute(self.part[3], 'col', IN)]]
    unnamed x129 -> x143, local copies, waits for them, and re-layouts: 21.9 us -> 17.4 us
  transfers between devices with their start and end apart: 89 -> 89, of which waited for: 36 -> 35; matrix products, arithmetic and copies ran while one was open for 12% -> 8% of each run, Pallas kernels for 22% -> 16%
where the time goes in v5:
time: 516 us; the launch traced here: 508 us
  waiting for transfers between devices  214 us (41%)
  starting transfers between devices  124 us (24%)
  Pallas kernels  106 us (21%)
  other arithmetic  32.7 us (6%)
  local copies, waits for them, and re-layouts  27.6 us (5%)
    ppermute x38, waiting for transfers between devices, swap(): return lax.ppermute(x, axis, [(0, 1), (1, 0)])  83.5 us
    ppermute x38, starting transfers between devices, swap(): return lax.ppermute(x, axis, [(0, 1), (1, 0)])  29.2 us
    pallas_call x16, Pallas kernels, grad_quarters(): pl.pallas_call(body, grid_spec=pltpu.PrefetchScalarGridSpec(num_scalar_pr...  26.8 us
    ppermute x4, waiting for transfers between devices, hop(): self.flying = [lax.ppermute(far, 'col', OUT)]  25 us
    ppermute x8, waiting for transfers between devices, hop(): self.flying = [lax.ppermute(one, 'col', MID), lax.ppermute(mid, 'col', OUT)]  24.4 us
    ppermute x4, starting transfers between devices, __init__(): self.two = lax.ppermute(self.part[2], 'col', IN)  21.7 us
    ppermute x4, waiting for transfers between devices, __init__(): self.two = lax.ppermute(self.part[2], 'col', IN)  20.8 us
    ppermute x4, waiting for transfers between devices, hop(): lax.ppermute(one, 'col', PAIR)  20 us
  transfers between devices with their start and end apart: 89, of which 35 were waited for; matrix products, arithmetic and copies ran while one was open for 8% of the time, Pallas kernels for 16%

profile of v5, /device:TPU:0, one launch (start us, length us, event | category | flops | bytes accessed | tf_op | source)
XLA Modules:
  0.0 507.6 jit_solution(239952053954990067)
XLA Ops:
  9.2 5.4 %constant_dynamic-slice_fusion.3 = bf16[1,512,2,1408]{3,2,1,0:T(2,128)(2,1)} fusion(bf16[1,1024,2,1408]{3,2,1,0:T(2,128)(2,1)} %param.20, s32[]{:T(128)S(6)} %select_n.340), kind=kLoop, calls=%fused_computation.101 | loop fusion | bytes 5767172 | tf_op jit(solution)/shard_map/dynamic-slice.4
  33.0 17.2 %collective-permute-done.6 = bf16[128,2048]{1,0:T(8,128)(2,1)S(1)} collective-permute-done((bf16[128,2048]{1,0:T(8,128)(2,1)S(1)}, bf16[128,2048]{1,0:T(8,128)(2,1)S(1)}, u32[]{:S(2)}, u32[]{:S(2)}) %collective-permute-start.6) | collective-permute-done | bytes 524320 | tf_op jit(solution)/shard_map/ppermute | solution.py:60
  51.5 5.8 %collective-permute-done.10 = bf16[128,1024]{1,0:T(8,128)(2,1)S(1)} collective-permute-done((bf16[128,1024]{1,0:T(8,128)(2,1)S(1)}, bf16[128,1024]{1,0:T(8,128)(2,1)S(1)}, u32[]{:S(2)}, u32[]{:S(2)}) %collective-permute-start.10) | collective-permute-done | bytes 262176 | tf_op jit(solution)/shard_map/ppermute | solution.py:755
  57.4 6.5 %collective-permute-done.7 = bf16[128,2048]{1,0:T(8,128)(2,1)S(1)} collective-permute-done((bf16[128,2048]{1,0:T(8,128)(2,1)S(1)}, bf16[128,2048]{1,0:T(8,128)(2,1)S(1)}, u32[]{:S(2)}, u32[]{:S(2)}) %collective-permute-start.7) | collective-permute-done | bytes 524320 | tf_op jit(solution)/shard_map/ppermute | solution.py:64
  77.4 7.9 %attend.1 = (bf16[512,256]{1,0:T(8,128)(2,1)S(1)}, bf16[512,256]{1,0:T(8,128)(2,1)S(1)}, f32[2,1024,2]{2,1,0:T(8,128)S(1)}) custom-call(s32[5]{0:T(128)S(1)} %pad_add_fusion.order_ref, bf16[3,512,256]{2,1,0:T(8,128)(2,1)S(1)} %qkv_columns.2.mine_ref, bf16[3,512,256]{2,1,0:T(8,128)(2,1)S(1)} %collective-permute-done.14.other_ref), custom_call_target="tpu_custom_call" | custom-call | flops 134217728 | bytes 262144 | tf_op jit(solution)/shard_map/attend/pallas_call | solution.py:346
  91.3 8.3 %collective-permute-start.18 = (bf16[128,2048]{1,0:T(8,128)(2,1)S(1)}, bf16[128,2048]{1,0:T(8,128)(2,1)S(1)}, u32[]{:S(2)}, u32[]{:S(2)}) collective-permute-start(bf16[128,2048]{1,0:T(8,128)(2,1)S(1)} %slice.154), channel_id=1, source_target_pairs={{0,1},{3,2},{4,5},{7,6},{8,9},{11,10},{12,13},{15,14},{16,17},{19,... | collective-permute-start | bytes 1572872 | tf_op jit(solution)/shard_map/ppermute | solution.py:80
  99.6 16.4 %collective-permute-done.21.refs_1_ = bf16[1408,512]{1,0:T(8,128)(2,1)S(1)} collective-permute-done((bf16[1408,512]{1,0:T(8,128)(2,1)S(1)}, bf16[1408,512]{1,0:T(8,128)(2,1)S(1)}, u32[]{:S(2)}, u32[]{:S(2)}) %collective-permute-start.21) | collective-permute-done | bytes 1441824 | tf_op jit(solution)/shard_map/ppermute | solution.py:23
  123.9 8.3 %collective-permute-done.23 = bf16[128,2048]{1,0:T(8,128)(2,1)S(1)} collective-permute-done((bf16[128,2048]{1,0:T(8,128)(2,1)S(1)}, bf16[128,2048]{1,0:T(8,128)(2,1)S(1)}, u32[]{:S(2)}, u32[]{:S(2)}) %collective-permute-start.23) | collective-permute-done | bytes 524320 | tf_op jit(solution)/shard_map/ppermute | solution.py:81
  142.4 7.2 %collective-permute-done.26.b_ref = bf16[128,2048]{1,0:T(8,128)(2,1)S(1)} collective-permute-done((bf16[128,2048]{1,0:T(8,128)(2,1)S(1)}, bf16[128,2048]{1,0:T(8,128)(2,1)S(1)}, u32[]{:S(2)}, u32[]{:S(2)}) %collective-permute-start.26) | collective-permute-done | bytes 524320 | tf_op jit(solution)/shard_map/ppermute | solution.py:91
  156.0 9.3 %collective-permute-done.28 = bf16[128,2048]{1,0:T(8,128)(2,1)S(1)} collective-permute-done((bf16[128,2048]{1,0:T(8,128)(2,1)S(1)}, bf16[128,2048]{1,0:T(8,128)(2,1)S(1)}, u32[]{:S(2)}, u32[]{:S(2)}) %collective-permute-start.28) | collective-permute-done | bytes 524320 | tf_op jit(solution)/shard_map/ppermute | solution.py:52
  167.3 19.1 %collective-permute-done.32.refs_1_ = bf16[2,512,1408]{2,1,0:T(8,128)(2,1)S(1)} collective-permute-done((bf16[2,512,1408]{2,1,0:T(8,128)(2,1)S(1)}, bf16[2,512,1408]{2,1,0:T(8,128)(2,1)S(1)}, u32[]{:S(2)}, u32[]{:S(2)}) %collective-permute-start.32) | collective-permute-done | bytes 2883616 | tf_op jit(solution)/shard_map/ppermute | solution.py:23
  188.4 14.3 %collective-permute-done.33 = bf16[128,2048]{1,0:T(8,128)(2,1)S(1)} collective-permute-done((bf16[128,2048]{1,0:T(8,128)(2,1)S(1)}, bf16[128,2048]{1,0:T(8,128)(2,1)S(1)}, u32[]{:S(2)}, u32[]{:S(2)}) %collective-permute-start.33) | collective-permute-done | bytes 524320 | tf_op jit(solution)/shard_map/ppermute | solution.py:64
  203.1 10.3 %feed_forward.1 = (bf16[512,1408]{1,0:T(8,128)(2,1)S(1)}, bf16[2,512,1408]{2,1,0:T(8,128)(2,1)S(1)}) custom-call(bf16[512,2048]{1,0:T(8,128)(2,1)S(1)} %pad_maximum_fusion.2.x_ref, bf16[2,1024,1408]{2,1,0:T(8,128)(2,1)S(1)} %bitcast.73, bf16[2,512,1408]{2,1,0:T(8,128)(2,1)S(1)} %collective-permute-done.32.refs_1_, ...), custom_call_target="tpu_custom_call" | custom-call | flops 738197504 | bytes 1703936 | tf_op jit(solution)/shard_map/feed_forward/pallas_call | solution.py:515
  215.2 8.0 %to_features.5 = bf16[512,2048]{1,0:T(8,128)(2,1)S(1)} custom-call(bf16[2,512,1408]{2,1,0:T(8,128)(2,1)S(1)} %get-tuple-element.205.v_ref.y_ref, bf16[2,1024,1408]{2,1,0:T(8,128)(2,1)S(1)} %bitcast.74, bf16[2,512,1408]{2,1,0:T(8,128)(2,1)S(1)} %copy-done.20, bf16[2,512,1408]{2,1,0:T(8,128)(2,1)S(1)} %collective-permute-done.34.refs_2_), custom_call_target="tpu_custom_call" | custom-call | flops 738197504 | bytes 2064384 | tf_op jit(solution)/shard_map/to_features/pallas_call | solution.py:565
  237.2 7.4 %collective-permute-start.37 = (bf16[128,2048]{1,0:T(8,128)(2,1)S(1)}, bf16[128,2048]{1,0:T(8,128)(2,1)S(1)}, u32[]{:S(2)}, u32[]{:S(2)}) collective-permute-start(bf16[128,2048]{1,0:T(8,128)(2,1)S(1)} %get-tuple-element.315), channel_id=1, source_target_pairs={{0,1},{3,2},{4,5},{7,6},{8,9},{11,10},{12,13},{15,14},{16,17},{19,... | collective-permute-start | bytes 1572872 | tf_op jit(solution)/shard_map/ppermute | solution.py:81
  262.9 7.8 %collective-permute-done.40.b_ref = bf16[128,2048]{1,0:T(8,128)(2,1)S(1)} collective-permute-done((bf16[128,2048]{1,0:T(8,128)(2,1)S(1)}, bf16[128,2048]{1,0:T(8,128)(2,1)S(1)}, u32[]{:S(2)}, u32[]{:S(2)}) %collective-permute-start.40) | collective-permute-done | bytes 524320 | tf_op jit(solution)/shard_map/ppermute | solution.py:91
  296.7 7.2 %collective-permute-done.46 = bf16[128,2048]{1,0:T(8,128)(2,1)S(1)} collective-permute-done((bf16[128,2048]{1,0:T(8,128)(2,1)S(1)}, bf16[128,2048]{1,0:T(8,128)(2,1)S(1)}, u32[]{:S(2)}, u32[]{:S(2)}) %collective-permute-start.46) | collective-permute-done | bytes 524320 | tf_op jit(solution)/shard_map/ppermute | solution.py:60
  307.2 12.0 %collective-permute-done.48.refs_1_ = bf16[1,1,512,1408]{3,2,1,0:T(8,128)(2,1)} collective-permute-done((bf16[1,1,512,1408]{3,2,1,0:T(8,128)(2,1)S(1)}, bf16[1,1,512,1408]{3,2,1,0:T(8,128)(2,1)}, u32[]{:S(2)}, u32[]{:S(2)}) %collective-permute-start.48) | collective-permute-done | bytes 1441824 | tf_op jit(solution)/shard_map/ppermute | solution.py:23
  336.5 14.2 %attend_back.1 = (bf16[3,512,256]{2,1,0:T(8,128)(2,1)S(1)}, bf16[3,512,256]{2,1,0:T(8,128)(2,1)S(1)}, f32[3,1,256]{2,1,0:T(1,128)S(1)}) custom-call(s32[5]{0:T(128)S(1)} %pad_add_fusion.order_ref, bf16[3,512,256]{2,1,0:T(8,128)(2,1)S(1)} %copy-done.26, bf16[3,512,256]{2,1,0:T(8,128)(2,1)S(1)} %collective-permute-done.14.other_ref, ...), custom_call_target="tpu_custom_call" | custom-call | flops 335544320 | bytes 655360 | tf_op jit(solution)/shard_map/attend_back/pallas_call | solution.py:456
  357.0 11.8 %collective-permute-done.57 = bf16[1,512,1408]{2,1,0:T(8,128)(2,1)S(1)} collective-permute-done((bf16[1,512,1408]{2,1,0:T(8,128)(2,1)S(1)}, bf16[1,512,1408]{2,1,0:T(8,128)(2,1)S(1)}, u32[]{:S(2)}, u32[]{:S(2)}) %collective-permute-start.57) | collective-permute-done | bytes 1441824 | tf_op jit(solution)/shard_map/ppermute | solution.py:23
  394.6 5.2 %collective-permute-done.60 = bf16[128,2048]{1,0:T(8,128)(2,1)S(1)} collective-permute-done((bf16[128,2048]{1,0:T(8,128)(2,1)S(1)}, bf16[128,2048]{1,0:T(8,128)(2,1)S(1)}, u32[]{:S(2)}, u32[]{:S(2)}) %collective-permute-start.60) | collective-permute-done | bytes 524320 | tf_op jit(solution)/shard_map/ppermute | solution.py:80
  400.5 7.1 %collective-permute-start.62 = (bf16[128,2048]{1,0:T(8,128)(2,1)S(1)}, bf16[128,2048]{1,0:T(8,128)(2,1)S(1)}, u32[]{:S(2)}, u32[]{:S(2)}) collective-permute-start(bf16[128,2048]{1,0:T(8,128)(2,1)S(1)} %get-tuple-element.308), channel_id=1, source_target_pairs={{0,1},{3,2},{4,5},{7,6},{8,9},{11,10},{12,13},{15,14},{16,17},{19,... | collective-permute-start | bytes 1572872 | tf_op jit(solution)/shard_map/ppermute | solution.py:81
  460.9 9.5 %join_pairs.1 = f32[1024,2,1408]{2,1,0:T(2,128)} custom-call(s32[1]{0:T(128)} %bitcast.12.half_ref.q_ref.index_ref.core_ref, bf16[1,512,1408]{2,1,0:T(8,128)(2,1)} %add_convert_fusion.1.refs_0_, bf16[1,512,1408]{2,1,0:T(8,128)(2,1)} %add_convert_fusion.refs_1_, bf16[1,512,1408]{2,1,0:T(8,128)(2,1)} %collective-permute-done.71.refs_2_, ...), custom_call_target="tpu_custom_call" | custom-call | flops 90112 | bytes 2162688 | tf_op jit(solution)/shard_map/join_pairs/pallas_call | solution.py:678
  477.6 6.2 %collective-permute-done.80 = f32[14,1024]{1,0:T(8,128)S(1)} collective-permute-done((f32[14,1024]{1,0:T(8,128)S(1)}, f32[14,1024]{1,0:T(8,128)S(1)}, u32[]{:S(2)}, u32[]{:S(2)}) %collective-permute-start.80) | collective-permute-done | bytes 57376 | tf_op jit(solution)/shard_map/ppermute | solution.py:996
  (433 shorter events, 272.3 us)
Async XLA Ops:
  18.3 45.7 %collective-permute-start.8 = (bf16[3,512,512]{2,1,0:T(8,128)(2,1)S(1)}, bf16[3,512,512]{2,1,0:T(8,128)(2,1)S(1)}, u32[]{:S(2)}, u32[]{:S(2)}) collective-permute-start(bf16[3,512,512]{2,1,0:T(8,128)(2,1)S(1)} %dynamic-slice_bitcast_fusion), channel_id=1, source_target_pairs={{0,4},{4,0},{1,5},{5,1},{2,6},{6,2},{3,7},{7,3},{8,12},{12,8},{9,1... | collective-permute-start | bytes 4718600 | tf_op jit(solution)/shard_map/ppermute | solution.py:23
  30.6 19.6 %collective-permute-start.6 = (bf16[128,2048]{1,0:T(8,128)(2,1)S(1)}, bf16[128,2048]{1,0:T(8,128)(2,1)S(1)}, u32[]{:S(2)}, u32[]{:S(2)}) collective-permute-start(bf16[128,2048]{1,0:T(8,128)(2,1)S(1)} %collective-permute-done.4), channel_id=1, source_target_pairs={{1,0},{2,3},{5,4},{6,7},{9,8},{10,11},{13,12},{14,15},{17,16},{18,... | collective-permute-start | bytes 1572872 | tf_op jit(solution)/shard_map/ppermute | solution.py:60
  32.1 25.2 %collective-permute-start.10 = (bf16[128,1024]{1,0:T(8,128)(2,1)S(1)}, bf16[128,1024]{1,0:T(8,128)(2,1)S(1)}, u32[]{:S(2)}, u32[]{:S(2)}) collective-permute-start(bf16[128,1024]{1,0:T(8,128)(2,1)S(1)} %get-tuple-element.347), channel_id=1, source_target_pairs={{0,8},{4,0},{8,12},{12,4},{1,9},{5,1},{9,13},{13,5},{2,10},{6,2},{... | collective-permute-start | bytes 786440 | tf_op jit(solution)/shard_map/ppermute | solution.py:755
  32.1 25.2 %collective-permute-start.9 = (bf16[128,1024]{1,0:T(8,128)(2,1)S(1)}, bf16[128,1024]{1,0:T(8,128)(2,1)S(1)}, u32[]{:S(2)}, u32[]{:S(2)}) collective-permute-start(bf16[128,1024]{1,0:T(8,128)(2,1)S(1)} %get-tuple-element.346), channel_id=1, source_target_pairs={{0,0},{4,8},{8,4},{12,12},{1,1},{5,9},{9,5},{13,13},{2,2},{6,10},{... | collective-permute-start | bytes 786440 | tf_op jit(solution)/shard_map/ppermute | solution.py:754
  73.9 42.1 %collective-permute-start.21 = (bf16[1408,512]{1,0:T(8,128)(2,1)S(1)}, bf16[1408,512]{1,0:T(8,128)(2,1)S(1)}, u32[]{:S(2)}, u32[]{:S(2)}) collective-permute-start(bf16[1408,512]{1,0:T(8,128)(2,1)S(1)} %dynamic-slice_bitcast_fusion.1), channel_id=1, source_target_pairs={{0,4},{4,0},{1,5},{5,1},{2,6},{6,2},{3,7},{7,3},{8,12},{12,8},{9,1... | collective-permute-start | bytes 4325384 | tf_op jit(solution)/shard_map/ppermute | solution.py:23
  86.9 29.0 %collective-permute-start.19 = (bf16[128,2048]{1,0:T(8,128)(2,1)S(1)}, bf16[128,2048]{1,0:T(8,128)(2,1)S(1)}, u32[]{:S(2)}, u32[]{:S(2)}) collective-permute-start(bf16[128,2048]{1,0:T(8,128)(2,1)S(1)} %collective-permute-done.11), channel_id=1, source_target_pairs={{1,2},{2,1},{5,6},{6,5},{9,10},{10,9},{13,14},{14,13},{17,18},{18,... | collective-permute-start | bytes 1572872 | tf_op jit(solution)/shard_map/ppermute | solution.py:60
  87.6 28.4 %collective-permute-start.20 = (bf16[128,2048]{1,0:T(8,128)(2,1)S(1)}, bf16[128,2048]{1,0:T(8,128)(2,1)S(1)}, u32[]{:S(2)}, u32[]{:S(2)}) collective-permute-start(bf16[128,2048]{1,0:T(8,128)(2,1)S(1)} %collective-permute-done.12), channel_id=1, source_target_pairs={{1,0},{2,3},{5,4},{6,7},{9,8},{10,11},{13,12},{14,15},{17,16},{18,... | collective-permute-start | bytes 1572872 | tf_op jit(solution)/shard_map/ppermute | solution.py:60
  91.3 24.7 %collective-permute-start.18 = (bf16[128,2048]{1,0:T(8,128)(2,1)S(1)}, bf16[128,2048]{1,0:T(8,128)(2,1)S(1)}, u32[]{:S(2)}, u32[]{:S(2)}) collective-permute-start(bf16[128,2048]{1,0:T(8,128)(2,1)S(1)} %slice.154), channel_id=1, source_target_pairs={{0,1},{3,2},{4,5},{7,6},{8,9},{11,10},{12,13},{15,14},{16,17},{19,... | collective-permute-start | bytes 1572872 | tf_op jit(solution)/shard_map/ppermute | solution.py:80
  116.0 20.4 %collective-permute-start.25 = (bf16[1408,512]{1,0:T(8,128)(2,1)S(1)}, bf16[1408,512]{1,0:T(8,128)(2,1)S(1)}, u32[]{:S(2)}, u32[]{:S(2)}) collective-permute-start(bf16[1408,512]{1,0:T(8,128)(2,1)S(1)} %collective-permute-done.21.refs_1_), channel_id=1, source_target_pairs={{0,8},{8,0},{1,9},{9,1},{2,10},{10,2},{3,11},{11,3},{4,12},{12,4},... | collective-permute-start | bytes 4325384 | tf_op jit(solution)/shard_map/ppermute | solution.py:23
  122.0 64.4 %collective-permute-start.32 = (bf16[2,512,1408]{2,1,0:T(8,128)(2,1)S(1)}, bf16[2,512,1408]{2,1,0:T(8,128)(2,1)S(1)}, u32[]{:S(2)}, u32[]{:S(2)}) collective-permute-start(bf16[2,512,1408]{2,1,0:T(8,128)(2,1)S(1)} %bitcast.107), channel_id=1, source_target_pairs={{0,4},{4,0},{1,5},{5,1},{2,6},{6,2},{3,7},{7,3},{8,12},{12,8},{9,1... | collective-permute-start | bytes 8650760 | tf_op jit(solution)/shard_map/ppermute | solution.py:23
  165.3 21.1 %collective-permute-start.30 = (bf16[128,2048]{1,0:T(8,128)(2,1)S(1)}, bf16[128,2048]{1,0:T(8,128)(2,1)S(1)}, u32[]{:S(2)}, u32[]{:S(2)}) collective-permute-start(bf16[128,2048]{1,0:T(8,128)(2,1)S(1)} %collective-permute-done.28), channel_id=1, source_target_pairs={{1,2},{2,1},{5,6},{6,5},{9,10},{10,9},{13,14},{14,13},{17,18},{18,... | collective-permute-start | bytes 1572872 | tf_op jit(solution)/shard_map/ppermute | solution.py:60
  166.0 20.4 %collective-permute-start.31 = (bf16[128,2048]{1,0:T(8,128)(2,1)S(1)}, bf16[128,2048]{1,0:T(8,128)(2,1)S(1)}, u32[]{:S(2)}, u32[]{:S(2)}) collective-permute-start(bf16[128,2048]{1,0:T(8,128)(2,1)S(1)} %collective-permute-done.29), channel_id=1, source_target_pairs={{1,0},{2,3},{5,4},{6,7},{9,8},{10,11},{13,12},{14,15},{17,16},{18,... | collective-permute-start | bytes 1572872 | tf_op jit(solution)/shard_map/ppermute | solution.py:60
  235.9 19.7 %collective-permute-start.39 = (bf16[2,2,512,1408]{3,2,1,0:T(8,128)(2,1)S(1)}, bf16[2,2,512,1408]{3,2,1,0:T(8,128)(2,1)S(1)}, u32[]{:S(2)}, u32[]{:S(2)}) collective-permute-start(bf16[2,2,512,1408]{3,2,1,0:T(8,128)(2,1)S(1)} %grad_quarters.17), channel_id=1, source_target_pairs={{0,8},{8,0},{1,9},{9,1},{2,10},{10,2},{3,11},{11,3},{4,12},{12,4},... | collective-permute-start | bytes 17301512 | tf_op jit(solution)/shard_map/ppermute | solution.py:23
  255.6 34.8 %collective-permute-start.44 = (bf16[1,1,1408,512]{3,2,1,0:T(8,128)(2,1)}, bf16[1,1,1408,512]{3,2,1,0:T(8,128)(2,1)}, u32[]{:S(2)}, u32[]{:S(2)}) collective-permute-start(bf16[1,1,1408,512]{3,2,1,0:T(8,128)(2,1)} %grad_quarters.18), channel_id=1, source_target_pairs={{0,4},{4,0},{1,5},{5,1},{2,6},{6,2},{3,7},{7,3},{8,12},{12,8},{9,1... | collective-permute-start | bytes 4325384 | tf_op jit(solution)/shard_map/ppermute | solution.py:23
  278.7 40.5 %collective-permute-start.48 = (bf16[1,1,512,1408]{3,2,1,0:T(8,128)(2,1)S(1)}, bf16[1,1,512,1408]{3,2,1,0:T(8,128)(2,1)}, u32[]{:S(2)}, u32[]{:S(2)}) collective-permute-start(bf16[1,1,512,1408]{3,2,1,0:T(8,128)(2,1)S(1)} %grad_quarters.19), channel_id=1, source_target_pairs={{0,4},{4,0},{1,5},{5,1},{2,6},{6,2},{3,7},{7,3},{8,12},{12,8},{9,1... | collective-permute-start | bytes 4325384 | tf_op jit(solution)/shard_map/ppermute | solution.py:23
  303.9 28.4 %collective-permute-start.50 = (bf16[1,1408,512]{2,1,0:T(8,128)(2,1)S(1)}, bf16[1,1408,512]{2,1,0:T(8,128)(2,1)S(1)}, u32[]{:S(2)}, u32[]{:S(2)}) collective-permute-start(bf16[1,1408,512]{2,1,0:T(8,128)(2,1)S(1)} %bitcast.87), channel_id=1, source_target_pairs={{0,16},{16,0},{1,17},{17,1},{2,18},{18,2},{3,19},{19,3},{4,20},{20... | collective-permute-start | bytes 4325384 | tf_op jit(solution)/shard_map/ppermute | solution.py:23
  319.3 31.5 %collective-permute-start.53 = (bf16[1,1,512,1408]{3,2,1,0:T(8,128)(2,1)S(1)}, bf16[1,1,512,1408]{3,2,1,0:T(8,128)(2,1)S(1)}, u32[]{:S(2)}, u32[]{:S(2)}) collective-permute-start(bf16[1,1,512,1408]{3,2,1,0:T(8,128)(2,1)S(1)} %grad_quarters.20), channel_id=1, source_target_pairs={{0,4},{4,0},{1,5},{5,1},{2,6},{6,2},{3,7},{7,3},{8,12},{12,8},{9,1... | collective-permute-start | bytes 4325384 | tf_op jit(solution)/shard_map/ppermute | solution.py:23
  332.3 18.5 %collective-permute-start.52 = (bf16[2,1,512,512]{3,2,1,0:T(8,128)(2,1)S(1)}, bf16[2,1,512,512]{3,2,1,0:T(8,128)(2,1)S(1)}, u32[]{:S(2)}, u32[]{:S(2)}) collective-permute-start(bf16[2,1,512,512]{3,2,1,0:T(8,128)(2,1)S(1)} %grad_quarters.22), channel_id=1, source_target_pairs={{0,8},{8,0},{1,9},{9,1},{2,10},{10,2},{3,11},{11,3},{4,12},{12,4},... | collective-permute-start | bytes 3145736 | tf_op jit(solution)/shard_map/ppermute | solution.py:23
  334.9 33.8 %collective-permute-start.57 = (bf16[1,512,1408]{2,1,0:T(8,128)(2,1)S(1)}, bf16[1,512,1408]{2,1,0:T(8,128)(2,1)S(1)}, u32[]{:S(2)}, u32[]{:S(2)}) collective-permute-start(bf16[1,512,1408]{2,1,0:T(8,128)(2,1)S(1)} %bitcast.89), channel_id=1, source_target_pairs={{0,16},{16,0},{1,17},{17,1},{2,18},{18,2},{3,19},{19,3},{4,20},{20... | collective-permute-start | bytes 4325384 | tf_op jit(solution)/shard_map/ppermute | solution.py:23
  374.8 36.0 %collective-permute-start.64 = (bf16[1,512,1408]{2,1,0:T(8,128)(2,1)S(1)}, bf16[1,512,1408]{2,1,0:T(8,128)(2,1)S(1)}, u32[]{:S(2)}, u32[]{:S(2)}) collective-permute-start(bf16[1,512,1408]{2,1,0:T(8,128)(2,1)S(1)} %bitcast.91), channel_id=1, source_target_pairs={{0,16},{16,0},{1,17},{17,1},{2,18},{18,2},{3,19},{19,3},{4,20},{20... | collective-permute-start | bytes 4325384 | tf_op jit(solution)/shard_map/ppermute | solution.py:23
  391.8 26.2 %collective-permute-start.63 = (bf16[1,2,512,512]{3,2,1,0:T(8,128)(2,1)S(1)}, bf16[1,2,512,512]{3,2,1,0:T(8,128)(2,1)S(1)}, u32[]{:S(2)}, u32[]{:S(2)}) collective-permute-start(bf16[1,2,512,512]{3,2,1,0:T(8,128)(2,1)S(1)} %grad_quarters.27), channel_id=1, source_target_pairs={{0,4},{4,0},{1,5},{5,1},{2,6},{6,2},{3,7},{7,3},{8,12},{12,8},{9,1... | collective-permute-start | bytes 3145736 | tf_op jit(solution)/shard_map/ppermute | solution.py:23
  422.6 19.2 %collective-permute-start.69 = (bf16[1,1408,512]{2,1,0:T(8,128)(2,1)}, bf16[1,1408,512]{2,1,0:T(8,128)(2,1)}, u32[]{:S(2)}, u32[]{:S(2)}) collective-permute-start(bf16[1,1408,512]{2,1,0:T(8,128)(2,1)} %add_convert_fusion.2), channel_id=1, source_target_pairs={{0,8},{8,0},{1,9},{9,1},{2,10},{10,2},{3,11},{11,3},{4,12},{12,4},... | collective-permute-start | bytes 4325384 | tf_op jit(solution)/shard_map/ppermute | solution.py:23
  432.7 37.7 %collective-permute-start.79 = (bf16[2,512,512]{2,1,0:T(8,128)(2,1)}, bf16[2,512,512]{2,1,0:T(8,128)(2,1)S(1)}, u32[]{:S(2)}, u32[]{:S(2)}) collective-permute-start(bf16[2,512,512]{2,1,0:T(8,128)(2,1)} %bitcast.95), channel_id=1, source_target_pairs={{0,16},{16,0},{1,17},{17,1},{2,18},{18,2},{3,19},{19,3},{4,20},{20... | collective-permute-start | bytes 3145736 | tf_op jit(solution)/shard_map/ppermute | solution.py:23
  472.9 20.4 %collective-permute-start.85 = (bf16[1,512,512]{2,1,0:T(8,128)(2,1)}, bf16[1,512,512]{2,1,0:T(8,128)(2,1)S(1)}, u32[]{:S(2)}, u32[]{:S(2)}) collective-permute-start(bf16[1,512,512]{2,1,0:T(8,128)(2,1)} %bitcast.97), channel_id=1, source_target_pairs={{0,16},{16,0},{1,17},{17,1},{2,18},{18,2},{3,19},{19,3},{4,20},{20... | collective-permute-start | bytes 1572872 | tf_op jit(solution)/shard_map/ppermute | solution.py:23
  (136 other events, 1620.8 us)

commit v6 on v5

--- a/solution.py
+++ b/solution.py
@@ -941,13 +941,13 @@
     out_arrived = swap(out_oth, "row")
     gate_other[1] = y_swap(gate_own[1])
     part_a = to_features(mixed, pieces_in, True)
-    part_a, in_got, out_arrived = sync([down_hops], part_a, in_got, out_arrived)
+    part_a, in_got, out_arrived = sync([], part_a, in_got, out_arrived)
     hops = Scatter(part_a, slots)
     spans = (dict(at=0, first=0, count=2), dict(at=2, first=2, count=1))
     in_oth = [for_row(tokens_a, mixed, True, in_got, **span) for span in spans]
     in_arrived = [swap(x, "row") for x in in_oth]
     out_own = for_y(g2_rows, attended[None], False, out_got, out_arrived)
-    *in_oth, out_own = sync([hops], *in_oth, out_own)
+    *in_oth, out_own = sync([hops, down_hops], *in_oth, out_own)
     hops.hop()
     down_total = y_total(down_own, down_other)
     gate_total = [y_total(gate_own[0], gate_other[0]), None]
@@ -987,38 +987,35 @@
         arrived = lax.ppermute(total, "col", PAIR)
         arrived, input_grad, down_grad = sync([], arrived, input_grad, down_grad)
         total = total + arrived
-        arrived = lax.ppermute(total, "col", MID)
-        down_hops.flying = list(tie(down_hops.flying, input_grad))
+        arrived = sync([], lax.ppermute(total, "col", MID))
+        total = total + arrived
+        outer, in_other[0], gate_total[0] = sync(
+            [], lax.ppermute(total, "col", OUT), in_other[0], gate_total[0]
+        )
+        total = jnp.where((place == 0) | (place == 3), outer, total)
+        down_hops.flying = list(tie(down_hops.flying, outer))
         down_hops.hop()
+        arrived = swap(total, "core")
         gate_grad = join_pairs(core[None], gate_total, gate_rest)
-        arrived, gate_grad, in_other[0] = sync([down_hops], arrived, gate_grad, in_other[0])
+        arrived, gate_grad, in_other[1] = sync([down_hops], arrived, gate_grad, in_other[1])
         total = total + arrived
-        outer = lax.ppermute(total, "col", OUT)
-        layer_low = (residual + sum(t.astype(F32) for t in down_hops.terms())).astype(BF16)
-        in_total = [y_total(in_own[0], in_other[0])]
-        in_rest = [swap(in_total[0], "core")]
-        outer, layer_low, in_rest[0] = sync([], outer, layer_low, in_rest[0])
-        total = jnp.where((place == 0) | (place == 3), outer, total)
     else:
         gate_grad = join_pairs(core[None], gate_total, gate_rest)
-        layer_low = (residual + sum(t.astype(F32) for t in down_hops.terms())).astype(BF16)
-        in_total = [y_total(in_own[0], in_other[0])]
-        in_rest = [swap(in_total[0], "core")]
         total = lax.psum(total, "col")
+        total = total + swap(total, "core")
+    cut = own.shape[0] + bias_all.shape[0]
+    arrived = swap(jnp.concatenate([total[cut:], total[own.shape[0] : cut]], axis=0), "row")
+    layer_low = (residual + sum(t.astype(F32) for t in down_hops.terms())).astype(BF16)
+    in_total = [y_total(x, o) for x, o in zip(in_own, in_other)]
+    in_rest = [swap(x, "core") for x in in_total]
+    arrived, layer_low, *in_rest = sync([], arrived, layer_low, *in_rest)
+    total = total[:cut] + arrived
+    vectors = lax.psum(total, "y") if y_count != 2 else total + swap(total, "y")
     layer_out = from_sequence(layer_low)
     out_grad = join(out_total, out_rest, 2)[0]
-    arrived = swap(total, "core")
-    arrived, layer_out, in_other[1], out_grad = sync([], arrived, layer_out, in_other[1], out_grad)
-    total = total + arrived
-    cut = own.shape[0] + bias_all.shape[0]
-    sent = jnp.concatenate([total[cut:], total[own.shape[0] : cut]], axis=0)
-    total = total[:cut] + swap(sent, "row")
-    vectors = lax.psum(total, "y") if y_count != 2 else total + swap(total, "y")
+    in_grad = jnp.concatenate([join(x, r, 1) for x, r in zip(in_total, in_rest)], axis=0)
     bias_grad = take(vectors[4:].reshape(3, -1), place * 2 * columns, 2 * columns, 1)
     input_grad = input_grad.astype(F32)
-    in_total.append(y_total(in_own[1], in_other[1]))
-    in_rest.append(swap(in_total[1], "core"))
-    in_grad = jnp.concatenate([join(x, r, 1) for x, r in zip(in_total, in_rest)], axis=0)
     return (
         layer_out[None],
         input_grad,

time: 516 us -> 510 us (0.988)
    unnamed x143 -> x129, local copies, waits for them, and re-layouts: 17.4 us -> 15.5 us
  transfers between devices with their start and end apart: 89 -> 89, of which waited for: 35 -> 34; matrix products, arithmetic and copies ran while one was open for 8% -> 9% of each run, Pallas kernels for 16% -> 16%
where the time goes in v6:
time: 510 us; the launch traced here: 500 us
  waiting for transfers between devices  213 us (42%)
  starting transfers between devices  121 us (24%)
  Pallas kernels  105 us (21%)
  other arithmetic  32.6 us (6%)
  local copies, waits for them, and re-layouts  25.7 us (5%)
    ppermute x38, waiting for transfers between devices, swap(): return lax.ppermute(x, axis, [(0, 1), (1, 0)])  82.2 us
    ppermute x38, starting transfers between devices, swap(): return lax.ppermute(x, axis, [(0, 1), (1, 0)])  27.6 us
    pallas_call x16, Pallas kernels, grad_quarters(): pl.pallas_call(body, grid_spec=pltpu.PrefetchScalarGridSpec(num_scalar_pr...  25.3 us
    ppermute x4, waiting for transfers between devices, hop(): self.flying = [lax.ppermute(far, 'col', OUT)]  25 us
    ppermute x8, waiting for transfers between devices, hop(): self.flying = [lax.ppermute(one, 'col', MID), lax.ppermute(mid, 'col', OUT)]  24.7 us
    ppermute x4, starting transfers between devices, __init__(): self.two = lax.ppermute(self.part[2], 'col', IN)  21.8 us
    ppermute x4, waiting for transfers between devices, hop(): lax.ppermute(one, 'col', PAIR)  20.4 us
    pallas_call x4, Pallas kernels, to_features(): pl.pallas_call(body, grid=(width // block,), in_specs=[pl.BlockSpec((coun...  19 us
  transfers between devices with their start and end apart: 89, of which 34 were waited for; matrix products, arithmetic and copies ran while one was open for 9% of the time, Pallas kernels for 16%

profile of v6, /device:TPU:0, one launch (start us, length us, event | category | flops | bytes accessed | tf_op | source)
XLA Modules:
  0.0 499.7 jit_solution(11284484216274836043)
XLA Ops:
  33.0 17.2 %collective-permute-done.6 = bf16[128,2048]{1,0:T(8,128)(2,1)S(1)} collective-permute-done((bf16[128,2048]{1,0:T(8,128)(2,1)S(1)}, bf16[128,2048]{1,0:T(8,128)(2,1)S(1)}, u32[]{:S(2)}, u32[]{:S(2)}) %collective-permute-start.6) | collective-permute-done | bytes 524320 | tf_op jit(solution)/shard_map/ppermute | solution.py:60
  51.5 5.8 %collective-permute-done.10 = bf16[128,1024]{1,0:T(8,128)(2,1)S(1)} collective-permute-done((bf16[128,1024]{1,0:T(8,128)(2,1)S(1)}, bf16[128,1024]{1,0:T(8,128)(2,1)S(1)}, u32[]{:S(2)}, u32[]{:S(2)}) %collective-permute-start.10) | collective-permute-done | bytes 262176 | tf_op jit(solution)/shard_map/ppermute | solution.py:755
  57.4 6.5 %collective-permute-done.7 = bf16[128,2048]{1,0:T(8,128)(2,1)S(1)} collective-permute-done((bf16[128,2048]{1,0:T(8,128)(2,1)S(1)}, bf16[128,2048]{1,0:T(8,128)(2,1)S(1)}, u32[]{:S(2)}, u32[]{:S(2)}) %collective-permute-start.7) | collective-permute-done | bytes 524320 | tf_op jit(solution)/shard_map/ppermute | solution.py:64
  77.4 7.9 %attend.1 = (bf16[512,256]{1,0:T(8,128)(2,1)S(1)}, bf16[512,256]{1,0:T(8,128)(2,1)S(1)}, f32[2,1024,2]{2,1,0:T(8,128)S(1)}) custom-call(s32[5]{0:T(128)S(1)} %pad_add_fusion.1.order_ref, bf16[3,512,256]{2,1,0:T(8,128)(2,1)S(1)} %qkv_columns.2.mine_ref, bf16[3,512,256]{2,1,0:T(8,128)(2,1)S(1)} %collective-permute-done.14.other_ref), custom_call_target="tpu_custom_call" | custom-call | flops 134217728 | bytes 262144 | tf_op jit(solution)/shard_map/attend/pallas_call | solution.py:346
  90.6 8.1 %collective-permute-start.18 = (bf16[128,2048]{1,0:T(8,128)(2,1)S(1)}, bf16[128,2048]{1,0:T(8,128)(2,1)S(1)}, u32[]{:S(2)}, u32[]{:S(2)}) collective-permute-start(bf16[128,2048]{1,0:T(8,128)(2,1)S(1)} %slice.154), channel_id=1, source_target_pairs={{0,1},{3,2},{4,5},{7,6},{8,9},{11,10},{12,13},{15,14},{16,17},{19,... | collective-permute-start | bytes 1572872 | tf_op jit(solution)/shard_map/ppermute | solution.py:80
  98.6 17.3 %collective-permute-done.21.refs_1_ = bf16[1408,512]{1,0:T(8,128)(2,1)S(1)} collective-permute-done((bf16[1408,512]{1,0:T(8,128)(2,1)S(1)}, bf16[1408,512]{1,0:T(8,128)(2,1)S(1)}, u32[]{:S(2)}, u32[]{:S(2)}) %collective-permute-start.21) | collective-permute-done | bytes 1441824 | tf_op jit(solution)/shard_map/ppermute | solution.py:23
  123.9 8.3 %collective-permute-done.23 = bf16[128,2048]{1,0:T(8,128)(2,1)S(1)} collective-permute-done((bf16[128,2048]{1,0:T(8,128)(2,1)S(1)}, bf16[128,2048]{1,0:T(8,128)(2,1)S(1)}, u32[]{:S(2)}, u32[]{:S(2)}) %collective-permute-start.23) | collective-permute-done | bytes 524320 | tf_op jit(solution)/shard_map/ppermute | solution.py:81
  143.5 6.1 %collective-permute-done.26.b_ref = bf16[128,2048]{1,0:T(8,128)(2,1)S(1)} collective-permute-done((bf16[128,2048]{1,0:T(8,128)(2,1)S(1)}, bf16[128,2048]{1,0:T(8,128)(2,1)S(1)}, u32[]{:S(2)}, u32[]{:S(2)}) %collective-permute-start.26) | collective-permute-done | bytes 524320 | tf_op jit(solution)/shard_map/ppermute | solution.py:91
  156.1 9.3 %collective-permute-done.28 = bf16[128,2048]{1,0:T(8,128)(2,1)S(1)} collective-permute-done((bf16[128,2048]{1,0:T(8,128)(2,1)S(1)}, bf16[128,2048]{1,0:T(8,128)(2,1)S(1)}, u32[]{:S(2)}, u32[]{:S(2)}) %collective-permute-start.28) | collective-permute-done | bytes 524320 | tf_op jit(solution)/shard_map/ppermute | solution.py:52
  167.3 19.0 %collective-permute-done.32.refs_1_ = bf16[2,512,1408]{2,1,0:T(8,128)(2,1)S(1)} collective-permute-done((bf16[2,512,1408]{2,1,0:T(8,128)(2,1)S(1)}, bf16[2,512,1408]{2,1,0:T(8,128)(2,1)S(1)}, u32[]{:S(2)}, u32[]{:S(2)}) %collective-permute-start.32) | collective-permute-done | bytes 2883616 | tf_op jit(solution)/shard_map/ppermute | solution.py:23
  188.4 14.3 %collective-permute-done.33 = bf16[128,2048]{1,0:T(8,128)(2,1)S(1)} collective-permute-done((bf16[128,2048]{1,0:T(8,128)(2,1)S(1)}, bf16[128,2048]{1,0:T(8,128)(2,1)S(1)}, u32[]{:S(2)}, u32[]{:S(2)}) %collective-permute-start.33) | collective-permute-done | bytes 524320 | tf_op jit(solution)/shard_map/ppermute | solution.py:64
  203.1 10.3 %feed_forward.1 = (bf16[512,1408]{1,0:T(8,128)(2,1)S(1)}, bf16[2,512,1408]{2,1,0:T(8,128)(2,1)S(1)}) custom-call(bf16[512,2048]{1,0:T(8,128)(2,1)S(1)} %pad_maximum_fusion.2.x_ref, bf16[2,1024,1408]{2,1,0:T(8,128)(2,1)S(1)} %bitcast.69, bf16[2,512,1408]{2,1,0:T(8,128)(2,1)S(1)} %collective-permute-done.32.refs_1_, ...), custom_call_target="tpu_custom_call" | custom-call | flops 738197504 | bytes 1703936 | tf_op jit(solution)/shard_map/feed_forward/pallas_call | solution.py:515
  215.2 8.0 %to_features.5 = bf16[512,2048]{1,0:T(8,128)(2,1)S(1)} custom-call(bf16[2,512,1408]{2,1,0:T(8,128)(2,1)S(1)} %get-tuple-element.205.v_ref.y_ref, bf16[2,1024,1408]{2,1,0:T(8,128)(2,1)S(1)} %bitcast.70, bf16[2,512,1408]{2,1,0:T(8,128)(2,1)S(1)} %copy-done.20, bf16[2,512,1408]{2,1,0:T(8,128)(2,1)S(1)} %collective-permute-done.34.refs_2_), custom_call_target="tpu_custom_call" | custom-call | flops 738197504 | bytes 2064384 | tf_op jit(solution)/shard_map/to_features/pallas_call | solution.py:565
  237.2 7.4 %collective-permute-start.37 = (bf16[128,2048]{1,0:T(8,128)(2,1)S(1)}, bf16[128,2048]{1,0:T(8,128)(2,1)S(1)}, u32[]{:S(2)}, u32[]{:S(2)}) collective-permute-start(bf16[128,2048]{1,0:T(8,128)(2,1)S(1)} %get-tuple-element.315), channel_id=1, source_target_pairs={{0,1},{3,2},{4,5},{7,6},{8,9},{11,10},{12,13},{15,14},{16,17},{19,... | collective-permute-start | bytes 1572872 | tf_op jit(solution)/shard_map/ppermute | solution.py:81
  262.9 7.8 %collective-permute-done.40.b_ref = bf16[128,2048]{1,0:T(8,128)(2,1)S(1)} collective-permute-done((bf16[128,2048]{1,0:T(8,128)(2,1)S(1)}, bf16[128,2048]{1,0:T(8,128)(2,1)S(1)}, u32[]{:S(2)}, u32[]{:S(2)}) %collective-permute-start.40) | collective-permute-done | bytes 524320 | tf_op jit(solution)/shard_map/ppermute | solution.py:91
  296.8 7.4 %collective-permute-done.46 = bf16[128,2048]{1,0:T(8,128)(2,1)S(1)} collective-permute-done((bf16[128,2048]{1,0:T(8,128)(2,1)}, bf16[128,2048]{1,0:T(8,128)(2,1)S(1)}, u32[]{:S(2)}, u32[]{:S(2)}) %collective-permute-start.46) | collective-permute-done | bytes 524320 | tf_op jit(solution)/shard_map/ppermute | solution.py:60
  308.6 10.5 %collective-permute-done.48.refs_1_ = bf16[1,1,512,1408]{3,2,1,0:T(8,128)(2,1)S(1)} collective-permute-done((bf16[1,1,512,1408]{3,2,1,0:T(8,128)(2,1)S(1)}, bf16[1,1,512,1408]{3,2,1,0:T(8,128)(2,1)S(1)}, u32[]{:S(2)}, u32[]{:S(2)}) %collective-permute-start.48) | collective-permute-done | bytes 1441824 | tf_op jit(solution)/shard_map/ppermute | solution.py:23
  336.5 14.2 %attend_back.1 = (bf16[3,512,256]{2,1,0:T(8,128)(2,1)S(1)}, bf16[3,512,256]{2,1,0:T(8,128)(2,1)S(1)}, f32[3,1,256]{2,1,0:T(1,128)S(1)}) custom-call(s32[5]{0:T(128)S(1)} %pad_add_fusion.1.order_ref, bf16[3,512,256]{2,1,0:T(8,128)(2,1)S(1)} %copy-done.26, bf16[3,512,256]{2,1,0:T(8,128)(2,1)S(1)} %collective-permute-done.14.other_ref, ...), custom_call_target="tpu_custom_call" | custom-call | flops 335544320 | bytes 655360 | tf_op jit(solution)/shard_map/attend_back/pallas_call | solution.py:456
  356.9 11.8 %collective-permute-done.55 = bf16[1,512,1408]{2,1,0:T(8,128)(2,1)S(1)} collective-permute-done((bf16[1,512,1408]{2,1,0:T(8,128)(2,1)S(1)}, bf16[1,512,1408]{2,1,0:T(8,128)(2,1)S(1)}, u32[]{:S(2)}, u32[]{:S(2)}) %collective-permute-start.55) | collective-permute-done | bytes 1441824 | tf_op jit(solution)/shard_map/ppermute | solution.py:23
  390.2 7.4 %collective-permute-done.58 = bf16[128,2048]{1,0:T(8,128)(2,1)S(1)} collective-permute-done((bf16[128,2048]{1,0:T(8,128)(2,1)S(1)}, bf16[128,2048]{1,0:T(8,128)(2,1)S(1)}, u32[]{:S(2)}, u32[]{:S(2)}) %collective-permute-start.58) | collective-permute-done | bytes 524320 | tf_op jit(solution)/shard_map/ppermute | solution.py:80
  398.4 6.7 %collective-permute-start.62 = (bf16[128,2048]{1,0:T(8,128)(2,1)S(1)}, bf16[128,2048]{1,0:T(8,128)(2,1)S(1)}, u32[]{:S(2)}, u32[]{:S(2)}) collective-permute-start(bf16[128,2048]{1,0:T(8,128)(2,1)S(1)} %get-tuple-element.308), channel_id=1, source_target_pairs={{0,1},{3,2},{4,5},{7,6},{8,9},{11,10},{12,13},{15,14},{16,17},{19,... | collective-permute-start | bytes 1572872 | tf_op jit(solution)/shard_map/ppermute | solution.py:81
  423.3 6.4 %collective-permute-done.65.b_ref = bf16[128,2048]{1,0:T(8,128)(2,1)S(1)} collective-permute-done((bf16[128,2048]{1,0:T(8,128)(2,1)S(1)}, bf16[128,2048]{1,0:T(8,128)(2,1)S(1)}, u32[]{:S(2)}, u32[]{:S(2)}) %collective-permute-start.65) | collective-permute-done | bytes 524320 | tf_op jit(solution)/shard_map/ppermute | solution.py:91
  457.3 8.3 %collective-permute-done.77 = f32[14,1024]{1,0:T(8,128)S(1)} collective-permute-done((f32[14,1024]{1,0:T(8,128)S(1)}, f32[14,1024]{1,0:T(8,128)S(1)}, u32[]{:S(2)}, u32[]{:S(2)}) %collective-permute-start.77) | collective-permute-done | bytes 57376 | tf_op jit(solution)/shard_map/ppermute | solution.py:993
  472.6 9.4 %join_pairs.1 = f32[1024,2,1408]{2,1,0:T(2,128)} custom-call(s32[1]{0:T(128)} %bitcast.12.half_ref.q_ref.index_ref.core_ref, bf16[1,512,1408]{2,1,0:T(8,128)(2,1)} %add_convert_fusion.1.refs_0_, bf16[1,512,1408]{2,1,0:T(8,128)(2,1)} %add_convert_fusion.refs_1_, bf16[1,512,1408]{2,1,0:T(8,128)(2,1)} %collective-permute-done.71.refs_2_, ...), custom_call_target="tpu_custom_call" | custom-call | flops 90112 | bytes 2162688 | tf_op jit(solution)/shard_map/join_pairs/pallas_call | solution.py:678
  (419 shorter events, 261.3 us)
Async XLA Ops:
  18.3 45.7 %collective-permute-start.8 = (bf16[3,512,512]{2,1,0:T(8,128)(2,1)S(1)}, bf16[3,512,512]{2,1,0:T(8,128)(2,1)S(1)}, u32[]{:S(2)}, u32[]{:S(2)}) collective-permute-start(bf16[3,512,512]{2,1,0:T(8,128)(2,1)S(1)} %dynamic-slice_bitcast_fusion), channel_id=1, source_target_pairs={{0,4},{4,0},{1,5},{5,1},{2,6},{6,2},{3,7},{7,3},{8,12},{12,8},{9,1... | collective-permute-start | bytes 4718600 | tf_op jit(solution)/shard_map/ppermute | solution.py:23
  30.6 19.6 %collective-permute-start.6 = (bf16[128,2048]{1,0:T(8,128)(2,1)S(1)}, bf16[128,2048]{1,0:T(8,128)(2,1)S(1)}, u32[]{:S(2)}, u32[]{:S(2)}) collective-permute-start(bf16[128,2048]{1,0:T(8,128)(2,1)S(1)} %collective-permute-done.4), channel_id=1, source_target_pairs={{1,0},{2,3},{5,4},{6,7},{9,8},{10,11},{13,12},{14,15},{17,16},{18,... | collective-permute-start | bytes 1572872 | tf_op jit(solution)/shard_map/ppermute | solution.py:60
  32.1 25.2 %collective-permute-start.10 = (bf16[128,1024]{1,0:T(8,128)(2,1)S(1)}, bf16[128,1024]{1,0:T(8,128)(2,1)S(1)}, u32[]{:S(2)}, u32[]{:S(2)}) collective-permute-start(bf16[128,1024]{1,0:T(8,128)(2,1)S(1)} %get-tuple-element.347), channel_id=1, source_target_pairs={{0,8},{4,0},{8,12},{12,4},{1,9},{5,1},{9,13},{13,5},{2,10},{6,2},{... | collective-permute-start | bytes 786440 | tf_op jit(solution)/shard_map/ppermute | solution.py:755
  32.1 25.2 %collective-permute-start.9 = (bf16[128,1024]{1,0:T(8,128)(2,1)S(1)}, bf16[128,1024]{1,0:T(8,128)(2,1)S(1)}, u32[]{:S(2)}, u32[]{:S(2)}) collective-permute-start(bf16[128,1024]{1,0:T(8,128)(2,1)S(1)} %get-tuple-element.346), channel_id=1, source_target_pairs={{0,0},{4,8},{8,4},{12,12},{1,1},{5,9},{9,5},{13,13},{2,2},{6,10},{... | collective-permute-start | bytes 786440 | tf_op jit(solution)/shard_map/ppermute | solution.py:754
  73.9 42.1 %collective-permute-start.21 = (bf16[1408,512]{1,0:T(8,128)(2,1)S(1)}, bf16[1408,512]{1,0:T(8,128)(2,1)S(1)}, u32[]{:S(2)}, u32[]{:S(2)}) collective-permute-start(bf16[1408,512]{1,0:T(8,128)(2,1)S(1)} %dynamic-slice_bitcast_fusion.1), channel_id=1, source_target_pairs={{0,4},{4,0},{1,5},{5,1},{2,6},{6,2},{3,7},{7,3},{8,12},{12,8},{9,1... | collective-permute-start | bytes 4325384 | tf_op jit(solution)/shard_map/ppermute | solution.py:23
  86.2 29.8 %collective-permute-start.19 = (bf16[128,2048]{1,0:T(8,128)(2,1)}, bf16[128,2048]{1,0:T(8,128)(2,1)S(1)}, u32[]{:S(2)}, u32[]{:S(2)}) collective-permute-start(bf16[128,2048]{1,0:T(8,128)(2,1)} %collective-permute-done.11), channel_id=1, source_target_pairs={{1,2},{2,1},{5,6},{6,5},{9,10},{10,9},{13,14},{14,13},{17,18},{18,... | collective-permute-start | bytes 1572872 | tf_op jit(solution)/shard_map/ppermute | solution.py:60
  86.9 29.1 %collective-permute-start.20 = (bf16[128,2048]{1,0:T(8,128)(2,1)S(1)}, bf16[128,2048]{1,0:T(8,128)(2,1)S(1)}, u32[]{:S(2)}, u32[]{:S(2)}) collective-permute-start(bf16[128,2048]{1,0:T(8,128)(2,1)S(1)} %collective-permute-done.12), channel_id=1, source_target_pairs={{1,0},{2,3},{5,4},{6,7},{9,8},{10,11},{13,12},{14,15},{17,16},{18,... | collective-permute-start | bytes 1572872 | tf_op jit(solution)/shard_map/ppermute | solution.py:60
  90.6 25.4 %collective-permute-start.18 = (bf16[128,2048]{1,0:T(8,128)(2,1)S(1)}, bf16[128,2048]{1,0:T(8,128)(2,1)S(1)}, u32[]{:S(2)}, u32[]{:S(2)}) collective-permute-start(bf16[128,2048]{1,0:T(8,128)(2,1)S(1)} %slice.154), channel_id=1, source_target_pairs={{0,1},{3,2},{4,5},{7,6},{8,9},{11,10},{12,13},{15,14},{16,17},{19,... | collective-permute-start | bytes 1572872 | tf_op jit(solution)/shard_map/ppermute | solution.py:80
  116.0 20.4 %collective-permute-start.25 = (bf16[1408,512]{1,0:T(8,128)(2,1)S(1)}, bf16[1408,512]{1,0:T(8,128)(2,1)S(1)}, u32[]{:S(2)}, u32[]{:S(2)}) collective-permute-start(bf16[1408,512]{1,0:T(8,128)(2,1)S(1)} %collective-permute-done.21.refs_1_), channel_id=1, source_target_pairs={{0,8},{8,0},{1,9},{9,1},{2,10},{10,2},{3,11},{11,3},{4,12},{12,4},... | collective-permute-start | bytes 4325384 | tf_op jit(solution)/shard_map/ppermute | solution.py:23
  122.0 64.4 %collective-permute-start.32 = (bf16[2,512,1408]{2,1,0:T(8,128)(2,1)S(1)}, bf16[2,512,1408]{2,1,0:T(8,128)(2,1)S(1)}, u32[]{:S(2)}, u32[]{:S(2)}) collective-permute-start(bf16[2,512,1408]{2,1,0:T(8,128)(2,1)S(1)} %bitcast.103), channel_id=1, source_target_pairs={{0,4},{4,0},{1,5},{5,1},{2,6},{6,2},{3,7},{7,3},{8,12},{12,8},{9,1... | collective-permute-start | bytes 8650760 | tf_op jit(solution)/shard_map/ppermute | solution.py:23
  165.3 21.0 %collective-permute-start.30 = (bf16[128,2048]{1,0:T(8,128)(2,1)S(1)}, bf16[128,2048]{1,0:T(8,128)(2,1)S(1)}, u32[]{:S(2)}, u32[]{:S(2)}) collective-permute-start(bf16[128,2048]{1,0:T(8,128)(2,1)S(1)} %collective-permute-done.28), channel_id=1, source_target_pairs={{1,2},{2,1},{5,6},{6,5},{9,10},{10,9},{13,14},{14,13},{17,18},{18,... | collective-permute-start | bytes 1572872 | tf_op jit(solution)/shard_map/ppermute | solution.py:60
  166.0 20.3 %collective-permute-start.31 = (bf16[128,2048]{1,0:T(8,128)(2,1)S(1)}, bf16[128,2048]{1,0:T(8,128)(2,1)S(1)}, u32[]{:S(2)}, u32[]{:S(2)}) collective-permute-start(bf16[128,2048]{1,0:T(8,128)(2,1)S(1)} %collective-permute-done.29), channel_id=1, source_target_pairs={{1,0},{2,3},{5,4},{6,7},{9,8},{10,11},{13,12},{14,15},{17,16},{18,... | collective-permute-start | bytes 1572872 | tf_op jit(solution)/shard_map/ppermute | solution.py:60
  235.9 19.7 %collective-permute-start.39 = (bf16[2,2,512,1408]{3,2,1,0:T(8,128)(2,1)S(1)}, bf16[2,2,512,1408]{3,2,1,0:T(8,128)(2,1)S(1)}, u32[]{:S(2)}, u32[]{:S(2)}) collective-permute-start(bf16[2,2,512,1408]{3,2,1,0:T(8,128)(2,1)S(1)} %grad_quarters.17), channel_id=1, source_target_pairs={{0,8},{8,0},{1,9},{9,1},{2,10},{10,2},{3,11},{11,3},{4,12},{12,4},... | collective-permute-start | bytes 17301512 | tf_op jit(solution)/shard_map/ppermute | solution.py:23
  255.6 34.8 %collective-permute-start.44 = (bf16[1,1,1408,512]{3,2,1,0:T(8,128)(2,1)}, bf16[1,1,1408,512]{3,2,1,0:T(8,128)(2,1)}, u32[]{:S(2)}, u32[]{:S(2)}) collective-permute-start(bf16[1,1,1408,512]{3,2,1,0:T(8,128)(2,1)} %grad_quarters.18), channel_id=1, source_target_pairs={{0,4},{4,0},{1,5},{5,1},{2,6},{6,2},{3,7},{7,3},{8,12},{12,8},{9,1... | collective-permute-start | bytes 4325384 | tf_op jit(solution)/shard_map/ppermute | solution.py:23
  279.4 39.7 %collective-permute-start.48 = (bf16[1,1,512,1408]{3,2,1,0:T(8,128)(2,1)S(1)}, bf16[1,1,512,1408]{3,2,1,0:T(8,128)(2,1)S(1)}, u32[]{:S(2)}, u32[]{:S(2)}) collective-permute-start(bf16[1,1,512,1408]{3,2,1,0:T(8,128)(2,1)S(1)} %grad_quarters.19), channel_id=1, source_target_pairs={{0,4},{4,0},{1,5},{5,1},{2,6},{6,2},{3,7},{7,3},{8,12},{12,8},{9,1... | collective-permute-start | bytes 4325384 | tf_op jit(solution)/shard_map/ppermute | solution.py:23
  304.2 28.3 %collective-permute-start.50 = (bf16[1,1408,512]{2,1,0:T(8,128)(2,1)S(1)}, bf16[1,1408,512]{2,1,0:T(8,128)(2,1)S(1)}, u32[]{:S(2)}, u32[]{:S(2)}) collective-permute-start(bf16[1,1408,512]{2,1,0:T(8,128)(2,1)S(1)} %bitcast.83), channel_id=1, source_target_pairs={{0,16},{16,0},{1,17},{17,1},{2,18},{18,2},{3,19},{19,3},{4,20},{20... | collective-permute-start | bytes 4325384 | tf_op jit(solution)/shard_map/ppermute | solution.py:23
  319.2 31.5 %collective-permute-start.53 = (bf16[1,1,512,1408]{3,2,1,0:T(8,128)(2,1)S(1)}, bf16[1,1,512,1408]{3,2,1,0:T(8,128)(2,1)S(1)}, u32[]{:S(2)}, u32[]{:S(2)}) collective-permute-start(bf16[1,1,512,1408]{3,2,1,0:T(8,128)(2,1)S(1)} %grad_quarters.20), channel_id=1, source_target_pairs={{0,4},{4,0},{1,5},{5,1},{2,6},{6,2},{3,7},{7,3},{8,12},{12,8},{9,1... | collective-permute-start | bytes 4325384 | tf_op jit(solution)/shard_map/ppermute | solution.py:23
  334.9 33.8 %collective-permute-start.55 = (bf16[1,512,1408]{2,1,0:T(8,128)(2,1)S(1)}, bf16[1,512,1408]{2,1,0:T(8,128)(2,1)S(1)}, u32[]{:S(2)}, u32[]{:S(2)}) collective-permute-start(bf16[1,512,1408]{2,1,0:T(8,128)(2,1)S(1)} %bitcast.85), channel_id=1, source_target_pairs={{0,16},{16,0},{1,17},{17,1},{2,18},{18,2},{3,19},{19,3},{4,20},{20... | collective-permute-start | bytes 4325384 | tf_op jit(solution)/shard_map/ppermute | solution.py:23
  370.5 19.7 %collective-permute-start.59 = (bf16[128,2048]{1,0:T(8,128)(2,1)S(1)}, bf16[128,2048]{1,0:T(8,128)(2,1)}, u32[]{:S(2)}, u32[]{:S(2)}) collective-permute-start(bf16[128,2048]{1,0:T(8,128)(2,1)S(1)} %get-tuple-element.311), channel_id=1, source_target_pairs={{1,2},{2,1},{5,6},{6,5},{9,10},{10,9},{13,14},{14,13},{17,18},{18,... | collective-permute-start | bytes 1572872 | tf_op jit(solution)/shard_map/ppermute | solution.py:88
  375.8 33.2 %collective-permute-start.64 = (bf16[1,512,1408]{2,1,0:T(8,128)(2,1)S(1)}, bf16[1,512,1408]{2,1,0:T(8,128)(2,1)S(1)}, u32[]{:S(2)}, u32[]{:S(2)}) collective-permute-start(bf16[1,512,1408]{2,1,0:T(8,128)(2,1)S(1)} %bitcast.87), channel_id=1, source_target_pairs={{0,16},{16,0},{1,17},{17,1},{2,18},{18,2},{3,19},{19,3},{4,20},{20... | collective-permute-start | bytes 4325384 | tf_op jit(solution)/shard_map/ppermute | solution.py:23
  387.4 27.8 %collective-permute-start.63 = (bf16[1,2,512,512]{3,2,1,0:T(8,128)(2,1)S(1)}, bf16[1,2,512,512]{3,2,1,0:T(8,128)(2,1)S(1)}, u32[]{:S(2)}, u32[]{:S(2)}) collective-permute-start(bf16[1,2,512,512]{3,2,1,0:T(8,128)(2,1)S(1)} %grad_quarters.27), channel_id=1, source_target_pairs={{0,4},{4,0},{1,5},{5,1},{2,6},{6,2},{3,7},{7,3},{8,12},{12,8},{9,1... | collective-permute-start | bytes 3145736 | tf_op jit(solution)/shard_map/ppermute | solution.py:23
  420.6 19.8 %collective-permute-start.69 = (bf16[1,1408,512]{2,1,0:T(8,128)(2,1)}, bf16[1,1408,512]{2,1,0:T(8,128)(2,1)}, u32[]{:S(2)}, u32[]{:S(2)}) collective-permute-start(bf16[1,1408,512]{2,1,0:T(8,128)(2,1)} %add_convert_fusion.2), channel_id=1, source_target_pairs={{0,8},{8,0},{1,9},{9,1},{2,10},{10,2},{3,11},{11,3},{4,12},{12,4},... | collective-permute-start | bytes 4325384 | tf_op jit(solution)/shard_map/ppermute | solution.py:23
  431.4 25.9 %collective-permute-start.78 = (bf16[2,512,512]{2,1,0:T(8,128)(2,1)}, bf16[2,512,512]{2,1,0:T(8,128)(2,1)}, u32[]{:S(2)}, u32[]{:S(2)}) collective-permute-start(bf16[2,512,512]{2,1,0:T(8,128)(2,1)} %bitcast.91), channel_id=1, source_target_pairs={{0,16},{16,0},{1,17},{17,1},{2,18},{18,2},{3,19},{19,3},{4,20},{20... | collective-permute-start | bytes 3145736 | tf_op jit(solution)/shard_map/ppermute | solution.py:23
  456.6 25.4 %collective-permute-start.82 = (bf16[1,512,512]{2,1,0:T(8,128)(2,1)S(1)}, bf16[1,512,512]{2,1,0:T(8,128)(2,1)S(1)}, u32[]{:S(2)}, u32[]{:S(2)}) collective-permute-start(bf16[1,512,512]{2,1,0:T(8,128)(2,1)S(1)} %bitcast.93), channel_id=1, source_target_pairs={{0,16},{16,0},{1,17},{17,1},{2,18},{18,2},{3,19},{19,3},{4,20},{20... | collective-permute-start | bytes 1572872 | tf_op jit(solution)/shard_map/ppermute | solution.py:23
  (129 other events, 1616.1 us)

commit v7 on v6

--- a/solution.py
+++ b/solution.py
@@ -934,13 +934,13 @@
         axis=2,
     )
     in_sent = for_core(tokens_a, mixed, True)
-    in_sent, mixed, gate_own[1], gate_other[0], out_oth = sync(
-        [], in_sent, mixed, gate_own[1], gate_other[0], out_oth
+    part_a = to_features(mixed, pieces_in, True)
+    part_a, in_sent, mixed, gate_own[1], gate_other[0], out_oth = sync(
+        [], part_a, in_sent, mixed, gate_own[1], gate_other[0], out_oth
     )
     in_got = swap(in_sent, "core")
     out_arrived = swap(out_oth, "row")
     gate_other[1] = y_swap(gate_own[1])
-    part_a = to_features(mixed, pieces_in, True)
     part_a, in_got, out_arrived = sync([], part_a, in_got, out_arrived)
     hops = Scatter(part_a, slots)
     spans = (dict(at=0, first=0, count=2), dict(at=2, first=2, count=1))

time: 510 us -> 508 us (level)
    unnamed x129 -> x135, local copies, waits for them, and re-layouts: 15.5 us -> 14 us
  transfers between devices with their start and end apart: 89 -> 89, of which waited for: 34 -> 33; matrix products, arithmetic and copies ran while one was open for 9% -> 9% of each run, Pallas kernels for 16% -> 17%
where the time goes in v7:
time: 508 us; the launch traced here: 498 us
  waiting for transfers between devices  210 us (41%)
  starting transfers between devices  120 us (24%)
  Pallas kernels  107 us (21%)
  other arithmetic  34.1 us (7%)
  local copies, waits for them, and re-layouts  24.1 us (5%)
    ppermute x38, waiting for transfers between devices, swap(): return lax.ppermute(x, axis, [(0, 1), (1, 0)])  78.1 us
    pallas_call x16, Pallas kernels, grad_quarters(): pl.pallas_call(body, grid_spec=pltpu.PrefetchScalarGridSpec(num_scalar_pr...  27.9 us
    ppermute x38, starting transfers between devices, swap(): return lax.ppermute(x, axis, [(0, 1), (1, 0)])  27.5 us
    ppermute x8, waiting for transfers between devices, hop(): self.flying = [lax.ppermute(one, 'col', MID), lax.ppermute(mid, 'col', OUT)]  26.4 us
    ppermute x4, waiting for transfers between devices, hop(): self.flying = [lax.ppermute(far, 'col', OUT)]  25 us
    ppermute x4, starting transfers between devices, __init__(): self.two = lax.ppermute(self.part[2], 'col', IN)  21.6 us
    ppermute x4, waiting for transfers between devices, hop(): lax.ppermute(one, 'col', PAIR)  19.2 us
    pallas_call x4, Pallas kernels, to_features(): pl.pallas_call(body, grid=(width // block,), in_specs=[pl.BlockSpec((coun...  19 us
  transfers between devices with their start and end apart: 89, of which 33 were waited for; matrix products, arithmetic and copies ran while one was open for 9% of the time, Pallas kernels for 17%

profile of v7, /device:TPU:0, one launch (start us, length us, event | category | flops | bytes accessed | tf_op | source)
XLA Modules:
  0.0 498.5 jit_solution(13456546382722926610)
XLA Ops:
  33.1 17.1 %collective-permute-done.6 = bf16[128,2048]{1,0:T(8,128)(2,1)S(1)} collective-permute-done((bf16[128,2048]{1,0:T(8,128)(2,1)S(1)}, bf16[128,2048]{1,0:T(8,128)(2,1)S(1)}, u32[]{:S(2)}, u32[]{:S(2)}) %collective-permute-start.6) | collective-permute-done | bytes 524320 | tf_op jit(solution)/shard_map/ppermute | solution.py:60
  57.4 6.5 %collective-permute-done.7 = bf16[128,2048]{1,0:T(8,128)(2,1)S(1)} collective-permute-done((bf16[128,2048]{1,0:T(8,128)(2,1)S(1)}, bf16[128,2048]{1,0:T(8,128)(2,1)S(1)}, u32[]{:S(2)}, u32[]{:S(2)}) %collective-permute-start.7) | collective-permute-done | bytes 524320 | tf_op jit(solution)/shard_map/ppermute | solution.py:64
  77.4 7.9 %attend.1 = (bf16[512,256]{1,0:T(8,128)(2,1)S(1)}, bf16[512,256]{1,0:T(8,128)(2,1)S(1)}, f32[2,1024,2]{2,1,0:T(8,128)S(1)}) custom-call(s32[5]{0:T(128)S(1)} %pad_add_fusion.order_ref, bf16[3,512,256]{2,1,0:T(8,128)(2,1)S(1)} %qkv_columns.2.mine_ref, bf16[3,512,256]{2,1,0:T(8,128)(2,1)S(1)} %collective-permute-done.14.other_ref), custom_call_target="tpu_custom_call" | custom-call | flops 134217728 | bytes 262144 | tf_op jit(solution)/shard_map/attend/pallas_call | solution.py:346
  90.6 8.1 %collective-permute-start.18 = (bf16[128,2048]{1,0:T(8,128)(2,1)S(1)}, bf16[128,2048]{1,0:T(8,128)(2,1)S(1)}, u32[]{:S(2)}, u32[]{:S(2)}) collective-permute-start(bf16[128,2048]{1,0:T(8,128)(2,1)S(1)} %slice.154), channel_id=1, source_target_pairs={{0,1},{3,2},{4,5},{7,6},{8,9},{11,10},{12,13},{15,14},{16,17},{19,... | collective-permute-start | bytes 1572872 | tf_op jit(solution)/shard_map/ppermute | solution.py:80
  98.6 17.3 %collective-permute-done.21.refs_1_ = bf16[1408,512]{1,0:T(8,128)(2,1)S(1)} collective-permute-done((bf16[1408,512]{1,0:T(8,128)(2,1)S(1)}, bf16[1408,512]{1,0:T(8,128)(2,1)S(1)}, u32[]{:S(2)}, u32[]{:S(2)}) %collective-permute-start.21) | collective-permute-done | bytes 1441824 | tf_op jit(solution)/shard_map/ppermute | solution.py:23
  123.9 8.3 %collective-permute-done.23 = bf16[128,2048]{1,0:T(8,128)(2,1)S(1)} collective-permute-done((bf16[128,2048]{1,0:T(8,128)(2,1)S(1)}, bf16[128,2048]{1,0:T(8,128)(2,1)S(1)}, u32[]{:S(2)}, u32[]{:S(2)}) %collective-permute-start.23) | collective-permute-done | bytes 524320 | tf_op jit(solution)/shard_map/ppermute | solution.py:81
  143.5 6.1 %collective-permute-done.26.b_ref = bf16[128,2048]{1,0:T(8,128)(2,1)S(1)} collective-permute-done((bf16[128,2048]{1,0:T(8,128)(2,1)S(1)}, bf16[128,2048]{1,0:T(8,128)(2,1)S(1)}, u32[]{:S(2)}, u32[]{:S(2)}) %collective-permute-start.26) | collective-permute-done | bytes 524320 | tf_op jit(solution)/shard_map/ppermute | solution.py:91
  156.1 9.3 %collective-permute-done.28 = bf16[128,2048]{1,0:T(8,128)(2,1)S(1)} collective-permute-done((bf16[128,2048]{1,0:T(8,128)(2,1)S(1)}, bf16[128,2048]{1,0:T(8,128)(2,1)S(1)}, u32[]{:S(2)}, u32[]{:S(2)}) %collective-permute-start.28) | collective-permute-done | bytes 524320 | tf_op jit(solution)/shard_map/ppermute | solution.py:52
  167.4 19.0 %collective-permute-done.32.refs_1_ = bf16[2,512,1408]{2,1,0:T(8,128)(2,1)S(1)} collective-permute-done((bf16[2,512,1408]{2,1,0:T(8,128)(2,1)S(1)}, bf16[2,512,1408]{2,1,0:T(8,128)(2,1)S(1)}, u32[]{:S(2)}, u32[]{:S(2)}) %collective-permute-start.32) | collective-permute-done | bytes 2883616 | tf_op jit(solution)/shard_map/ppermute | solution.py:23
  188.4 14.3 %collective-permute-done.33 = bf16[128,2048]{1,0:T(8,128)(2,1)S(1)} collective-permute-done((bf16[128,2048]{1,0:T(8,128)(2,1)S(1)}, bf16[128,2048]{1,0:T(8,128)(2,1)S(1)}, u32[]{:S(2)}, u32[]{:S(2)}) %collective-permute-start.33) | collective-permute-done | bytes 524320 | tf_op jit(solution)/shard_map/ppermute | solution.py:64
  203.1 10.3 %feed_forward.1 = (bf16[512,1408]{1,0:T(8,128)(2,1)S(1)}, bf16[2,512,1408]{2,1,0:T(8,128)(2,1)S(1)}) custom-call(bf16[512,2048]{1,0:T(8,128)(2,1)S(1)} %pad_maximum_fusion.2.x_ref, bf16[2,1024,1408]{2,1,0:T(8,128)(2,1)S(1)} %bitcast.69, bf16[2,512,1408]{2,1,0:T(8,128)(2,1)S(1)} %collective-permute-done.32.refs_1_, ...), custom_call_target="tpu_custom_call" | custom-call | flops 738197504 | bytes 1703936 | tf_op jit(solution)/shard_map/feed_forward/pallas_call | solution.py:515
  215.2 8.0 %to_features.5 = bf16[512,2048]{1,0:T(8,128)(2,1)S(1)} custom-call(bf16[2,512,1408]{2,1,0:T(8,128)(2,1)S(1)} %get-tuple-element.206.v_ref.y_ref, bf16[2,1024,1408]{2,1,0:T(8,128)(2,1)S(1)} %bitcast.70, bf16[2,512,1408]{2,1,0:T(8,128)(2,1)S(1)} %copy-done.21, bf16[2,512,1408]{2,1,0:T(8,128)(2,1)S(1)} %collective-permute-done.34.refs_2_), custom_call_target="tpu_custom_call" | custom-call | flops 738197504 | bytes 2064384 | tf_op jit(solution)/shard_map/to_features/pallas_call | solution.py:565
  237.2 7.4 %collective-permute-start.37 = (bf16[128,2048]{1,0:T(8,128)(2,1)S(1)}, bf16[128,2048]{1,0:T(8,128)(2,1)S(1)}, u32[]{:S(2)}, u32[]{:S(2)}) collective-permute-start(bf16[128,2048]{1,0:T(8,128)(2,1)S(1)} %get-tuple-element.317), channel_id=1, source_target_pairs={{0,1},{3,2},{4,5},{7,6},{8,9},{11,10},{12,13},{15,14},{16,17},{19,... | collective-permute-start | bytes 1572872 | tf_op jit(solution)/shard_map/ppermute | solution.py:81
  263.9 6.8 %collective-permute-done.40.b_ref = bf16[128,2048]{1,0:T(8,128)(2,1)S(1)} collective-permute-done((bf16[128,2048]{1,0:T(8,128)(2,1)S(1)}, bf16[128,2048]{1,0:T(8,128)(2,1)S(1)}, u32[]{:S(2)}, u32[]{:S(2)}) %collective-permute-start.40) | collective-permute-done | bytes 524320 | tf_op jit(solution)/shard_map/ppermute | solution.py:91
  294.9 9.2 %collective-permute-done.46 = bf16[128,2048]{1,0:T(8,128)(2,1)S(1)} collective-permute-done((bf16[128,2048]{1,0:T(8,128)(2,1)}, bf16[128,2048]{1,0:T(8,128)(2,1)S(1)}, u32[]{:S(2)}, u32[]{:S(2)}) %collective-permute-start.46) | collective-permute-done | bytes 524320 | tf_op jit(solution)/shard_map/ppermute | solution.py:60
  308.4 10.7 %collective-permute-done.48.refs_1_ = bf16[1,1,512,1408]{3,2,1,0:T(8,128)(2,1)} collective-permute-done((bf16[1,1,512,1408]{3,2,1,0:T(8,128)(2,1)}, bf16[1,1,512,1408]{3,2,1,0:T(8,128)(2,1)}, u32[]{:S(2)}, u32[]{:S(2)}) %collective-permute-start.48) | collective-permute-done | bytes 1441824 | tf_op jit(solution)/shard_map/ppermute | solution.py:23
  336.5 14.2 %attend_back.1 = (bf16[3,512,256]{2,1,0:T(8,128)(2,1)S(1)}, bf16[3,512,256]{2,1,0:T(8,128)(2,1)S(1)}, f32[3,1,256]{2,1,0:T(1,128)S(1)}) custom-call(s32[5]{0:T(128)S(1)} %pad_add_fusion.order_ref, bf16[3,512,256]{2,1,0:T(8,128)(2,1)S(1)} %copy-done.25, bf16[3,512,256]{2,1,0:T(8,128)(2,1)S(1)} %collective-permute-done.14.other_ref, ...), custom_call_target="tpu_custom_call" | custom-call | flops 335544320 | bytes 655360 | tf_op jit(solution)/shard_map/attend_back/pallas_call | solution.py:456
  361.6 7.3 %collective-permute-done.55 = bf16[1,512,1408]{2,1,0:T(8,128)(2,1)} collective-permute-done((bf16[1,512,1408]{2,1,0:T(8,128)(2,1)S(1)}, bf16[1,512,1408]{2,1,0:T(8,128)(2,1)}, u32[]{:S(2)}, u32[]{:S(2)}) %collective-permute-start.55) | collective-permute-done | bytes 1441824 | tf_op jit(solution)/shard_map/ppermute | solution.py:23
  376.6 6.6 %collective-permute-done.57.refs_1_ = bf16[1,1,512,512]{3,2,1,0:T(8,128)(2,1)S(1)} collective-permute-done((bf16[1,1,512,512]{3,2,1,0:T(8,128)(2,1)S(1)}, bf16[1,1,512,512]{3,2,1,0:T(8,128)(2,1)S(1)}, u32[]{:S(2)}, u32[]{:S(2)}) %collective-permute-start.57) | collective-permute-done | bytes 524320 | tf_op jit(solution)/shard_map/ppermute | solution.py:23
  390.4 7.1 %collective-permute-done.58 = bf16[128,2048]{1,0:T(8,128)(2,1)S(1)} collective-permute-done((bf16[128,2048]{1,0:T(8,128)(2,1)S(1)}, bf16[128,2048]{1,0:T(8,128)(2,1)S(1)}, u32[]{:S(2)}, u32[]{:S(2)}) %collective-permute-start.58) | collective-permute-done | bytes 524320 | tf_op jit(solution)/shard_map/ppermute | solution.py:80
  398.3 6.8 %collective-permute-start.62 = (bf16[128,2048]{1,0:T(8,128)(2,1)S(1)}, bf16[128,2048]{1,0:T(8,128)(2,1)S(1)}, u32[]{:S(2)}, u32[]{:S(2)}) collective-permute-start(bf16[128,2048]{1,0:T(8,128)(2,1)S(1)} %get-tuple-element.310), channel_id=1, source_target_pairs={{0,1},{3,2},{4,5},{7,6},{8,9},{11,10},{12,13},{15,14},{16,17},{19,... | collective-permute-start | bytes 1572872 | tf_op jit(solution)/shard_map/ppermute | solution.py:81
  423.4 6.4 %collective-permute-done.65.b_ref = bf16[128,2048]{1,0:T(8,128)(2,1)S(1)} collective-permute-done((bf16[128,2048]{1,0:T(8,128)(2,1)S(1)}, bf16[128,2048]{1,0:T(8,128)(2,1)S(1)}, u32[]{:S(2)}, u32[]{:S(2)}) %collective-permute-start.65) | collective-permute-done | bytes 524320 | tf_op jit(solution)/shard_map/ppermute | solution.py:91
  457.5 8.1 %collective-permute-done.77 = f32[14,1024]{1,0:T(8,128)S(1)} collective-permute-done((f32[14,1024]{1,0:T(8,128)S(1)}, f32[14,1024]{1,0:T(8,128)S(1)}, u32[]{:S(2)}, u32[]{:S(2)}) %collective-permute-start.77) | collective-permute-done | bytes 57376 | tf_op jit(solution)/shard_map/ppermute | solution.py:993
  471.4 9.4 %join_pairs.1 = f32[1024,2,1408]{2,1,0:T(2,128)} custom-call(s32[1]{0:T(128)} %bitcast.12.half_ref.q_ref.index_ref.core_ref, bf16[1,512,1408]{2,1,0:T(8,128)(2,1)} %add_convert_fusion.1.refs_0_, bf16[1,512,1408]{2,1,0:T(8,128)(2,1)} %add_convert_fusion.refs_1_, bf16[1,512,1408]{2,1,0:T(8,128)(2,1)} %collective-permute-done.71.refs_2_, ...), custom_call_target="tpu_custom_call" | custom-call | flops 90112 | bytes 2162688 | tf_op jit(solution)/shard_map/join_pairs/pallas_call | solution.py:678
  (425 shorter events, 263.3 us)
Async XLA Ops:
  18.3 45.7 %collective-permute-start.8 = (bf16[3,512,512]{2,1,0:T(8,128)(2,1)S(1)}, bf16[3,512,512]{2,1,0:T(8,128)(2,1)S(1)}, u32[]{:S(2)}, u32[]{:S(2)}) collective-permute-start(bf16[3,512,512]{2,1,0:T(8,128)(2,1)S(1)} %dynamic-slice_bitcast_fusion), channel_id=1, source_target_pairs={{0,4},{4,0},{1,5},{5,1},{2,6},{6,2},{3,7},{7,3},{8,12},{12,8},{9,1... | collective-permute-start | bytes 4718600 | tf_op jit(solution)/shard_map/ppermute | solution.py:23
  30.7 19.5 %collective-permute-start.6 = (bf16[128,2048]{1,0:T(8,128)(2,1)S(1)}, bf16[128,2048]{1,0:T(8,128)(2,1)S(1)}, u32[]{:S(2)}, u32[]{:S(2)}) collective-permute-start(bf16[128,2048]{1,0:T(8,128)(2,1)S(1)} %collective-permute-done.4), channel_id=1, source_target_pairs={{1,0},{2,3},{5,4},{6,7},{9,8},{10,11},{13,12},{14,15},{17,16},{18,... | collective-permute-start | bytes 1572872 | tf_op jit(solution)/shard_map/ppermute | solution.py:60
  32.2 25.1 %collective-permute-start.10 = (bf16[128,1024]{1,0:T(8,128)(2,1)S(1)}, bf16[128,1024]{1,0:T(8,128)(2,1)S(1)}, u32[]{:S(2)}, u32[]{:S(2)}) collective-permute-start(bf16[128,1024]{1,0:T(8,128)(2,1)S(1)} %get-tuple-element.349), channel_id=1, source_target_pairs={{0,8},{4,0},{8,12},{12,4},{1,9},{5,1},{9,13},{13,5},{2,10},{6,2},{... | collective-permute-start | bytes 786440 | tf_op jit(solution)/shard_map/ppermute | solution.py:755
  32.2 25.1 %collective-permute-start.9 = (bf16[128,1024]{1,0:T(8,128)(2,1)S(1)}, bf16[128,1024]{1,0:T(8,128)(2,1)S(1)}, u32[]{:S(2)}, u32[]{:S(2)}) collective-permute-start(bf16[128,1024]{1,0:T(8,128)(2,1)S(1)} %get-tuple-element.348), channel_id=1, source_target_pairs={{0,0},{4,8},{8,4},{12,12},{1,1},{5,9},{9,5},{13,13},{2,2},{6,10},{... | collective-permute-start | bytes 786440 | tf_op jit(solution)/shard_map/ppermute | solution.py:754
  73.9 42.1 %collective-permute-start.21 = (bf16[1408,512]{1,0:T(8,128)(2,1)S(1)}, bf16[1408,512]{1,0:T(8,128)(2,1)S(1)}, u32[]{:S(2)}, u32[]{:S(2)}) collective-permute-start(bf16[1408,512]{1,0:T(8,128)(2,1)S(1)} %dynamic-slice_bitcast_fusion.1), channel_id=1, source_target_pairs={{0,4},{4,0},{1,5},{5,1},{2,6},{6,2},{3,7},{7,3},{8,12},{12,8},{9,1... | collective-permute-start | bytes 4325384 | tf_op jit(solution)/shard_map/ppermute | solution.py:23
  86.2 29.8 %collective-permute-start.19 = (bf16[128,2048]{1,0:T(8,128)(2,1)}, bf16[128,2048]{1,0:T(8,128)(2,1)S(1)}, u32[]{:S(2)}, u32[]{:S(2)}) collective-permute-start(bf16[128,2048]{1,0:T(8,128)(2,1)} %collective-permute-done.11), channel_id=1, source_target_pairs={{1,2},{2,1},{5,6},{6,5},{9,10},{10,9},{13,14},{14,13},{17,18},{18,... | collective-permute-start | bytes 1572872 | tf_op jit(solution)/shard_map/ppermute | solution.py:60
  86.9 29.1 %collective-permute-start.20 = (bf16[128,2048]{1,0:T(8,128)(2,1)S(1)}, bf16[128,2048]{1,0:T(8,128)(2,1)S(1)}, u32[]{:S(2)}, u32[]{:S(2)}) collective-permute-start(bf16[128,2048]{1,0:T(8,128)(2,1)S(1)} %collective-permute-done.12), channel_id=1, source_target_pairs={{1,0},{2,3},{5,4},{6,7},{9,8},{10,11},{13,12},{14,15},{17,16},{18,... | collective-permute-start | bytes 1572872 | tf_op jit(solution)/shard_map/ppermute | solution.py:60
  90.6 25.4 %collective-permute-start.18 = (bf16[128,2048]{1,0:T(8,128)(2,1)S(1)}, bf16[128,2048]{1,0:T(8,128)(2,1)S(1)}, u32[]{:S(2)}, u32[]{:S(2)}) collective-permute-start(bf16[128,2048]{1,0:T(8,128)(2,1)S(1)} %slice.154), channel_id=1, source_target_pairs={{0,1},{3,2},{4,5},{7,6},{8,9},{11,10},{12,13},{15,14},{16,17},{19,... | collective-permute-start | bytes 1572872 | tf_op jit(solution)/shard_map/ppermute | solution.py:80
  116.0 20.4 %collective-permute-start.25 = (bf16[1408,512]{1,0:T(8,128)(2,1)S(1)}, bf16[1408,512]{1,0:T(8,128)(2,1)S(1)}, u32[]{:S(2)}, u32[]{:S(2)}) collective-permute-start(bf16[1408,512]{1,0:T(8,128)(2,1)S(1)} %collective-permute-done.21.refs_1_), channel_id=1, source_target_pairs={{0,8},{8,0},{1,9},{9,1},{2,10},{10,2},{3,11},{11,3},{4,12},{12,4},... | collective-permute-start | bytes 4325384 | tf_op jit(solution)/shard_map/ppermute | solution.py:23
  122.0 64.4 %collective-permute-start.32 = (bf16[2,512,1408]{2,1,0:T(8,128)(2,1)S(1)}, bf16[2,512,1408]{2,1,0:T(8,128)(2,1)S(1)}, u32[]{:S(2)}, u32[]{:S(2)}) collective-permute-start(bf16[2,512,1408]{2,1,0:T(8,128)(2,1)S(1)} %bitcast.103), channel_id=1, source_target_pairs={{0,4},{4,0},{1,5},{5,1},{2,6},{6,2},{3,7},{7,3},{8,12},{12,8},{9,1... | collective-permute-start | bytes 8650760 | tf_op jit(solution)/shard_map/ppermute | solution.py:23
  165.4 21.0 %collective-permute-start.30 = (bf16[128,2048]{1,0:T(8,128)(2,1)S(1)}, bf16[128,2048]{1,0:T(8,128)(2,1)S(1)}, u32[]{:S(2)}, u32[]{:S(2)}) collective-permute-start(bf16[128,2048]{1,0:T(8,128)(2,1)S(1)} %collective-permute-done.28), channel_id=1, source_target_pairs={{1,2},{2,1},{5,6},{6,5},{9,10},{10,9},{13,14},{14,13},{17,18},{18,... | collective-permute-start | bytes 1572872 | tf_op jit(solution)/shard_map/ppermute | solution.py:60
  166.1 20.3 %collective-permute-start.31 = (bf16[128,2048]{1,0:T(8,128)(2,1)S(1)}, bf16[128,2048]{1,0:T(8,128)(2,1)S(1)}, u32[]{:S(2)}, u32[]{:S(2)}) collective-permute-start(bf16[128,2048]{1,0:T(8,128)(2,1)S(1)} %collective-permute-done.29), channel_id=1, source_target_pairs={{1,0},{2,3},{5,4},{6,7},{9,8},{10,11},{13,12},{14,15},{17,16},{18,... | collective-permute-start | bytes 1572872 | tf_op jit(solution)/shard_map/ppermute | solution.py:60
  235.9 19.7 %collective-permute-start.39 = (bf16[2,2,512,1408]{3,2,1,0:T(8,128)(2,1)S(1)}, bf16[2,2,512,1408]{3,2,1,0:T(8,128)(2,1)S(1)}, u32[]{:S(2)}, u32[]{:S(2)}) collective-permute-start(bf16[2,2,512,1408]{3,2,1,0:T(8,128)(2,1)S(1)} %grad_quarters.17), channel_id=1, source_target_pairs={{0,8},{8,0},{1,9},{9,1},{2,10},{10,2},{3,11},{11,3},{4,12},{12,4},... | collective-permute-start | bytes 17301512 | tf_op jit(solution)/shard_map/ppermute | solution.py:23
  255.6 34.8 %collective-permute-start.44 = (bf16[1,1,1408,512]{3,2,1,0:T(8,128)(2,1)}, bf16[1,1,1408,512]{3,2,1,0:T(8,128)(2,1)}, u32[]{:S(2)}, u32[]{:S(2)}) collective-permute-start(bf16[1,1,1408,512]{3,2,1,0:T(8,128)(2,1)} %grad_quarters.18), channel_id=1, source_target_pairs={{0,4},{4,0},{1,5},{5,1},{2,6},{6,2},{3,7},{7,3},{8,12},{12,8},{9,1... | collective-permute-start | bytes 4325384 | tf_op jit(solution)/shard_map/ppermute | solution.py:23
  279.3 39.8 %collective-permute-start.48 = (bf16[1,1,512,1408]{3,2,1,0:T(8,128)(2,1)}, bf16[1,1,512,1408]{3,2,1,0:T(8,128)(2,1)}, u32[]{:S(2)}, u32[]{:S(2)}) collective-permute-start(bf16[1,1,512,1408]{3,2,1,0:T(8,128)(2,1)} %grad_quarters.19), channel_id=1, source_target_pairs={{0,4},{4,0},{1,5},{5,1},{2,6},{6,2},{3,7},{7,3},{8,12},{12,8},{9,1... | collective-permute-start | bytes 4325384 | tf_op jit(solution)/shard_map/ppermute | solution.py:23
  304.1 28.4 %collective-permute-start.50 = (bf16[1,1408,512]{2,1,0:T(8,128)(2,1)S(1)}, bf16[1,1408,512]{2,1,0:T(8,128)(2,1)S(1)}, u32[]{:S(2)}, u32[]{:S(2)}) collective-permute-start(bf16[1,1408,512]{2,1,0:T(8,128)(2,1)S(1)} %bitcast.83), channel_id=1, source_target_pairs={{0,16},{16,0},{1,17},{17,1},{2,18},{18,2},{3,19},{19,3},{4,20},{20... | collective-permute-start | bytes 4325384 | tf_op jit(solution)/shard_map/ppermute | solution.py:23
  319.3 31.5 %collective-permute-start.53 = (bf16[1,1,512,1408]{3,2,1,0:T(8,128)(2,1)S(1)}, bf16[1,1,512,1408]{3,2,1,0:T(8,128)(2,1)S(1)}, u32[]{:S(2)}, u32[]{:S(2)}) collective-permute-start(bf16[1,1,512,1408]{3,2,1,0:T(8,128)(2,1)S(1)} %grad_quarters.20), channel_id=1, source_target_pairs={{0,4},{4,0},{1,5},{5,1},{2,6},{6,2},{3,7},{7,3},{8,12},{12,8},{9,1... | collective-permute-start | bytes 4325384 | tf_op jit(solution)/shard_map/ppermute | solution.py:23
  334.9 33.9 %collective-permute-start.55 = (bf16[1,512,1408]{2,1,0:T(8,128)(2,1)S(1)}, bf16[1,512,1408]{2,1,0:T(8,128)(2,1)}, u32[]{:S(2)}, u32[]{:S(2)}) collective-permute-start(bf16[1,512,1408]{2,1,0:T(8,128)(2,1)S(1)} %bitcast.85), channel_id=1, source_target_pairs={{0,16},{16,0},{1,17},{17,1},{2,18},{18,2},{3,19},{19,3},{4,20},{20... | collective-permute-start | bytes 4325384 | tf_op jit(solution)/shard_map/ppermute | solution.py:23
  370.7 19.7 %collective-permute-start.59 = (bf16[128,2048]{1,0:T(8,128)(2,1)S(1)}, bf16[128,2048]{1,0:T(8,128)(2,1)S(1)}, u32[]{:S(2)}, u32[]{:S(2)}) collective-permute-start(bf16[128,2048]{1,0:T(8,128)(2,1)S(1)} %get-tuple-element.313), channel_id=1, source_target_pairs={{1,2},{2,1},{5,6},{6,5},{9,10},{10,9},{13,14},{14,13},{17,18},{18,... | collective-permute-start | bytes 1572872 | tf_op jit(solution)/shard_map/ppermute | solution.py:88
  375.0 33.2 %collective-permute-start.64 = (bf16[1,512,1408]{2,1,0:T(8,128)(2,1)S(1)}, bf16[1,512,1408]{2,1,0:T(8,128)(2,1)S(1)}, u32[]{:S(2)}, u32[]{:S(2)}) collective-permute-start(bf16[1,512,1408]{2,1,0:T(8,128)(2,1)S(1)} %bitcast.87), channel_id=1, source_target_pairs={{0,16},{16,0},{1,17},{17,1},{2,18},{18,2},{3,19},{19,3},{4,20},{20... | collective-permute-start | bytes 4325384 | tf_op jit(solution)/shard_map/ppermute | solution.py:23
  387.5 27.7 %collective-permute-start.63 = (bf16[1,2,512,512]{3,2,1,0:T(8,128)(2,1)S(1)}, bf16[1,2,512,512]{3,2,1,0:T(8,128)(2,1)S(1)}, u32[]{:S(2)}, u32[]{:S(2)}) collective-permute-start(bf16[1,2,512,512]{3,2,1,0:T(8,128)(2,1)S(1)} %grad_quarters.27), channel_id=1, source_target_pairs={{0,4},{4,0},{1,5},{5,1},{2,6},{6,2},{3,7},{7,3},{8,12},{12,8},{9,1... | collective-permute-start | bytes 3145736 | tf_op jit(solution)/shard_map/ppermute | solution.py:23
  420.6 19.8 %collective-permute-start.69 = (bf16[1,1408,512]{2,1,0:T(8,128)(2,1)}, bf16[1,1408,512]{2,1,0:T(8,128)(2,1)}, u32[]{:S(2)}, u32[]{:S(2)}) collective-permute-start(bf16[1,1408,512]{2,1,0:T(8,128)(2,1)} %add_convert_fusion.2), channel_id=1, source_target_pairs={{0,8},{8,0},{1,9},{9,1},{2,10},{10,2},{3,11},{11,3},{4,12},{12,4},... | collective-permute-start | bytes 4325384 | tf_op jit(solution)/shard_map/ppermute | solution.py:23
  431.4 26.1 %collective-permute-start.78 = (bf16[2,512,512]{2,1,0:T(8,128)(2,1)}, bf16[2,512,512]{2,1,0:T(8,128)(2,1)}, u32[]{:S(2)}, u32[]{:S(2)}) collective-permute-start(bf16[2,512,512]{2,1,0:T(8,128)(2,1)} %bitcast.91), channel_id=1, source_target_pairs={{0,16},{16,0},{1,17},{17,1},{2,18},{18,2},{3,19},{19,3},{4,20},{20... | collective-permute-start | bytes 3145736 | tf_op jit(solution)/shard_map/ppermute | solution.py:23
  456.8 24.1 %collective-permute-start.82 = (bf16[1,512,512]{2,1,0:T(8,128)(2,1)S(1)}, bf16[1,512,512]{2,1,0:T(8,128)(2,1)S(1)}, u32[]{:S(2)}, u32[]{:S(2)}) collective-permute-start(bf16[1,512,512]{2,1,0:T(8,128)(2,1)S(1)} %bitcast.93), channel_id=1, source_target_pairs={{0,16},{16,0},{1,17},{17,1},{2,18},{18,2},{3,19},{19,3},{4,20},{20... | collective-permute-start | bytes 1572872 | tf_op jit(solution)/shard_map/ppermute | solution.py:23
  (132 other events, 1609.4 us)

commit v8 on v7

--- a/solution.py
+++ b/solution.py
@@ -652,7 +652,7 @@
 
 def join_pairs(core, parts, rests):
     rows, units = parts[0].shape[1:]
-    block = 128 if rows % 128 == 0 else rows
+    block = 64 if rows % 64 == 0 else rows
     steps = rows // block
 
     def body(core_ref, *refs):
@@ -684,7 +684,7 @@
             out_specs=pl.BlockSpec((block, 2, units), lambda h, j, c: (h * steps + j, 0, 0)),
         ),
         out_shape=jax.ShapeDtypeStruct((2 * rows, 2, units), F32),
-        compiler_params=params(16, 2),
+        compiler_params=params(8, 2),
         cost_estimate=cost(rows * units, 24 * rows * units),
         name="join_pairs",
     )(core, *parts, *rests)

time: 508 us -> 512 us (level)
  transfers between devices with their start and end apart: 89 -> 89, of which waited for: 33 -> 33; matrix products, arithmetic and copies ran while one was open for 9% -> 9% of each run, Pallas kernels for 17% -> 18%
where the time goes in v8:
time: 512 us; the launch traced here: 502 us
  waiting for transfers between devices  210 us (41%)
  starting transfers between devices  120 us (23%)
  Pallas kernels  111 us (22%)
  other arithmetic  34.1 us (7%)
  local copies, waits for them, and re-layouts  24.1 us (5%)
    ppermute x38, waiting for transfers between devices, swap(): return lax.ppermute(x, axis, [(0, 1), (1, 0)])  78.2 us
    pallas_call x16, Pallas kernels, grad_quarters(): pl.pallas_call(body, grid_spec=pltpu.PrefetchScalarGridSpec(num_scalar_pr...  27.9 us
    ppermute x38, starting transfers between devices, swap(): return lax.ppermute(x, axis, [(0, 1), (1, 0)])  27.4 us
    ppermute x8, waiting for transfers between devices, hop(): self.flying = [lax.ppermute(one, 'col', MID), lax.ppermute(mid, 'col', OUT)]  26.4 us
    ppermute x4, waiting for transfers between devices, hop(): self.flying = [lax.ppermute(far, 'col', OUT)]  25 us
    ppermute x4, starting transfers between devices, __init__(): self.two = lax.ppermute(self.part[2], 'col', IN)  21.6 us
    ppermute x4, waiting for transfers between devices, hop(): lax.ppermute(one, 'col', PAIR)  19.2 us
    pallas_call x4, Pallas kernels, to_features(): pl.pallas_call(body, grid=(width // block,), in_specs=[pl.BlockSpec((coun...  19 us
  transfers between devices with their start and end apart: 89, of which 33 were waited for; matrix products, arithmetic and copies ran while one was open for 9% of the time, Pallas kernels for 18%

profile of v8, /device:TPU:0, one launch (start us, length us, event | category | flops | bytes accessed | tf_op | source)
XLA Modules:
  0.0 502.5 jit_solution(13106101597907895438)
XLA Ops:
  33.1 17.1 %collective-permute-done.6 = bf16[128,2048]{1,0:T(8,128)(2,1)S(1)} collective-permute-done((bf16[128,2048]{1,0:T(8,128)(2,1)S(1)}, bf16[128,2048]{1,0:T(8,128)(2,1)S(1)}, u32[]{:S(2)}, u32[]{:S(2)}) %collective-permute-start.6) | collective-permute-done | bytes 524320 | tf_op jit(solution)/shard_map/ppermute | solution.py:60
  57.4 6.5 %collective-permute-done.7 = bf16[128,2048]{1,0:T(8,128)(2,1)S(1)} collective-permute-done((bf16[128,2048]{1,0:T(8,128)(2,1)S(1)}, bf16[128,2048]{1,0:T(8,128)(2,1)S(1)}, u32[]{:S(2)}, u32[]{:S(2)}) %collective-permute-start.7) | collective-permute-done | bytes 524320 | tf_op jit(solution)/shard_map/ppermute | solution.py:64
  77.4 7.9 %attend.1 = (bf16[512,256]{1,0:T(8,128)(2,1)S(1)}, bf16[512,256]{1,0:T(8,128)(2,1)S(1)}, f32[2,1024,2]{2,1,0:T(8,128)S(1)}) custom-call(s32[5]{0:T(128)S(1)} %pad_add_fusion.order_ref, bf16[3,512,256]{2,1,0:T(8,128)(2,1)S(1)} %qkv_columns.2.mine_ref, bf16[3,512,256]{2,1,0:T(8,128)(2,1)S(1)} %collective-permute-done.14.other_ref), custom_call_target="tpu_custom_call" | custom-call | flops 134217728 | bytes 262144 | tf_op jit(solution)/shard_map/attend/pallas_call | solution.py:346
  90.6 8.1 %collective-permute-start.18 = (bf16[128,2048]{1,0:T(8,128)(2,1)S(1)}, bf16[128,2048]{1,0:T(8,128)(2,1)S(1)}, u32[]{:S(2)}, u32[]{:S(2)}) collective-permute-start(bf16[128,2048]{1,0:T(8,128)(2,1)S(1)} %slice.154), channel_id=1, source_target_pairs={{0,1},{3,2},{4,5},{7,6},{8,9},{11,10},{12,13},{15,14},{16,17},{19,... | collective-permute-start | bytes 1572872 | tf_op jit(solution)/shard_map/ppermute | solution.py:80
  98.6 17.3 %collective-permute-done.21.refs_1_ = bf16[1408,512]{1,0:T(8,128)(2,1)S(1)} collective-permute-done((bf16[1408,512]{1,0:T(8,128)(2,1)S(1)}, bf16[1408,512]{1,0:T(8,128)(2,1)S(1)}, u32[]{:S(2)}, u32[]{:S(2)}) %collective-permute-start.21) | collective-permute-done | bytes 1441824 | tf_op jit(solution)/shard_map/ppermute | solution.py:23
  123.9 8.3 %collective-permute-done.23 = bf16[128,2048]{1,0:T(8,128)(2,1)S(1)} collective-permute-done((bf16[128,2048]{1,0:T(8,128)(2,1)S(1)}, bf16[128,2048]{1,0:T(8,128)(2,1)S(1)}, u32[]{:S(2)}, u32[]{:S(2)}) %collective-permute-start.23) | collective-permute-done | bytes 524320 | tf_op jit(solution)/shard_map/ppermute | solution.py:81
  143.5 6.1 %collective-permute-done.26.b_ref = bf16[128,2048]{1,0:T(8,128)(2,1)S(1)} collective-permute-done((bf16[128,2048]{1,0:T(8,128)(2,1)S(1)}, bf16[128,2048]{1,0:T(8,128)(2,1)S(1)}, u32[]{:S(2)}, u32[]{:S(2)}) %collective-permute-start.26) | collective-permute-done | bytes 524320 | tf_op jit(solution)/shard_map/ppermute | solution.py:91
  156.1 9.3 %collective-permute-done.28 = bf16[128,2048]{1,0:T(8,128)(2,1)S(1)} collective-permute-done((bf16[128,2048]{1,0:T(8,128)(2,1)S(1)}, bf16[128,2048]{1,0:T(8,128)(2,1)S(1)}, u32[]{:S(2)}, u32[]{:S(2)}) %collective-permute-start.28) | collective-permute-done | bytes 524320 | tf_op jit(solution)/shard_map/ppermute | solution.py:52
  167.4 19.0 %collective-permute-done.32.refs_1_ = bf16[2,512,1408]{2,1,0:T(8,128)(2,1)S(1)} collective-permute-done((bf16[2,512,1408]{2,1,0:T(8,128)(2,1)S(1)}, bf16[2,512,1408]{2,1,0:T(8,128)(2,1)S(1)}, u32[]{:S(2)}, u32[]{:S(2)}) %collective-permute-start.32) | collective-permute-done | bytes 2883616 | tf_op jit(solution)/shard_map/ppermute | solution.py:23
  188.4 14.3 %collective-permute-done.33 = bf16[128,2048]{1,0:T(8,128)(2,1)S(1)} collective-permute-done((bf16[128,2048]{1,0:T(8,128)(2,1)S(1)}, bf16[128,2048]{1,0:T(8,128)(2,1)S(1)}, u32[]{:S(2)}, u32[]{:S(2)}) %collective-permute-start.33) | collective-permute-done | bytes 524320 | tf_op jit(solution)/shard_map/ppermute | solution.py:64
  203.1 10.3 %feed_forward.1 = (bf16[512,1408]{1,0:T(8,128)(2,1)S(1)}, bf16[2,512,1408]{2,1,0:T(8,128)(2,1)S(1)}) custom-call(bf16[512,2048]{1,0:T(8,128)(2,1)S(1)} %pad_maximum_fusion.2.x_ref, bf16[2,1024,1408]{2,1,0:T(8,128)(2,1)S(1)} %bitcast.69, bf16[2,512,1408]{2,1,0:T(8,128)(2,1)S(1)} %collective-permute-done.32.refs_1_, ...), custom_call_target="tpu_custom_call" | custom-call | flops 738197504 | bytes 1703936 | tf_op jit(solution)/shard_map/feed_forward/pallas_call | solution.py:515
  215.2 8.0 %to_features.5 = bf16[512,2048]{1,0:T(8,128)(2,1)S(1)} custom-call(bf16[2,512,1408]{2,1,0:T(8,128)(2,1)S(1)} %get-tuple-element.206.v_ref.y_ref, bf16[2,1024,1408]{2,1,0:T(8,128)(2,1)S(1)} %bitcast.70, bf16[2,512,1408]{2,1,0:T(8,128)(2,1)S(1)} %copy-done.21, bf16[2,512,1408]{2,1,0:T(8,128)(2,1)S(1)} %collective-permute-done.34.refs_2_), custom_call_target="tpu_custom_call" | custom-call | flops 738197504 | bytes 2064384 | tf_op jit(solution)/shard_map/to_features/pallas_call | solution.py:565
  237.2 7.4 %collective-permute-start.37 = (bf16[128,2048]{1,0:T(8,128)(2,1)S(1)}, bf16[128,2048]{1,0:T(8,128)(2,1)S(1)}, u32[]{:S(2)}, u32[]{:S(2)}) collective-permute-start(bf16[128,2048]{1,0:T(8,128)(2,1)S(1)} %get-tuple-element.317), channel_id=1, source_target_pairs={{0,1},{3,2},{4,5},{7,6},{8,9},{11,10},{12,13},{15,14},{16,17},{19,... | collective-permute-start | bytes 1572872 | tf_op jit(solution)/shard_map/ppermute | solution.py:81
  263.9 6.8 %collective-permute-done.40.b_ref = bf16[128,2048]{1,0:T(8,128)(2,1)S(1)} collective-permute-done((bf16[128,2048]{1,0:T(8,128)(2,1)S(1)}, bf16[128,2048]{1,0:T(8,128)(2,1)S(1)}, u32[]{:S(2)}, u32[]{:S(2)}) %collective-permute-start.40) | collective-permute-done | bytes 524320 | tf_op jit(solution)/shard_map/ppermute | solution.py:91
  294.9 9.2 %collective-permute-done.46 = bf16[128,2048]{1,0:T(8,128)(2,1)S(1)} collective-permute-done((bf16[128,2048]{1,0:T(8,128)(2,1)}, bf16[128,2048]{1,0:T(8,128)(2,1)S(1)}, u32[]{:S(2)}, u32[]{:S(2)}) %collective-permute-start.46) | collective-permute-done | bytes 524320 | tf_op jit(solution)/shard_map/ppermute | solution.py:60
  308.4 10.7 %collective-permute-done.48.refs_1_ = bf16[1,1,512,1408]{3,2,1,0:T(8,128)(2,1)} collective-permute-done((bf16[1,1,512,1408]{3,2,1,0:T(8,128)(2,1)}, bf16[1,1,512,1408]{3,2,1,0:T(8,128)(2,1)}, u32[]{:S(2)}, u32[]{:S(2)}) %collective-permute-start.48) | collective-permute-done | bytes 1441824 | tf_op jit(solution)/shard_map/ppermute | solution.py:23
  336.5 14.2 %attend_back.1 = (bf16[3,512,256]{2,1,0:T(8,128)(2,1)S(1)}, bf16[3,512,256]{2,1,0:T(8,128)(2,1)S(1)}, f32[3,1,256]{2,1,0:T(1,128)S(1)}) custom-call(s32[5]{0:T(128)S(1)} %pad_add_fusion.order_ref, bf16[3,512,256]{2,1,0:T(8,128)(2,1)S(1)} %copy-done.25, bf16[3,512,256]{2,1,0:T(8,128)(2,1)S(1)} %collective-permute-done.14.other_ref, ...), custom_call_target="tpu_custom_call" | custom-call | flops 335544320 | bytes 655360 | tf_op jit(solution)/shard_map/attend_back/pallas_call | solution.py:456
  361.6 7.3 %collective-permute-done.55 = bf16[1,512,1408]{2,1,0:T(8,128)(2,1)} collective-permute-done((bf16[1,512,1408]{2,1,0:T(8,128)(2,1)S(1)}, bf16[1,512,1408]{2,1,0:T(8,128)(2,1)}, u32[]{:S(2)}, u32[]{:S(2)}) %collective-permute-start.55) | collective-permute-done | bytes 1441824 | tf_op jit(solution)/shard_map/ppermute | solution.py:23
  376.6 6.6 %collective-permute-done.57.refs_1_ = bf16[1,1,512,512]{3,2,1,0:T(8,128)(2,1)S(1)} collective-permute-done((bf16[1,1,512,512]{3,2,1,0:T(8,128)(2,1)S(1)}, bf16[1,1,512,512]{3,2,1,0:T(8,128)(2,1)S(1)}, u32[]{:S(2)}, u32[]{:S(2)}) %collective-permute-start.57) | collective-permute-done | bytes 524320 | tf_op jit(solution)/shard_map/ppermute | solution.py:23
  390.4 7.1 %collective-permute-done.58 = bf16[128,2048]{1,0:T(8,128)(2,1)S(1)} collective-permute-done((bf16[128,2048]{1,0:T(8,128)(2,1)S(1)}, bf16[128,2048]{1,0:T(8,128)(2,1)S(1)}, u32[]{:S(2)}, u32[]{:S(2)}) %collective-permute-start.58) | collective-permute-done | bytes 524320 | tf_op jit(solution)/shard_map/ppermute | solution.py:80
  398.3 6.8 %collective-permute-start.62 = (bf16[128,2048]{1,0:T(8,128)(2,1)S(1)}, bf16[128,2048]{1,0:T(8,128)(2,1)S(1)}, u32[]{:S(2)}, u32[]{:S(2)}) collective-permute-start(bf16[128,2048]{1,0:T(8,128)(2,1)S(1)} %get-tuple-element.310), channel_id=1, source_target_pairs={{0,1},{3,2},{4,5},{7,6},{8,9},{11,10},{12,13},{15,14},{16,17},{19,... | collective-permute-start | bytes 1572872 | tf_op jit(solution)/shard_map/ppermute | solution.py:81
  423.4 6.4 %collective-permute-done.65.b_ref = bf16[128,2048]{1,0:T(8,128)(2,1)S(1)} collective-permute-done((bf16[128,2048]{1,0:T(8,128)(2,1)S(1)}, bf16[128,2048]{1,0:T(8,128)(2,1)S(1)}, u32[]{:S(2)}, u32[]{:S(2)}) %collective-permute-start.65) | collective-permute-done | bytes 524320 | tf_op jit(solution)/shard_map/ppermute | solution.py:91
  457.5 8.1 %collective-permute-done.77 = f32[14,1024]{1,0:T(8,128)S(1)} collective-permute-done((f32[14,1024]{1,0:T(8,128)S(1)}, f32[14,1024]{1,0:T(8,128)S(1)}, u32[]{:S(2)}, u32[]{:S(2)}) %collective-permute-start.77) | collective-permute-done | bytes 57376 | tf_op jit(solution)/shard_map/ppermute | solution.py:993
  471.4 13.4 %join_pairs.1 = f32[1024,2,1408]{2,1,0:T(2,128)} custom-call(s32[1]{0:T(128)} %bitcast.12.half_ref.q_ref.index_ref.core_ref, bf16[1,512,1408]{2,1,0:T(8,128)(2,1)} %add_convert_fusion.1.refs_0_, bf16[1,512,1408]{2,1,0:T(8,128)(2,1)} %add_convert_fusion.refs_1_, bf16[1,512,1408]{2,1,0:T(8,128)(2,1)} %collective-permute-done.71.refs_2_, ...), custom_call_target="tpu_custom_call" | custom-call | flops 90112 | bytes 2162688 | tf_op jit(solution)/shard_map/join_pairs/pallas_call | solution.py:678
  (425 shorter events, 263.3 us)
Async XLA Ops:
  18.3 45.7 %collective-permute-start.8 = (bf16[3,512,512]{2,1,0:T(8,128)(2,1)S(1)}, bf16[3,512,512]{2,1,0:T(8,128)(2,1)S(1)}, u32[]{:S(2)}, u32[]{:S(2)}) collective-permute-start(bf16[3,512,512]{2,1,0:T(8,128)(2,1)S(1)} %dynamic-slice_bitcast_fusion), channel_id=1, source_target_pairs={{0,4},{4,0},{1,5},{5,1},{2,6},{6,2},{3,7},{7,3},{8,12},{12,8},{9,1... | collective-permute-start | bytes 4718600 | tf_op jit(solution)/shard_map/ppermute | solution.py:23
  32.2 25.1 %collective-permute-start.10 = (bf16[128,1024]{1,0:T(8,128)(2,1)S(1)}, bf16[128,1024]{1,0:T(8,128)(2,1)S(1)}, u32[]{:S(2)}, u32[]{:S(2)}) collective-permute-start(bf16[128,1024]{1,0:T(8,128)(2,1)S(1)} %get-tuple-element.349), channel_id=1, source_target_pairs={{0,8},{4,0},{8,12},{12,4},{1,9},{5,1},{9,13},{13,5},{2,10},{6,2},{... | collective-permute-start | bytes 786440 | tf_op jit(solution)/shard_map/ppermute | solution.py:755
  32.2 25.1 %collective-permute-start.9 = (bf16[128,1024]{1,0:T(8,128)(2,1)S(1)}, bf16[128,1024]{1,0:T(8,128)(2,1)S(1)}, u32[]{:S(2)}, u32[]{:S(2)}) collective-permute-start(bf16[128,1024]{1,0:T(8,128)(2,1)S(1)} %get-tuple-element.348), channel_id=1, source_target_pairs={{0,0},{4,8},{8,4},{12,12},{1,1},{5,9},{9,5},{13,13},{2,2},{6,10},{... | collective-permute-start | bytes 786440 | tf_op jit(solution)/shard_map/ppermute | solution.py:754
  73.9 42.1 %collective-permute-start.21 = (bf16[1408,512]{1,0:T(8,128)(2,1)S(1)}, bf16[1408,512]{1,0:T(8,128)(2,1)S(1)}, u32[]{:S(2)}, u32[]{:S(2)}) collective-permute-start(bf16[1408,512]{1,0:T(8,128)(2,1)S(1)} %dynamic-slice_bitcast_fusion.1), channel_id=1, source_target_pairs={{0,4},{4,0},{1,5},{5,1},{2,6},{6,2},{3,7},{7,3},{8,12},{12,8},{9,1... | collective-permute-start | bytes 4325384 | tf_op jit(solution)/shard_map/ppermute | solution.py:23
  86.2 29.8 %collective-permute-start.19 = (bf16[128,2048]{1,0:T(8,128)(2,1)}, bf16[128,2048]{1,0:T(8,128)(2,1)S(1)}, u32[]{:S(2)}, u32[]{:S(2)}) collective-permute-start(bf16[128,2048]{1,0:T(8,128)(2,1)} %collective-permute-done.11), channel_id=1, source_target_pairs={{1,2},{2,1},{5,6},{6,5},{9,10},{10,9},{13,14},{14,13},{17,18},{18,... | collective-permute-start | bytes 1572872 | tf_op jit(solution)/shard_map/ppermute | solution.py:60
  86.9 29.1 %collective-permute-start.20 = (bf16[128,2048]{1,0:T(8,128)(2,1)S(1)}, bf16[128,2048]{1,0:T(8,128)(2,1)S(1)}, u32[]{:S(2)}, u32[]{:S(2)}) collective-permute-start(bf16[128,2048]{1,0:T(8,128)(2,1)S(1)} %collective-permute-done.12), channel_id=1, source_target_pairs={{1,0},{2,3},{5,4},{6,7},{9,8},{10,11},{13,12},{14,15},{17,16},{18,... | collective-permute-start | bytes 1572872 | tf_op jit(solution)/shard_map/ppermute | solution.py:60
  90.6 25.4 %collective-permute-start.18 = (bf16[128,2048]{1,0:T(8,128)(2,1)S(1)}, bf16[128,2048]{1,0:T(8,128)(2,1)S(1)}, u32[]{:S(2)}, u32[]{:S(2)}) collective-permute-start(bf16[128,2048]{1,0:T(8,128)(2,1)S(1)} %slice.154), channel_id=1, source_target_pairs={{0,1},{3,2},{4,5},{7,6},{8,9},{11,10},{12,13},{15,14},{16,17},{19,... | collective-permute-start | bytes 1572872 | tf_op jit(solution)/shard_map/ppermute | solution.py:80
  116.0 20.4 %collective-permute-start.25 = (bf16[1408,512]{1,0:T(8,128)(2,1)S(1)}, bf16[1408,512]{1,0:T(8,128)(2,1)S(1)}, u32[]{:S(2)}, u32[]{:S(2)}) collective-permute-start(bf16[1408,512]{1,0:T(8,128)(2,1)S(1)} %collective-permute-done.21.refs_1_), channel_id=1, source_target_pairs={{0,8},{8,0},{1,9},{9,1},{2,10},{10,2},{3,11},{11,3},{4,12},{12,4},... | collective-permute-start | bytes 4325384 | tf_op jit(solution)/shard_map/ppermute | solution.py:23
  122.0 64.4 %collective-permute-start.32 = (bf16[2,512,1408]{2,1,0:T(8,128)(2,1)S(1)}, bf16[2,512,1408]{2,1,0:T(8,128)(2,1)S(1)}, u32[]{:S(2)}, u32[]{:S(2)}) collective-permute-start(bf16[2,512,1408]{2,1,0:T(8,128)(2,1)S(1)} %bitcast.103), channel_id=1, source_target_pairs={{0,4},{4,0},{1,5},{5,1},{2,6},{6,2},{3,7},{7,3},{8,12},{12,8},{9,1... | collective-permute-start | bytes 8650760 | tf_op jit(solution)/shard_map/ppermute | solution.py:23
  165.4 21.0 %collective-permute-start.30 = (bf16[128,2048]{1,0:T(8,128)(2,1)S(1)}, bf16[128,2048]{1,0:T(8,128)(2,1)S(1)}, u32[]{:S(2)}, u32[]{:S(2)}) collective-permute-start(bf16[128,2048]{1,0:T(8,128)(2,1)S(1)} %collective-permute-done.28), channel_id=1, source_target_pairs={{1,2},{2,1},{5,6},{6,5},{9,10},{10,9},{13,14},{14,13},{17,18},{18,... | collective-permute-start | bytes 1572872 | tf_op jit(solution)/shard_map/ppermute | solution.py:60
  166.1 20.3 %collective-permute-start.31 = (bf16[128,2048]{1,0:T(8,128)(2,1)S(1)}, bf16[128,2048]{1,0:T(8,128)(2,1)S(1)}, u32[]{:S(2)}, u32[]{:S(2)}) collective-permute-start(bf16[128,2048]{1,0:T(8,128)(2,1)S(1)} %collective-permute-done.29), channel_id=1, source_target_pairs={{1,0},{2,3},{5,4},{6,7},{9,8},{10,11},{13,12},{14,15},{17,16},{18,... | collective-permute-start | bytes 1572872 | tf_op jit(solution)/shard_map/ppermute | solution.py:60
  235.9 19.7 %collective-permute-start.39 = (bf16[2,2,512,1408]{3,2,1,0:T(8,128)(2,1)S(1)}, bf16[2,2,512,1408]{3,2,1,0:T(8,128)(2,1)S(1)}, u32[]{:S(2)}, u32[]{:S(2)}) collective-permute-start(bf16[2,2,512,1408]{3,2,1,0:T(8,128)(2,1)S(1)} %grad_quarters.17), channel_id=1, source_target_pairs={{0,8},{8,0},{1,9},{9,1},{2,10},{10,2},{3,11},{11,3},{4,12},{12,4},... | collective-permute-start | bytes 17301512 | tf_op jit(solution)/shard_map/ppermute | solution.py:23
  255.6 34.8 %collective-permute-start.44 = (bf16[1,1,1408,512]{3,2,1,0:T(8,128)(2,1)}, bf16[1,1,1408,512]{3,2,1,0:T(8,128)(2,1)}, u32[]{:S(2)}, u32[]{:S(2)}) collective-permute-start(bf16[1,1,1408,512]{3,2,1,0:T(8,128)(2,1)} %grad_quarters.18), channel_id=1, source_target_pairs={{0,4},{4,0},{1,5},{5,1},{2,6},{6,2},{3,7},{7,3},{8,12},{12,8},{9,1... | collective-permute-start | bytes 4325384 | tf_op jit(solution)/shard_map/ppermute | solution.py:23
  279.3 39.8 %collective-permute-start.48 = (bf16[1,1,512,1408]{3,2,1,0:T(8,128)(2,1)}, bf16[1,1,512,1408]{3,2,1,0:T(8,128)(2,1)}, u32[]{:S(2)}, u32[]{:S(2)}) collective-permute-start(bf16[1,1,512,1408]{3,2,1,0:T(8,128)(2,1)} %grad_quarters.19), channel_id=1, source_target_pairs={{0,4},{4,0},{1,5},{5,1},{2,6},{6,2},{3,7},{7,3},{8,12},{12,8},{9,1... | collective-permute-start | bytes 4325384 | tf_op jit(solution)/shard_map/ppermute | solution.py:23
  304.1 28.4 %collective-permute-start.50 = (bf16[1,1408,512]{2,1,0:T(8,128)(2,1)S(1)}, bf16[1,1408,512]{2,1,0:T(8,128)(2,1)S(1)}, u32[]{:S(2)}, u32[]{:S(2)}) collective-permute-start(bf16[1,1408,512]{2,1,0:T(8,128)(2,1)S(1)} %bitcast.83), channel_id=1, source_target_pairs={{0,16},{16,0},{1,17},{17,1},{2,18},{18,2},{3,19},{19,3},{4,20},{20... | collective-permute-start | bytes 4325384 | tf_op jit(solution)/shard_map/ppermute | solution.py:23
  319.3 31.5 %collective-permute-start.53 = (bf16[1,1,512,1408]{3,2,1,0:T(8,128)(2,1)S(1)}, bf16[1,1,512,1408]{3,2,1,0:T(8,128)(2,1)S(1)}, u32[]{:S(2)}, u32[]{:S(2)}) collective-permute-start(bf16[1,1,512,1408]{3,2,1,0:T(8,128)(2,1)S(1)} %grad_quarters.20), channel_id=1, source_target_pairs={{0,4},{4,0},{1,5},{5,1},{2,6},{6,2},{3,7},{7,3},{8,12},{12,8},{9,1... | collective-permute-start | bytes 4325384 | tf_op jit(solution)/shard_map/ppermute | solution.py:23
  334.9 33.9 %collective-permute-start.55 = (bf16[1,512,1408]{2,1,0:T(8,128)(2,1)S(1)}, bf16[1,512,1408]{2,1,0:T(8,128)(2,1)}, u32[]{:S(2)}, u32[]{:S(2)}) collective-permute-start(bf16[1,512,1408]{2,1,0:T(8,128)(2,1)S(1)} %bitcast.85), channel_id=1, source_target_pairs={{0,16},{16,0},{1,17},{17,1},{2,18},{18,2},{3,19},{19,3},{4,20},{20... | collective-permute-start | bytes 4325384 | tf_op jit(solution)/shard_map/ppermute | solution.py:23
  370.7 19.7 %collective-permute-start.59 = (bf16[128,2048]{1,0:T(8,128)(2,1)S(1)}, bf16[128,2048]{1,0:T(8,128)(2,1)S(1)}, u32[]{:S(2)}, u32[]{:S(2)}) collective-permute-start(bf16[128,2048]{1,0:T(8,128)(2,1)S(1)} %get-tuple-element.313), channel_id=1, source_target_pairs={{1,2},{2,1},{5,6},{6,5},{9,10},{10,9},{13,14},{14,13},{17,18},{18,... | collective-permute-start | bytes 1572872 | tf_op jit(solution)/shard_map/ppermute | solution.py:88
  375.0 33.2 %collective-permute-start.64 = (bf16[1,512,1408]{2,1,0:T(8,128)(2,1)S(1)}, bf16[1,512,1408]{2,1,0:T(8,128)(2,1)S(1)}, u32[]{:S(2)}, u32[]{:S(2)}) collective-permute-start(bf16[1,512,1408]{2,1,0:T(8,128)(2,1)S(1)} %bitcast.87), channel_id=1, source_target_pairs={{0,16},{16,0},{1,17},{17,1},{2,18},{18,2},{3,19},{19,3},{4,20},{20... | collective-permute-start | bytes 4325384 | tf_op jit(solution)/shard_map/ppermute | solution.py:23
  387.5 27.7 %collective-permute-start.63 = (bf16[1,2,512,512]{3,2,1,0:T(8,128)(2,1)S(1)}, bf16[1,2,512,512]{3,2,1,0:T(8,128)(2,1)S(1)}, u32[]{:S(2)}, u32[]{:S(2)}) collective-permute-start(bf16[1,2,512,512]{3,2,1,0:T(8,128)(2,1)S(1)} %grad_quarters.27), channel_id=1, source_target_pairs={{0,4},{4,0},{1,5},{5,1},{2,6},{6,2},{3,7},{7,3},{8,12},{12,8},{9,1... | collective-permute-start | bytes 3145736 | tf_op jit(solution)/shard_map/ppermute | solution.py:23
  420.6 19.8 %collective-permute-start.69 = (bf16[1,1408,512]{2,1,0:T(8,128)(2,1)}, bf16[1,1408,512]{2,1,0:T(8,128)(2,1)}, u32[]{:S(2)}, u32[]{:S(2)}) collective-permute-start(bf16[1,1408,512]{2,1,0:T(8,128)(2,1)} %add_convert_fusion.2), channel_id=1, source_target_pairs={{0,8},{8,0},{1,9},{9,1},{2,10},{10,2},{3,11},{11,3},{4,12},{12,4},... | collective-permute-start | bytes 4325384 | tf_op jit(solution)/shard_map/ppermute | solution.py:23
  431.4 26.1 %collective-permute-start.78 = (bf16[2,512,512]{2,1,0:T(8,128)(2,1)}, bf16[2,512,512]{2,1,0:T(8,128)(2,1)}, u32[]{:S(2)}, u32[]{:S(2)}) collective-permute-start(bf16[2,512,512]{2,1,0:T(8,128)(2,1)} %bitcast.91), channel_id=1, source_target_pairs={{0,16},{16,0},{1,17},{17,1},{2,18},{18,2},{3,19},{19,3},{4,20},{20... | collective-permute-start | bytes 3145736 | tf_op jit(solution)/shard_map/ppermute | solution.py:23
  456.8 28.1 %collective-permute-start.82 = (bf16[1,512,512]{2,1,0:T(8,128)(2,1)S(1)}, bf16[1,512,512]{2,1,0:T(8,128)(2,1)S(1)}, u32[]{:S(2)}, u32[]{:S(2)}) collective-permute-start(bf16[1,512,512]{2,1,0:T(8,128)(2,1)S(1)} %bitcast.93), channel_id=1, source_target_pairs={{0,16},{16,0},{1,17},{17,1},{2,18},{18,2},{3,19},{19,3},{4,20},{20... | collective-permute-start | bytes 1572872 | tf_op jit(solution)/shard_map/ppermute | solution.py:23
  468.2 21.8 %collective-permute-start.84 = (bf16[2,512,512]{2,1,0:T(8,128)(2,1)S(1)}, bf16[2,512,512]{2,1,0:T(8,128)(2,1)S(1)}, u32[]{:S(2)}, u32[]{:S(2)}) collective-permute-start(bf16[2,512,512]{2,1,0:T(8,128)(2,1)S(1)} %add_convert_fusion.3), channel_id=1, source_target_pairs={{0,8},{8,0},{1,9},{9,1},{2,10},{10,2},{3,11},{11,3},{4,12},{12,4},... | collective-permute-start | bytes 3145736 | tf_op jit(solution)/shard_map/ppermute | solution.py:23
  (132 other events, 1622.9 us)
